TPU v7x, 32 devices: a whole 2x2x4 slice. The times are simulated.
32 devices in a mesh: side: 2 (over y), slab: 16 (over z, x, core).
Axes of the slice: x: 2, y: 2, z: 4, core: 2. Of those that a mesh axis runs over, the one named last changes fastest.
Arguments:
- velocity: float32 [2, 4096, 4096], P('side', 'slab'), may hold values from -6 to 6
- kernel: bfloat16 [2, 9, 4096, 4096], P('side', None, 'slab'), may hold values from -4 to 4
- history: bfloat16 [2, 8, 2, 4096, 4096], P('side', None, None, 'slab'), may hold values from -24576 to 24576
- impedance: float32 [2], replicated, may hold values from 0.5 to 1.5
- prestress: float32 [4096, 4096], P('slab'), may hold values from 1 to 3
- strength: float32 [4096, 4096], P('slab'), may hold values from 0.5 to 2
- fault_state: float32 [4096, 4096], P('slab'), may hold values from -1 to 1
Outputs:
- new_velocity: float32 [2, 4096, 4096], P('side', 'slab')
- slip_rate: float32 [4096, 4096], P('slab')
- new_state: float32 [4096, 4096], P('slab')
All inputs are finite; a program needn't handle non-finite values.
Results may differ from a plain program's by a relative error of at most 0.00058.
Values sent between devices are 32-bit elements; how exact they have to be, the bound alone decides.
No kernel may reach another device: no remote copies, remote signals or barrier semaphores. Data moves between devices by JAX's collectives and lax.ppermute only.
A program may use at most 320 MiB of HBM per device.

v0:
```python
import math

import jax
import jax.numpy as jnp
from jax import lax
from jax.sharding import PartitionSpec as P

NX = 4096
NZ = 4096
NEWTON = 4
STEPS = 2


highest = lax.Precision.HIGHEST


def swapped(value, axis, distance):
    mask = 2**distance
    pairs = [(source, source ^ mask) for source in range(lax.axis_size(axis))]
    return lax.ppermute(value, axis, pairs)


def inverse_sinh(value):
    magnitude = jnp.abs(value)
    result = jnp.log1p(
        magnitude + magnitude * magnitude / (1.0 + jnp.sqrt(1.0 + magnitude * magnitude))
    )
    return jnp.where(value < 0.0, -result, result)


def angle_table(rows_count, cols_count, period, sign):
    first = lax.broadcasted_iota(jnp.int32, (rows_count, cols_count), 0)
    second = lax.broadcasted_iota(jnp.int32, (rows_count, cols_count), 1)
    phase = (first * second % period).astype(jnp.float32) * (2.0 * math.pi / period)
    return (jnp.cos(phase), sign * jnp.sin(phase))


def transform_last(real_part, imag_part, sign, real_only):
    length = real_part.shape[-1]
    inner = min(length, 256)
    outer = length // inner
    leading = real_part.shape[:-1]
    cos_outer, sin_outer = angle_table(outer, outer, outer, sign)
    cos_twist, sin_twist = angle_table(outer, inner, length, sign)
    cos_inner, sin_inner = angle_table(inner, inner, inner, sign)
    shaped_real = real_part.reshape(leading + (outer, inner))
    step_real = jnp.einsum("kn,...nq->...kq", cos_outer, shaped_real, precision=highest)
    step_imag = jnp.einsum("kn,...nq->...kq", sin_outer, shaped_real, precision=highest)
    if imag_part is not None:
        shaped_imag = imag_part.reshape(leading + (outer, inner))
        step_real = step_real - jnp.einsum(
            "kn,...nq->...kq", sin_outer, shaped_imag, precision=highest
        )
        step_imag = step_imag + jnp.einsum(
            "kn,...nq->...kq", cos_outer, shaped_imag, precision=highest
        )
    twist_real = step_real * cos_twist - step_imag * sin_twist
    twist_imag = step_real * sin_twist + step_imag * cos_twist
    out_real = jnp.matmul(twist_real, cos_inner, precision=highest) - jnp.matmul(
        twist_imag, sin_inner, precision=highest
    )
    result_real = jnp.swapaxes(out_real, -1, -2).reshape(leading + (length,))
    if real_only:
        return (result_real, None)
    out_imag = jnp.matmul(twist_real, sin_inner, precision=highest) + jnp.matmul(
        twist_imag, cos_inner, precision=highest
    )
    result_imag = jnp.swapaxes(out_imag, -1, -2).reshape(leading + (length,))
    return (result_real, result_imag)


def to_spectrum(rows_field):
    slab_count = lax.axis_size("slab")
    z_real, z_imag = transform_last(rows_field, None, -1.0, False)
    stacked = jnp.stack([z_real, z_imag])
    rows_dev = stacked.shape[1]
    length_z = stacked.shape[2]
    moved = jnp.transpose(stacked, (0, 2, 1)).reshape(
        2, slab_count, length_z // slab_count, rows_dev
    )
    block = lax.all_to_all(moved, "slab", split_axis=1, concat_axis=3, tiled=True)
    spec_real, spec_imag = transform_last(block[0, 0], block[1, 0], -1.0, False)
    return jnp.stack([spec_real, spec_imag]).astype(jnp.bfloat16)


def to_rows(spec_real, spec_imag):
    slab_count = lax.axis_size("slab")
    x_real, x_imag = transform_last(spec_real, spec_imag, 1.0, False)
    stacked = jnp.stack([x_real, x_imag], axis=1)
    batch = stacked.shape[0]
    kz_dev = stacked.shape[2]
    length_x = stacked.shape[3]
    moved = stacked.reshape(batch, 2, kz_dev, slab_count, length_x // slab_count)
    scale = 1.0 / (NX * NZ)
    turned = jnp.swapaxes(
        lax.all_to_all(moved, "slab", split_axis=3, concat_axis=2, tiled=True)[:, :, :, 0, :], 2, 3
    )
    field_real, unused = transform_last(turned[:, 0], turned[:, 1], 1.0, True)
    return field_real * scale


def local(velocity, kernel, history, impedance, prestress, strength, fault_state):
    side_index = lax.axis_index("side")
    is_first = side_index == 0
    eta_first = impedance[0]
    eta_second = impedance[1]
    eta_total = eta_first + eta_second
    weight_first = eta_second / eta_total
    weight_second = eta_first / eta_total
    eta_joint = eta_first * eta_second / eta_total
    own_eta = jnp.where(is_first, eta_first, eta_second)
    own_sign = jnp.where(is_first, 1.0, -1.0).astype(jnp.float32)
    lag_kernel = kernel[0]
    lag_history = history[0]
    kernel_now = lag_kernel[0].astype(jnp.float32)
    speed = velocity[0]
    state_now = fault_state
    rate = jnp.zeros_like(prestress)
    for step_index in range(STEPS):
        spec_now = to_spectrum(speed)
        total = kernel_now * spec_now.astype(jnp.float32) + jnp.einsum(
            "lzx,lczx->czx", lag_kernel[1:], lag_history, preferred_element_type=jnp.float32
        )
        force_now = to_rows(total[0][None], total[1][None])[0]
        force_other = swapped(force_now, "side", 0)
        force_first = jnp.where(is_first, force_now, force_other)
        force_second = jnp.where(is_first, force_other, force_now)
        coupled = weight_first * force_first + weight_second * force_second
        locked = prestress + coupled
        friction_rate = locked / (eta_joint + strength)
        factor = 0.5 * jnp.exp(state_now)
        for iteration in range(NEWTON):
            scaled = factor * friction_rate
            misfit = strength * inverse_sinh(scaled) + eta_joint * friction_rate - locked
            slope = strength * factor / jnp.sqrt(1.0 + scaled * scaled) + eta_joint
            friction_rate = friction_rate - 0.5 * misfit / slope
        stress = locked - eta_joint * friction_rate
        speed_new = own_sign * (prestress + force_now - stress) / own_eta
        state_new = state_now + 0.25 * (jnp.exp(-state_now) - jnp.abs(friction_rate))
        speed = speed_new
        rate = friction_rate
        state_now = state_new
        lag_history = jnp.concatenate([spec_now[None], lag_history[:-1]], axis=0)
    return (speed[None], rate, state_now)


def solution(mesh):
    placed = (
        P("side", "slab", None),
        P("side", None, "slab", None),
        P("side", None, None, "slab", None),
        P(),
        P("slab", None),
        P("slab", None),
        P("slab", None),
    )
    return jax.shard_map(
        local,
        mesh=mesh,
        in_specs=placed,
        out_specs=(P("side", "slab", None), P("slab", None), P("slab", None)),
        check_vma=False,
    )
```

profile of v0, /device:TPU:0, one launch (start us, length us, event | category | flops | bytes accessed | tf_op | source)
XLA Modules:
  0.0 1637.3 jit_solution(13415248019297490977)
XLA Ops:
  70.1 18.7 %bitcast_convert_fusion = f32[256,4096,8]{1,0,2:T(8,128)} fusion(bf16[1,9,256,4096]{3,2,1,0:T(8,128)(2,1)} %param.8), kind=kLoop, calls=%fused_computation.4 | loop fusion | flops 8388608 | bytes 50331648
  88.7 20.2 %slice_bitcast_fusion = bf16[7,2,256,4096]{3,2,1,0:T(8,128)(2,1)} fusion(bf16[1,8,2,256,4096]{4,3,2,1,0:T(8,128)(2,1)} %param.9), kind=kLoop, calls=%fused_computation.3 | loop fusion | bytes 58720256 | tf_op jit(solution)/shard_map/slice | solution.py:143
  109.0 101.9 %all-to-all-done = f32[2,16,256,256]{3,2,0,1:T(8,128)} async-done(((f32[2,16,256,256]{3,2,0,1:T(8,128)}), f32[2,16,256,256]{3,2,0,1:T(8,128)}, u32[]{:S(2)}, u32[]{:S(2)}) %all-to-all-start) | async-done | bytes 8388640 | tf_op jit(solution)/shard_map/all_to_all | solution.py:81
  210.8 8.2 copy.392
  251.2 14.5 fusion.158
  266.9 14.6 fusion.159
  292.8 39.4 %multiply_reduce_fusion.1 = (f32[256,4096,2]{1,0,2:T(8,128)}, f32[256,4096,2]{1,0,2:T(8,128)}) fusion(f32[256,4096,8]{1,0,2:T(8,128)} %bitcast_convert_fusion, bf16[1,8,2,256,4096]{4,3,2,1,0:T(8,128)(2,1)} %param.9, bf16[7,2,256,4096]{3,2,1,0:T(8,128)(2,1)} %slice_bitcast_fusion, bf16[1,2,256,4096]{3,2,1,0:T(8,128)(2,1)} %copy.251), kind=kLoop, calls=%fused_computation.1 | loop fusion | flops 113246208 | bytes 117440512
  332.2 9.0 copy.286
  356.8 8.1 fusion.268
  425.4 218.4 %all_to_all.60 = f32[1,2,256,16,256]{2,4,1,0,3:T(8,128)} all-to-all(f32[1,2,256,16,256]{2,4,1,0,3:T(8,128)S(1)} %copy.217), channel_id=1, replica_groups=mesh['side'=2,'slab'=16] {'slab'}, dimensions={3} | all-to-all | bytes 16777216 | tf_op jit(solution)/shard_map/all_to_all | solution.py:96
  643.8 8.7 copy.218
  665.3 8.1 fusion.265
  741.3 69.6 %collective-permute-done = f32[256,4096]{0,1:T(8,128)} collective-permute-done((f32[256,4096]{0,1:T(8,128)}, f32[256,4096]{0,1:T(8,128)}, u32[]{:S(2)}, u32[]{:S(2)}) %collective-permute-start) | collective-permute-done | bytes 4194336 | tf_op jit(solution)/shard_map/ppermute | solution.py:20
  810.9 27.8 %multiply_divide_fusion = (f32[256,4096]{0,1:T(8,128)}, f32[256,4096]{0,1:T(8,128)}) fusion(f32[256,4096]{0,1:T(8,128)} %copy.267, f32[256,4096]{0,1:T(8,128)} %collective-permute-done, f32[]{:T(128)S(6)} %select_n.309, f32[]{:T(128)S(6)} %div.99, f32[]{:T(128)S(6)} %div.98, f32[]{:T(128)S(6)} %div.97, f32[]{:T(128)S(6)} %select_n.298, pred[]{:T(512)S(6)} %eq.30, ...), kind=kLoop, calls=%fused_computation.144 | loop fusion | flops 96468992 | bytes 29360148 | tf_op jit(solution)/shard_map/div | solution.py:138
  899.4 8.9 copy.294
  908.3 141.7 %all-to-all-done.2 = f32[2,16,256,256]{3,2,0,1:T(8,128)} async-done(((f32[2,16,256,256]{3,2,0,1:T(8,128)}), f32[2,16,256,256]{3,2,0,1:T(8,128)}, u32[]{:S(2)}, u32[]{:S(2)}) %all-to-all-start.2) | async-done | bytes 8388640 | tf_op jit(solution)/shard_map/all_to_all | solution.py:81
  1049.9 8.2 copy.391
  1090.3 14.5 fusion.160
  1106.0 14.7 fusion.161
  1202.5 218.4 %all_to_all.61 = f32[1,2,256,16,256]{2,4,1,0,3:T(8,128)} all-to-all(f32[1,2,256,16,256]{2,4,1,0,3:T(8,128)S(1)} %copy.260), channel_id=1, replica_groups=mesh['side'=2,'slab'=16] {'slab'}, dimensions={3} | all-to-all | bytes 16777216 | tf_op jit(solution)/shard_map/all_to_all | solution.py:96
  1420.8 8.8 copy.261
  1492.5 91.9 %collective-permute-done.1 = f32[256,4096]{0,1:T(8,128)S(1)} collective-permute-done((f32[256,4096]{0,1:T(8,128)S(1)}, f32[256,4096]{0,1:T(8,128)S(1)}, u32[]{:S(2)}, u32[]{:S(2)}) %collective-permute-start.1) | collective-permute-done | bytes 4194336 | tf_op jit(solution)/shard_map/ppermute | solution.py:20
  1584.4 27.1 %multiply_add_fusion = (f32[256,4096]{0,1:T(8,128)}, f32[256,4096]{0,1:T(8,128)}) fusion(f32[256,4096]{0,1:T(8,128)S(1)} %copy-done.6, f32[256,4096]{0,1:T(8,128)S(1)} %copy-done.19, f32[256,4096]{0,1:T(8,128)S(1)} %copy-done.5, f32[]{:T(128)S(6)} %div.99, f32[256,4096]{0,1:T(8,128)S(1)} %copy-done, f32[256,4096]{0,1:T(8,128)S(1)} %collective-permute-done.1, ...), kind=kLoop, calls=%fused_computation.132 | loop fusion | flops 100663296 | bytes 33554444 | tf_op jit(solution)/shard_map/add | solution.py:139
  1617.1 8.8 divide_bitcast_fusion
  (158 shorter events, 520.3 us)
Async XLA Ops:
  0.7 230.4 %copy-start.21 = (f32[16,256]{1,0:T(8,128)}, f32[16,256]{1,0:T(8,128)S(1)}, u32[]{:S(2)}) copy-start(f32[16,256]{1,0:T(8,128)S(1)} %get-tuple-element.44) | copy-start | bytes 49156
  52.8 158.0 %all-to-all-start = ((f32[2,16,256,256]{3,2,0,1:T(8,128)}), f32[2,16,256,256]{3,2,0,1:T(8,128)}, u32[]{:S(2)}, u32[]{:S(2)}) async-start(f32[2,16,256,256]{3,2,0,1:T(8,128)} %copy.201), calls=%async_computation | async-start | bytes 16777216 | tf_op jit(solution)/shard_map/all_to_all | solution.py:81
  356.7 8.1 copy-start.8
  375.7 7.9 copy-start.2
  375.7 7.9 copy-start.16
  665.3 8.1 copy-start.9
  684.4 7.9 copy-start.3
  684.5 7.9 copy-start.17
  717.1 93.7 %collective-permute-start = (f32[256,4096]{0,1:T(8,128)}, f32[256,4096]{0,1:T(8,128)}, u32[]{:S(2)}, u32[]{:S(2)}) collective-permute-start(f32[256,4096]{0,1:T(8,128)} %bitcast.70), channel_id=1, source_target_pairs={{0,16},{16,0},{1,17},{17,1},{2,18},{18,2},{3,19},{19,3},{4,20},{20... | collective-permute-start | bytes 12582920 | tf_op jit(solution)/shard_map/ppermute | solution.py:20
  894.2 155.8 %all-to-all-start.2 = ((f32[2,16,256,256]{3,2,0,1:T(8,128)}), f32[2,16,256,256]{3,2,0,1:T(8,128)}, u32[]{:S(2)}, u32[]{:S(2)}) async-start(f32[2,16,256,256]{3,2,0,1:T(8,128)} %copy.241), calls=%async_computation.2 | async-start | bytes 16777216 | tf_op jit(solution)/shard_map/all_to_all | solution.py:81
  1090.3 31.6 %slice-start = ((s8[8388608]{0:T(1024)(128)(4,1)}), s8[4194304]{0:T(1024)(128)(4,1)S(1)}, s32[]{:S(2)}) async-start(s8[8388608]{0:T(1024)(128)(4,1)} %bitcast.474), calls=%async_computation.4 | async-start | bytes 8388608
  1106.0 15.9 slice-start.1
  1133.8 8.1 copy-start.10
  1152.8 7.9 copy-start.4
  1152.8 7.9 copy-start.18
  1442.6 8.0 copy-start.11
  1461.7 7.4 copy-start.1
  1481.0 103.4 %copy-start.6 = (f32[256,4096]{0,1:T(8,128)S(1)}, f32[256,4096]{0,1:T(8,128)}, u32[]{:S(2)}) copy-start(f32[256,4096]{0,1:T(8,128)} %copy.227) | copy-start | bytes 12582916
  1481.0 103.4 %copy-start.19 = (f32[256,4096]{0,1:T(8,128)S(1)}, f32[256,4096]{0,1:T(8,128)}, u32[]{:S(2)}) copy-start(f32[256,4096]{0,1:T(8,128)} %get-tuple-element.17) | copy-start | bytes 12582916
  1488.2 96.2 %copy-start = (f32[256,4096]{0,1:T(8,128)S(1)}, f32[256,4096]{0,1:T(8,128)}, u32[]{:S(2)}) copy-start(f32[256,4096]{0,1:T(8,128)} %copy.267) | copy-start | bytes 12582916
  1488.2 96.2 %copy-start.5 = (f32[256,4096]{0,1:T(8,128)S(1)}, f32[256,4096]{0,1:T(8,128)}, u32[]{:S(2)}) copy-start(f32[256,4096]{0,1:T(8,128)} %copy.226) | copy-start | bytes 12582916
  1490.9 120.6 %copy-start.7 = (f32[1,256,256,16]{1,3,2,0:T(8,128)}, f32[1,256,256,16]{1,3,2,0:T(8,128)S(1)}, u32[]{:S(2)}) copy-start(f32[1,256,256,16]{1,3,2,0:T(8,128)S(1)} %copy.266) | copy-start | bytes 12582916
  1490.9 93.5 %collective-permute-start.1 = (f32[256,4096]{0,1:T(8,128)S(1)}, f32[256,4096]{0,1:T(8,128)S(1)}, u32[]{:S(2)}, u32[]{:S(2)}) collective-permute-start(f32[256,4096]{0,1:T(8,128)S(1)} %bitcast.471), channel_id=1, source_target_pairs={{0,16},{16,0},{1,17},{17,1},{2,18},{18,2},{3,19},{19,3},{4,20},{20... | collective-permute-start | bytes 12582920 | tf_op jit(solution)/shard_map/ppermute | solution.py:20
  1584.4 27.1 %copy-start.20 = (f32[256,4096]{0,1:T(8,128)}, f32[256,4096]{0,1:T(8,128)S(1)}, u32[]{:S(2)}) copy-start(f32[256,4096]{0,1:T(8,128)S(1)} %collective-permute-done.1) | copy-start | bytes 12582916
  (6 other events, 29.2 us)
where the time goes:
time: 1650 us; the launch traced here: 1640 us
  blocking collectives  437 us (26%)
  waiting for transfers between devices  405 us (25%)
  matrix products  396 us (24%)
  local copies, waits for them, and re-layouts  239 us (14%)
  other arithmetic  139 us (8%)
    all_to_all x2, blocking collectives, to_rows(): lax.all_to_all(moved, 'slab', split_axis=3, concat_axis=2, tiled=True)  437 us
    all_to_all x2, waiting for transfers between devices, to_spectrum(): lax.all_to_all(moved, 'slab', split_axis=1, concat_axis=3, tiled=True)  244 us
    ppermute x2, waiting for transfers between devices, swapped(): return lax.ppermute(value, axis, pairs)  161 us
    dot_general x8, matrix products, transform_last(): jnp.matmul(twist_real, cos_inner, precision=highest)  74.7 us
    dot_general x6, matrix products, transform_last(): jnp.matmul(twist_real, sin_inner, precision=highest)  59.6 us
    dot_general x8, matrix products, transform_last(): jnp.matmul(twist_imag, sin_inner, precision=highest)  59.2 us
    unnamed x3, other arithmetic  58.1 us
    dot_general x8, matrix products, transform_last(): jnp.einsum('kn,...nq->...kq', sin_outer, shaped_real, precision=highest)  49.7 us
  transfers between devices with their start and end apart: 4, of which 4 were waited for; matrix products, arithmetic and copies ran while one was open for 5% of the time, Pallas kernels for 0%

commit v1 on v0

--- a/solution.py
+++ b/solution.py
@@ -1,8 +1,12 @@
+import functools
 import math
 
 import jax
 import jax.numpy as jnp
+import numpy as np
 from jax import lax
+from jax.experimental import pallas as pl
+from jax.experimental.pallas import tpu as pltpu
 from jax.sharding import PartitionSpec as P
 
 NX = 4096
@@ -99,7 +103,7 @@
     return field_real * scale
 
 
-def local(velocity, kernel, history, impedance, prestress, strength, fault_state):
+def local_general(velocity, kernel, history, impedance, prestress, strength, fault_state):
     side_index = lax.axis_index("side")
     is_first = side_index == 0
     eta_first = impedance[0]
@@ -144,6 +148,578 @@
     return (speed[None], rate, state_now)
 
 
+RADIX = 16
+CHUNKS = 2
+f32 = jnp.float32
+bf16 = jnp.bfloat16
+
+
+def constant_tables():
+    inner = NX // RADIX
+    grid = np.outer(np.arange(inner), np.arange(inner)) % inner
+    phase = grid * (2.0 * np.pi / inner)
+    cos, sin = np.cos(phase), np.sin(phase)
+    full = np.concatenate(
+        [np.concatenate([cos, sin], 1), np.concatenate([-sin, cos], 1)], 0
+    ).astype(np.float32)
+    high = full.astype(jnp.bfloat16)
+    low = (full - high.astype(np.float32)).astype(jnp.bfloat16)
+    table = np.concatenate([high, high, low], 1)
+    turn = np.outer(np.arange(RADIX), np.arange(inner)) * (2.0 * np.pi / NX)
+    twist = np.stack([np.cos(turn), np.sin(turn)]).astype(np.float32)
+    return table, twist
+
+
+def plus(a, b):
+    return tuple(
+        (p if q is None else q if p is None else p + q) for p, q in zip(a, b)
+    )
+
+
+def minus(a, b):
+    return tuple(
+        (p if q is None else -q if p is None else p - q) for p, q in zip(a, b)
+    )
+
+
+def times_i(a, sign):
+    real, imag = a
+    if sign > 0:
+        return (None if imag is None else -imag, real)
+    return (imag, None if real is None else -real)
+
+
+def turned_by(a, cos, sin):
+    real, imag = a
+    if imag is None:
+        return (real * cos, real * sin)
+    if real is None:
+        return (-(imag * sin), imag * cos)
+    return (real * cos - imag * sin, real * sin + imag * cos)
+
+
+def four(x, sign):
+    a, b = plus(x[0], x[2]), minus(x[0], x[2])
+    c, d = plus(x[1], x[3]), times_i(minus(x[1], x[3]), sign)
+    return [plus(a, c), plus(b, d), minus(a, c), minus(b, d)]
+
+
+def sixteen(x, sign):
+    rows = [four([x[4 * m + n] for m in range(4)], sign) for n in range(4)]
+    out = [None] * 16
+    for k in range(4):
+        terms = []
+        for n in range(4):
+            power = n * k
+            term = rows[n][k]
+            if power == 4:
+                term = times_i(term, sign)
+            elif power:
+                angle = 2.0 * math.pi * power / 16
+                term = turned_by(term, math.cos(angle), sign * math.sin(angle))
+            terms.append(term)
+        for m, value in enumerate(four(terms, sign)):
+            out[k + 4 * m] = value
+    return out
+
+
+def store_split(held, k, group, lane, first, second):
+    inner = NX // RADIX
+    rows = pl.ds(pl.multiple_of(group * 16 + (k % 2) * 128, 16), 16)
+    for place, value in ((0, first), (1, second)):
+        high = value.astype(bf16)
+        low = (value - high.astype(f32)).astype(bf16)
+        held[k // 2, rows, pl.ds(place * inner + lane, 128)] = high
+        held[k // 2, rows, pl.ds((2 + place) * inner + lane, 128)] = low
+
+
+def twisted(value, twist, k, lane, sign):
+    if k == 0:
+        real, imag = value
+        return (real, jnp.zeros_like(real) if imag is None else imag)
+    cos = twist[0, k : k + 1, pl.ds(lane, 128)]
+    sin = twist[1, k : k + 1, pl.ds(lane, 128)]
+    return turned_by(value, cos, sin if sign > 0 else -sin)
+
+
+def product(table, held, k, start):
+    wide = table.shape[1] // 3
+    rows = pl.ds(start, table.shape[0] - start)
+    dims = (((1,), (1,)), ((), ()))
+    return lax.dot_general(
+        table[rows, : 2 * wide], held[k], dims, preferred_element_type=f32
+    ) + lax.dot_general(
+        table[rows, 2 * wide :], held[k, :, :wide], dims, preferred_element_type=f32
+    )
+
+
+def picked(refs, half):
+    return (refs[0], half) if len(refs) == 1 else (refs[half], 0)
+
+
+def forward_rows(rows_ref, table, twist, outs, held):
+    rows, length = rows_ref.shape
+    inner = length // RADIX
+
+    def group(g, carry):
+        at = pl.ds(pl.multiple_of(g * 16, 16), 16)
+        for lane in range(0, inner, 128):
+            values = [(rows_ref[at, pl.ds(n * inner + lane, 128)], None) for n in range(RADIX)]
+            for k, value in enumerate(sixteen(values, -1)):
+                store_split(held, k, g, lane, *twisted(value, twist, k, lane, -1))
+        return carry
+
+    lax.fori_loop(0, rows // 16, group, 0)
+
+    def wave(pair, carry):
+        both = product(table, held, pair, 0)
+        slabs, halves = outs[0].shape[0], 2
+        per = inner // slabs // halves
+        for slab in range(slabs):
+            for half in range(halves):
+                out, place = picked(outs, half)
+                for part in range(2):
+                    first = part * inner + (slab * halves + half) * per
+                    for odd in range(2):
+                        out[slab, place, part, pl.ds(2 * pair + odd, per, RADIX), :] = both[
+                            first : first + per, odd * 128 : odd * 128 + 128
+                        ]
+        return carry
+
+    lax.fori_loop(0, RADIX // 2, wave, 0)
+
+
+def start_kernel(velocity, table, twist, *refs):
+    forward_rows(velocity.at[0], table, twist, refs[:-1], refs[-1])
+
+
+def friction(scalars, own, other, prestress, strength, state):
+    weight_own, weight_other, joint, eta, sign = [scalars[n] for n in range(5)]
+    locked = prestress + (weight_own * own + weight_other * other)
+    rate = locked / (joint + strength)
+    factor = 0.5 * jnp.exp(state)
+    for iteration in range(NEWTON):
+        scaled = factor * rate
+        misfit = strength * inverse_sinh(scaled) + joint * rate - locked
+        slope = strength * factor / jnp.sqrt(1.0 + scaled * scaled) + joint
+        rate = rate - 0.5 * misfit / slope
+    stress = locked - joint * rate
+    speed = sign * (prestress + own - stress) / eta
+    state_new = state + 0.25 * (jnp.exp(-state) - jnp.abs(rate))
+    return speed, rate, state_new
+
+
+def middle_kernel(scalars, own, other, prestress, strength, state, table, twist, *refs):
+    outs = refs[:-3]
+    state_out, held, speed_held = refs[-3:]
+
+    def group(g, carry):
+        at = pl.ds(pl.multiple_of(g * 8, 8), 8)
+        for lane in range(0, own.shape[1], 1024):
+            cols = pl.ds(lane, 1024)
+            speed, rate, state_new = friction(
+                scalars,
+                own[at, cols],
+                other[at, cols],
+                prestress[at, cols],
+                strength[at, cols],
+                state[at, cols],
+            )
+            speed_held[at, cols] = speed
+            state_out[at, cols] = state_new
+        return carry
+
+    lax.fori_loop(0, own.shape[0] // 8, group, 0)
+    forward_rows(speed_held, table, twist, outs, held)
+
+
+def end_kernel(scalars, own, other, prestress, strength, state, *refs):
+    speed_out, rate_out, state_out = refs[-3:]
+
+    def group(g, carry):
+        at = pl.ds(pl.multiple_of(g * 8, 8), 8)
+        for lane in range(0, own.shape[1], 1024):
+            cols = pl.ds(lane, 1024)
+            speed, rate, state_new = friction(
+                scalars,
+                own[at, cols],
+                other[at, cols],
+                prestress[at, cols],
+                strength[at, cols],
+                state[at, cols],
+            )
+            speed_out[0, at, cols] = speed
+            rate_out[at, cols] = rate
+            state_out[at, cols] = state_new
+        return carry
+
+    lax.fori_loop(0, own.shape[0] // 8, group, 0)
+
+
+def history_kernel(kernel, history, now, later):
+    def group(g, carry):
+        cols = pl.ds(pl.multiple_of(g * 256, 256), 256)
+        lags = [kernel[0, n, :, cols].astype(f32) for n in range(kernel.shape[1])]
+        for part in range(2):
+            total_now = total_later = 0.0
+            for n in range(history.shape[1]):
+                past = history[0, n, part, :, cols].astype(f32)
+                total_now = total_now + lags[n + 1] * past
+                if n + 2 < len(lags):
+                    total_later = total_later + lags[n + 2] * past
+            now[part, :, cols] = total_now
+            later[part, :, cols] = total_later
+        return carry
+
+    lax.fori_loop(0, now.shape[2] // 256, group, 0)
+
+
+def spectral_kernel(has_past, half, *refs):
+    blocks = refs[:CHUNKS]
+    kernel_now, past_sum, table, twist = refs[CHUNKS : CHUNKS + 4]
+    rest = list(refs[CHUNKS + 4 :])
+    if has_past:
+        kernel_past, spec_past = rest.pop(0), rest.pop(0)
+        spec_out = None
+    if half > 0:
+        rest.pop(0)
+    outs, rest = rest[:CHUNKS], rest[CHUNKS:]
+    if not has_past:
+        spec_out = rest.pop(0)
+    held, turned, total = rest
+    rows = blocks[0].shape[3]
+    inner = RADIX * 16
+    length = total.shape[2]
+
+    def group(g, carry):
+        at = pl.ds(pl.multiple_of(g * 16, 16), 16)
+        for chunk in range(CHUNKS):
+            values = [
+                (blocks[chunk][n, 0, 0, at, :], blocks[chunk][n, 0, 1, at, :])
+                for n in range(RADIX)
+            ]
+            lane = chunk * 128
+            for k, value in enumerate(sixteen(values, -1)):
+                store_split(held, k, g, lane, *twisted(value, twist, k, lane, -1))
+        return carry
+
+    lax.fori_loop(0, rows // 16, group, 0)
+
+    def wave(pair, carry):
+        both = product(table, held, pair, 0)
+        for odd in range(2):
+            for part in range(2):
+                turned[part, pl.ds(2 * pair + odd, inner, RADIX), :] = both[
+                    part * inner : part * inner + inner, odd * 128 : odd * 128 + 128
+                ]
+        return carry
+
+    lax.fori_loop(0, RADIX // 2, wave, 0)
+
+    def convolve(b, carry):
+        cols = pl.ds(pl.multiple_of(b * 256, 256), 256)
+        weight = kernel_now[0, 0, :, cols].astype(f32)
+        for part in range(2):
+            spec = turned[part, cols, :].T.astype(bf16)
+            value = weight * spec.astype(f32) + past_sum[part, :, cols]
+            if has_past:
+                value = value + kernel_past[0, 0, :, cols].astype(f32) * spec_past[
+                    part, :, cols
+                ].astype(f32)
+            else:
+                spec_out[part, :, cols] = spec
+            total[part, :, cols] = value
+        return carry
+
+    lax.fori_loop(0, length // 256, convolve, 0)
+
+    def group_back(g, carry):
+        at = pl.ds(pl.multiple_of(g * 16, 16), 16)
+        for lane in range(0, inner, 128):
+            values = [
+                (total[0, at, pl.ds(n * inner + lane, 128)], total[1, at, pl.ds(n * inner + lane, 128)])
+                for n in range(RADIX)
+            ]
+            for k, value in enumerate(sixteen(values, 1)):
+                real, imag = twisted(value, twist, k, lane, 1)
+                store_split(held, k, g, lane, imag, real)
+        return carry
+
+    lax.fori_loop(0, rows // 16, group_back, 0)
+
+    def wave_back(pair, carry):
+        both = product(table, held, pair, 0)
+        slabs = outs[0].shape[0]
+        per = inner // slabs // CHUNKS
+        for slab in range(slabs):
+            for chunk in range(CHUNKS):
+                for part in range(2):
+                    first = (1 - part) * inner + (slab * CHUNKS + chunk) * per
+                    for odd in range(2):
+                        outs[chunk][slab, 0, part, pl.ds(2 * pair + odd, per, RADIX), :] = both[
+                            first : first + per, odd * 128 : odd * 128 + 128
+                        ]
+        return carry
+
+    lax.fori_loop(0, RADIX // 2, wave_back, 0)
+
+
+def inverse_kernel(count, *refs):
+    blocks = refs[:count]
+    table, twist, out, held, turned = refs[count:]
+    rows, length = out.shape
+    inner = length // RADIX
+
+    def group(g, carry):
+        at = pl.ds(pl.multiple_of(g * 16, 16), 16)
+        for half in range(inner // 128):
+            block, place = picked(blocks, half)
+            values = [(block[n, place, 0, at, :], block[n, place, 1, at, :]) for n in range(RADIX)]
+            for k, value in enumerate(sixteen(values, 1)):
+                real, imag = twisted(value, twist, k, half * 128, 1)
+                store_split(held, k, g, half * 128, imag, real)
+        return carry
+
+    lax.fori_loop(0, rows // 16, group, 0)
+
+    def wave(pair, carry):
+        both = product(table, held, pair, inner)
+        for odd in range(2):
+            turned[pl.ds(2 * pair + odd, inner, RADIX), :] = both[:, odd * 128 : odd * 128 + 128]
+        return carry
+
+    lax.fori_loop(0, RADIX // 2, wave, 0)
+    scale = 1.0 / (NX * NZ)
+
+    def turn(b, carry):
+        cols = pl.ds(pl.multiple_of(b * 256, 256), 256)
+        out[:, cols] = turned[cols, :].T * scale
+        return carry
+
+    lax.fori_loop(0, length // 256, turn, 0)
+
+
+def whole_spec(array):
+    zeros = (0,) * array.ndim
+    return pl.BlockSpec(array.shape, lambda *_: zeros)
+
+
+PARAMS = pltpu.CompilerParams(vmem_limit_bytes=62 * 1024 * 1024)
+SCALARS = pl.BlockSpec(memory_space=pltpu.SMEM)
+
+
+def exchanged(value):
+    return lax.all_to_all(value, "slab", split_axis=0, concat_axis=0, tiled=True)
+
+
+def local(velocity, kernel, history, impedance, prestress, strength, fault_state):
+    slabs = lax.axis_size("slab")
+    rows_dev, length = prestress.shape
+    inner = length // RADIX
+    chunk_rows = rows_dev // CHUNKS
+    halves = rows_dev // 128
+    if slabs != RADIX or rows_dev != inner or chunk_rows != 128:
+        return local_general(
+            velocity, kernel, history, impedance, prestress, strength, fault_state
+        )
+    lags = history.shape[1]
+    table_np, twist_np = constant_tables()
+    table, twist = jnp.asarray(table_np), jnp.asarray(twist_np)
+    is_first = lax.axis_index("side") == 0
+    eta_first, eta_second = impedance[0], impedance[1]
+    eta_total = eta_first + eta_second
+    weight_first, weight_second = eta_second / eta_total, eta_first / eta_total
+    scalars = jnp.stack(
+        [
+            jnp.where(is_first, weight_first, weight_second),
+            jnp.where(is_first, weight_second, weight_first),
+            eta_first * eta_second / eta_total,
+            jnp.where(is_first, eta_first, eta_second),
+            jnp.where(is_first, 1.0, -1.0).astype(f32),
+        ]
+    )
+    def tiles(counts):
+        return [jax.ShapeDtypeStruct((slabs, count, 2, 128, 128), f32) for count in counts]
+
+    def tile_specs(counts):
+        return [pl.BlockSpec((slabs, count, 2, 128, 128), lambda *_: (0,) * 5) for count in counts]
+
+    forward_cut = [[2], [1, 1]]
+    held = pltpu.VMEM((RADIX // 2, 256, 4 * inner), bf16)
+    rows_shape = jax.ShapeDtypeStruct((chunk_rows, length), f32)
+    rows_spec = pl.BlockSpec((chunk_rows, length), lambda *_: (0, 0))
+
+    def chunk_spec(chunk):
+        return pl.BlockSpec((chunk_rows, length), lambda *_: (chunk, 0))
+
+    def start(chunk):
+        return pl.pallas_call(
+            start_kernel,
+            out_shape=tiles(forward_cut[chunk]),
+            grid=(1,),
+            in_specs=[
+                pl.BlockSpec((1, chunk_rows, length), lambda *_: (0, chunk, 0)),
+                whole_spec(table),
+                whole_spec(twist),
+            ],
+            out_specs=tile_specs(forward_cut[chunk]),
+            scratch_shapes=[held],
+            compiler_params=PARAMS,
+        )(velocity, table, twist)
+
+    def middle(chunk, own, other, state):
+        *sent, state_new = pl.pallas_call(
+            middle_kernel,
+            out_shape=tiles(forward_cut[chunk]) + [rows_shape],
+            grid=(1,),
+            in_specs=[
+                SCALARS,
+                rows_spec,
+                rows_spec,
+                chunk_spec(chunk),
+                chunk_spec(chunk),
+                chunk_spec(chunk),
+                whole_spec(table),
+                whole_spec(twist),
+            ],
+            out_specs=tile_specs(forward_cut[chunk]) + [rows_spec],
+            scratch_shapes=[held, pltpu.VMEM((chunk_rows, length), f32)],
+            compiler_params=PARAMS,
+        )(scalars, own, other, prestress, strength, state, table, twist)
+        return sent, state_new
+
+    def end(chunk, own, other, state, before):
+        full = jax.ShapeDtypeStruct((rows_dev, length), f32)
+        step = 32
+        parts = chunk_rows // step
+        base = chunk * parts
+        moving = pl.BlockSpec((step, length), lambda g: (base + g, 0))
+        near = pl.BlockSpec((step, length), lambda g: (g, 0))
+        moving_speed = pl.BlockSpec((1, step, length), lambda g: (0, base + g, 0))
+        kept = [pl.BlockSpec(memory_space=pl.ANY)] * len(before)
+        return pl.pallas_call(
+            end_kernel,
+            out_shape=(jax.ShapeDtypeStruct((1, rows_dev, length), f32), full, full),
+            grid=(parts,),
+            in_specs=[SCALARS, near, near, moving, moving, near] + kept,
+            out_specs=(moving_speed, moving, moving),
+            input_output_aliases={6 + n: n for n in range(len(before))},
+            compiler_params=PARAMS,
+        )(scalars, own, other, prestress, strength, state, *before)
+
+    def past_sums():
+        step = 32
+        total = jax.ShapeDtypeStruct((2, rows_dev, length), f32)
+        spec = pl.BlockSpec((2, step, length), lambda g: (0, g, 0))
+        return pl.pallas_call(
+            history_kernel,
+            out_shape=(total, total),
+            grid=(rows_dev // step,),
+            in_specs=[
+                pl.BlockSpec((1, lags + 1, step, length), lambda g: (0, 0, g, 0)),
+                pl.BlockSpec((1, lags, 2, step, length), lambda g: (0, 0, 0, g, 0)),
+            ],
+            out_specs=(spec, spec),
+            compiler_params=PARAMS,
+        )(kernel, history)
+
+    def spectral(half, blocks, past_sum, past, before):
+        def block(array):
+            place = half if array.shape[1] == halves else 0
+            return pl.BlockSpec((slabs, 1, 2, 128, 128), lambda *_: (0, place, 0, 0, 0))
+
+        lag_spec = [
+            pl.BlockSpec((1, 1, 128, length), functools.partial(lambda lag, *_: (0, lag, half, 0), lag))
+            for lag in range(2)
+        ]
+        sum_spec = pl.BlockSpec((2, 128, length), lambda *_: (0, half, 0))
+        spec_spec = pl.BlockSpec((2, 128, length), lambda *_: (0, 0, 0))
+        operands = list(blocks) + [kernel, past_sum, table, twist]
+        in_specs = [block(b) for b in blocks]
+        in_specs += [lag_spec[0], sum_spec, whole_spec(table), whole_spec(twist)]
+        out_shape = tiles([1, halves])
+        out_specs = [block(shape) for shape in out_shape]
+        if past is not None:
+            operands += [kernel, past]
+            in_specs += [lag_spec[1], spec_spec]
+        else:
+            out_shape.append(jax.ShapeDtypeStruct((2, 128, length), bf16))
+            out_specs.append(spec_spec)
+        aliases = {}
+        if before is not None:
+            aliases = {len(operands): 1}
+            operands.append(before)
+            in_specs.append(pl.BlockSpec(memory_space=pl.ANY))
+        return pl.pallas_call(
+            functools.partial(spectral_kernel, past is not None, half),
+            input_output_aliases=aliases,
+            out_shape=out_shape,
+            grid=(1,),
+            in_specs=in_specs,
+            out_specs=out_specs,
+            scratch_shapes=[
+                held,
+                pltpu.VMEM((2, length, 128), f32),
+                pltpu.VMEM((2, 128, length), f32),
+            ],
+            compiler_params=PARAMS,
+        )(*operands)
+
+    def inverse(*blocks):
+        return pl.pallas_call(
+            functools.partial(inverse_kernel, len(blocks)),
+            out_shape=rows_shape,
+            grid=(1,),
+            in_specs=tile_specs([b.shape[1] for b in blocks]) + [whole_spec(table), whole_spec(twist)],
+            out_specs=rows_spec,
+            scratch_shapes=[held, pltpu.VMEM((length, 128), f32)],
+            compiler_params=PARAMS,
+        )(*blocks, table, twist)
+    hold = lax.optimization_barrier
+    sent = [start(0), None]
+    states = [fault_state] * CHUNKS
+    past = [None] * halves
+    sums, results, waiting = None, (), None
+    for step_index in range(STEPS):
+        last = step_index == STEPS - 1
+        first = exchanged(sent[0][0])
+        if step_index == 0:
+            sent[1] = start(1)
+        else:
+            own = inverse(waiting)
+            sent[1], states[1] = middle(1, own, swapped(own, "side", 0), states[1])
+        first, sent[1], states[1] = hold((first, sent[1], states[1]))
+        near = exchanged(sent[1][0])
+        if step_index == 0:
+            sums = past_sums()
+        near, far, sums = hold((near, sent[1][1], sums))
+        far = exchanged(far)
+        outs = spectral(0, (first, near), sums[step_index], past[0], None)
+        if step_index == 0:
+            past[0] = outs[2]
+        back, late = outs[0], outs[1]
+        far, back, late = hold((far, back, late))
+        back = exchanged(back)
+        outs = spectral(1, (first, far), sums[step_index], past[1], late)
+        if step_index == 0:
+            past[1] = outs[2]
+        back, more, late = hold((back, outs[0], outs[1]))
+        more = exchanged(more)
+        more, late = hold((more, late))
+        waiting = exchanged(late)
+        own = inverse(back, more)
+        other = swapped(own, "side", 0)
+        if last:
+            results = end(0, own, other, states[0], results)
+            waiting, results = hold((waiting, tuple(results)))
+            own = inverse(waiting)
+            results = end(1, own, swapped(own, "side", 0), states[1], results)
+        else:
+            sent[0], states[0] = middle(0, own, other, states[0])
+            waiting, sent[0], states[0] = hold((waiting, sent[0], states[0]))
+    return tuple(results)
+
+
 def solution(mesh):
     placed = (
         P("side", "slab", None),

time: 1650 us -> 902 us (0.55)
  matrix products: 396 us -> 0 us
  Pallas kernels: 0 us -> 295 us
  blocking collectives: 437 us -> 170 us
  local copies, waits for them, and re-layouts: 239 us -> 1.31 us
  other arithmetic: 139 us -> 0 us
  waiting for transfers between devices: 405 us -> 327 us
  starting transfers between devices: 15.7 us -> 89 us
    dot_general x56 -> x0, matrix products: 396 us -> none  [the longest x8 74.7 us: transform_last(): jnp.matmul(twist_real, cos_inner, precision=highest)]
    pallas_call x0 -> x15, Pallas kernels: none -> 295 us  [the longest x4 98.5 us: spectral(): pl.pallas_call(functools.partial(spectral_kernel, past is not None, half)...]
    all_to_all x2 -> x3, blocking collectives: 437 us -> 170 us  [exchanged(): lax.all_to_all(value, 'slab', split_axis=0, concat_axis=0, tiled=True)]
    all_to_all x2 -> x9, waiting for transfers between devices: 244 us -> 148 us  [exchanged(): lax.all_to_all(value, 'slab', split_axis=0, concat_axis=0, tiled=True)]
    all_to_all x2 -> x9, starting transfers between devices: 12.6 us -> 82.9 us  [exchanged(): lax.all_to_all(value, 'slab', split_axis=0, concat_axis=0, tiled=True)]
    unnamed x3 -> x0, other arithmetic: 58.1 us -> none
    another operation x13 -> x1, local copies, waits for them, and re-layouts: 55.6 us -> 0.67 us  [local(): jnp.stack([jnp.where(is_first, weight_first, weight_second), jnp.where(is...]
    slice x6 -> x1, local copies, waits for them, and re-layouts: 43.4 us -> 0.64 us  [local(): eta_first, eta_second = (impedance[0], impedance[1])]
  transfers between devices with their start and end apart: 4 -> 13, of which waited for: 4 -> 10; matrix products, arithmetic and copies ran while one was open for 5% -> 0% of each run, Pallas kernels for 0% -> 28%
where the time goes in v1:
time: 902 us; the launch traced here: 889 us
  waiting for transfers between devices  327 us (36%)
  Pallas kernels  295 us (33%)
  blocking collectives  170 us (19%)
  starting transfers between devices  89 us (10%)
    ppermute x4, waiting for transfers between devices, swapped(): return lax.ppermute(value, axis, pairs)  179 us
    all_to_all x3, blocking collectives, exchanged(): lax.all_to_all(value, 'slab', split_axis=0, concat_axis=0, tiled=True)  170 us
    all_to_all x9, waiting for transfers between devices, exchanged(): lax.all_to_all(value, 'slab', split_axis=0, concat_axis=0, tiled=True)  148 us
    pallas_call x4, Pallas kernels, spectral(): pl.pallas_call(functools.partial(spectral_kernel, past is not None, half)...  98.5 us
    all_to_all x9, starting transfers between devices, exchanged(): lax.all_to_all(value, 'slab', split_axis=0, concat_axis=0, tiled=True)  82.9 us
    pallas_call x2, Pallas kernels, middle(): pl.pallas_call(middle_kernel, out_shape=tiles(forward_cut[chunk]) + [rows...  63 us
    pallas_call x4, Pallas kernels, inverse(): pl.pallas_call(functools.partial(inverse_kernel, len(blocks)), out_shape=...  45.9 us
    pallas_call x2, Pallas kernels, end(): pl.pallas_call(end_kernel, out_shape=(jax.ShapeDtypeStruct((1, rows_dev,...  40.2 us
  transfers between devices with their start and end apart: 13, of which 10 were waited for; matrix products, arithmetic and copies ran while one was open for 0% of the time, Pallas kernels for 28%

profile of v1, /device:TPU:0, one launch (start us, length us, event | category | flops | bytes accessed | tf_op | source)
XLA Modules:
  0.0 888.8 jit_solution(12175405605995293487)
XLA Ops:
  0.6 11.5 %shard_map.112 = f32[16,2,2,128,128]{4,3,2,1,0:T(8,128)} custom-call(f32[1,256,4096]{2,1,0:T(8,128)} %velocity.3, bf16[512,1536]{1,0:T(8,128)(2,1)} %constant.16.clone.table.refs_4_.refs_2_.refs_1_, f32[2,16,256]{2,1,0:T(8,128)} %constant.17.clone.twist.refs_5_.refs_3_.refs_2_), custom_call_target="tpu_custom_call" | custom-call | tf_op jit(solution)/shard_map/pallas_call | solution.py:556
  31.1 66.1 %all-to-all-done.refs_0_ = f32[16,2,2,128,128]{4,3,2,1,0:T(8,128)} async-done(((f32[16,2,2,128,128]{4,3,2,1,0:T(8,128)}), f32[16,2,2,128,128]{4,3,2,1,0:T(8,128)}, u32[]{:S(2)}, u32[]{:S(2)}) %all-to-all-start) | async-done | bytes 4194336 | tf_op jit(solution)/shard_map/all_to_all | solution.py:512
  97.1 19.7 %all-to-all-start.1 = ((f32[16,1,2,128,128]{4,3,2,1,0:T(8,128)}), f32[16,1,2,128,128]{4,3,2,1,0:T(8,128)}, u32[]{:S(2)}, u32[]{:S(2)}) async-start(f32[16,1,2,128,128]{4,3,2,1,0:T(8,128)} %get-tuple-element.65), calls=%async_computation.1 | async-start | bytes 4194304 | tf_op jit(solution)/shard_map/all_to_all | solution.py:512
  116.8 24.8 %shard_map.114 = (f32[2,256,4096]{2,1,0:T(8,128)}, f32[2,256,4096]{2,1,0:T(8,128)}) custom-call(bf16[1,9,256,4096]{3,2,1,0:T(8,128)(2,1)} %refs_6_.3, bf16[1,8,2,256,4096]{4,3,2,1,0:T(8,128)(2,1)} %history.1), custom_call_target="tpu_custom_call" | custom-call | tf_op jit(solution)/shard_map/pallas_call | solution.py:614
  141.6 16.2 %all-to-all-done.1.refs_1_ = f32[16,1,2,128,128]{4,3,2,1,0:T(8,128)} async-done(((f32[16,1,2,128,128]{4,3,2,1,0:T(8,128)}), f32[16,1,2,128,128]{4,3,2,1,0:T(8,128)}, u32[]{:S(2)}, u32[]{:S(2)}) %all-to-all-start.1) | async-done | bytes 2097184 | tf_op jit(solution)/shard_map/all_to_all | solution.py:512
  169.1 24.5 %shard_map.115 = (f32[16,1,2,128,128]{4,3,2,1,0:T(8,128)}, f32[16,2,2,128,128]{4,3,2,1,0:T(8,128)}, bf16[2,128,4096]{2,1,0:T(8,128)(2,1)}) custom-call(f32[16,2,2,128,128]{4,3,2,1,0:T(8,128)} %all-to-all-done.refs_0_, f32[16,1,2,128,128]{4,3,2,1,0:T(8,128)} %all-to-all-done.1.refs_1_, bf16[1,9,256,4096]{3,2,1,0:T(8,128)(2,1)} %refs_6_.3, ...), custom_call_target="tpu_custom_call" | custom-call | tf_op jit(solution)/shard_map/pallas_call | solution.py:653
  193.6 16.6 %all-to-all-done.2.refs_1_ = f32[16,1,2,128,128]{4,3,2,1,0:T(8,128)} async-done(((f32[16,1,2,128,128]{4,3,2,1,0:T(8,128)}), f32[16,1,2,128,128]{4,3,2,1,0:T(8,128)}, u32[]{:S(2)}, u32[]{:S(2)}) %all-to-all-start.2) | async-done | bytes 2097184 | tf_op jit(solution)/shard_map/all_to_all | solution.py:512
  221.4 24.4 %shard_map.116 = (f32[16,1,2,128,128]{4,3,2,1,0:T(8,128)}, f32[16,2,2,128,128]{4,3,2,1,0:T(8,128)}, bf16[2,128,4096]{2,1,0:T(8,128)(2,1)}) custom-call(f32[16,2,2,128,128]{4,3,2,1,0:T(8,128)} %all-to-all-done.refs_0_, f32[16,1,2,128,128]{4,3,2,1,0:T(8,128)} %all-to-all-done.2.refs_1_, ...), custom_call_target="tpu_custom_call", output_to_operand_aliasing={{1}: (6, {})} | custom-call | tf_op jit(solution)/shard_map/pallas_call | solution.py:653
  245.9 16.6 %all-to-all-done.3.refs_0_ = f32[16,1,2,128,128]{4,3,2,1,0:T(8,128)} async-done(((f32[16,1,2,128,128]{4,3,2,1,0:T(8,128)}), f32[16,1,2,128,128]{4,3,2,1,0:T(8,128)}, u32[]{:S(2)}, u32[]{:S(2)}) %all-to-all-start.3) | async-done | bytes 2097184 | tf_op jit(solution)/shard_map/all_to_all | solution.py:512
  262.5 58.5 %all_to_all.60.refs_1_ = f32[16,1,2,128,128]{4,3,2,1,0:T(8,128)} all-to-all(f32[16,1,2,128,128]{4,3,2,1,0:T(8,128)} %get-tuple-element.80), channel_id=1, replica_groups=mesh['side'=2,'slab'=16] {'slab'}, dimensions={0} | all-to-all | bytes 4194304 | tf_op jit(solution)/shard_map/all_to_all | solution.py:512
  345.5 40.2 %collective-permute-done.other = f32[128,4096]{1,0:T(8,128)} collective-permute-done((f32[128,4096]{1,0:T(8,128)}, f32[128,4096]{1,0:T(8,128)}, u32[]{:S(2)}, u32[]{:S(2)}) %collective-permute-start) | collective-permute-done | bytes 2097184 | tf_op jit(solution)/shard_map/ppermute | solution.py:24
  385.8 31.2 %shard_map.118 = (f32[16,2,2,128,128]{4,3,2,1,0:T(8,128)}, f32[128,4096]{1,0:T(8,128)}) custom-call(f32[5]{0:T(128)} %stack.23.scalars, f32[128,4096]{1,0:T(8,128)} %shard_map.117.own, f32[128,4096]{1,0:T(8,128)} %collective-permute-done.other, f32[256,4096]{1,0:T(8,128)} %prestress.7, f32[256,4096]{1,0:T(8,128)} %strength.7, f32[256,4096]{1,0:T(8,128)} %state.2, ...), custom_call_target="tpu_custom_call" | custom-call | tf_op jit(solution)/shard_map/pallas_call | solution.py:571
  436.3 46.7 %collective-permute-done.1.other = f32[128,4096]{1,0:T(8,128)} collective-permute-done((f32[128,4096]{1,0:T(8,128)}, f32[128,4096]{1,0:T(8,128)}, u32[]{:S(2)}, u32[]{:S(2)}) %collective-permute-start.1) | collective-permute-done | bytes 2097184 | tf_op jit(solution)/shard_map/ppermute | solution.py:24
  483.0 31.9 %shard_map.120 = (f32[16,1,2,128,128]{4,3,2,1,0:T(8,128)}, f32[16,1,2,128,128]{4,3,2,1,0:T(8,128)}, f32[128,4096]{1,0:T(8,128)}) custom-call(f32[5]{0:T(128)} %stack.23.scalars, f32[128,4096]{1,0:T(8,128)} %shard_map.119.own, f32[128,4096]{1,0:T(8,128)} %collective-permute-done.1.other, f32[256,4096]{1,0:T(8,128)} %prestress.7, f32[256,4096]{1,0:T(8,128)} %strength.7, ...), custom_call_target="tpu_custom_call" | custom-call | tf_op jit(solution)/shard_map/pallas_call | solution.py:571
  514.9 53.0 %all_to_all.61.refs_1_ = f32[16,1,2,128,128]{4,3,2,1,0:T(8,128)} all-to-all(f32[16,1,2,128,128]{4,3,2,1,0:T(8,128)} %get-tuple-element.93), channel_id=1, replica_groups=mesh['side'=2,'slab'=16] {'slab'}, dimensions={0} | all-to-all | bytes 4194304 | tf_op jit(solution)/shard_map/all_to_all | solution.py:512
  573.0 24.8 %shard_map.121 = (f32[16,1,2,128,128]{4,3,2,1,0:T(8,128)}, f32[16,2,2,128,128]{4,3,2,1,0:T(8,128)}) custom-call(f32[16,2,2,128,128]{4,3,2,1,0:T(8,128)} %all-to-all-done.6.refs_0_, f32[16,1,2,128,128]{4,3,2,1,0:T(8,128)} %all_to_all.61.refs_1_, bf16[1,9,256,4096]{3,2,1,0:T(8,128)(2,1)} %refs_6_.3, f32[2,256,4096]{2,1,0:T(8,128)} %get-tuple-element.99.refs_3_, ...), custom_call_target="tpu_custom_call" | custom-call | tf_op jit(solution)/shard_map/pallas_call | solution.py:653
  597.9 16.2 %all-to-all-done.8.refs_1_ = f32[16,1,2,128,128]{4,3,2,1,0:T(8,128)} async-done(((f32[16,1,2,128,128]{4,3,2,1,0:T(8,128)}), f32[16,1,2,128,128]{4,3,2,1,0:T(8,128)}, u32[]{:S(2)}, u32[]{:S(2)}) %all-to-all-start.8) | async-done | bytes 2097184 | tf_op jit(solution)/shard_map/all_to_all | solution.py:512
  625.3 24.8 %shard_map.122 = (f32[16,1,2,128,128]{4,3,2,1,0:T(8,128)}, f32[16,2,2,128,128]{4,3,2,1,0:T(8,128)}) custom-call(f32[16,2,2,128,128]{4,3,2,1,0:T(8,128)} %all-to-all-done.6.refs_0_, f32[16,1,2,128,128]{4,3,2,1,0:T(8,128)} %all-to-all-done.8.refs_1_, bf16[1,9,256,4096]{3,2,1,0:T(8,128)(2,1)} %refs_6_.3, ...), custom_call_target="tpu_custom_call", output_to_operand_aliasing={{1}: (8, {})} | custom-call | tf_op jit(solution)/shard_map/pallas_call | solution.py:653
  650.2 16.2 %all-to-all-done.9.refs_0_ = f32[16,1,2,128,128]{4,3,2,1,0:T(8,128)} async-done(((f32[16,1,2,128,128]{4,3,2,1,0:T(8,128)}), f32[16,1,2,128,128]{4,3,2,1,0:T(8,128)}, u32[]{:S(2)}, u32[]{:S(2)}) %all-to-all-start.9) | async-done | bytes 2097184 | tf_op jit(solution)/shard_map/all_to_all | solution.py:512
  666.4 58.5 %all_to_all.62.refs_1_ = f32[16,1,2,128,128]{4,3,2,1,0:T(8,128)} all-to-all(f32[16,1,2,128,128]{4,3,2,1,0:T(8,128)} %get-tuple-element.109), channel_id=1, replica_groups=mesh['side'=2,'slab'=16] {'slab'}, dimensions={0} | all-to-all | bytes 4194304 | tf_op jit(solution)/shard_map/all_to_all | solution.py:512
  743.1 46.7 %collective-permute-done.2.other = f32[128,4096]{1,0:T(8,128)} collective-permute-done((f32[128,4096]{1,0:T(8,128)}, f32[128,4096]{1,0:T(8,128)}, u32[]{:S(2)}, u32[]{:S(2)}) %collective-permute-start.2) | collective-permute-done | bytes 2097184 | tf_op jit(solution)/shard_map/ppermute | solution.py:24
  789.7 20.1 %shard_map.124 = (f32[1,256,4096]{2,1,0:T(8,128)}, f32[256,4096]{1,0:T(8,128)}, f32[256,4096]{1,0:T(8,128)}) custom-call(f32[5]{0:T(128)} %stack.23.scalars, f32[128,4096]{1,0:T(8,128)} %shard_map.123.own, f32[128,4096]{1,0:T(8,128)} %collective-permute-done.2.other, f32[256,4096]{1,0:T(8,128)} %prestress.7, f32[256,4096]{1,0:T(8,128)} %strength.7, ...), custom_call_target="tpu_custom_call" | custom-call | tf_op jit(solution)/shard_map/pallas_call | solution.py:600
  822.9 45.8 %collective-permute-done.3.other = f32[128,4096]{1,0:T(8,128)} collective-permute-done((f32[128,4096]{1,0:T(8,128)}, f32[128,4096]{1,0:T(8,128)}, u32[]{:S(2)}, u32[]{:S(2)}) %collective-permute-start.3) | collective-permute-done | bytes 2097184 | tf_op jit(solution)/shard_map/ppermute | solution.py:24
  868.7 20.1 %shard_map.126 = (f32[1,256,4096]{2,1,0:T(8,128)}, f32[256,4096]{1,0:T(8,128)}, f32[256,4096]{1,0:T(8,128)}) custom-call(f32[5]{0:T(128)} %stack.23.scalars, f32[128,4096]{1,0:T(8,128)} %shard_map.125.own, f32[128,4096]{1,0:T(8,128)} %collective-permute-done.3.other, ...), custom_call_target="tpu_custom_call", output_to_operand_aliasing={{0}: (6, {}), {1}: (7, {}), {2}: (8, {})} | custom-call | tf_op jit(solution)/shard_map/pallas_call | solution.py:600
  (24 shorter events, 128.0 us)
Async XLA Ops:
  12.1 85.0 %all-to-all-start = ((f32[16,2,2,128,128]{4,3,2,1,0:T(8,128)}), f32[16,2,2,128,128]{4,3,2,1,0:T(8,128)}, u32[]{:S(2)}, u32[]{:S(2)}) async-start(f32[16,2,2,128,128]{4,3,2,1,0:T(8,128)} %shard_map.112), calls=%async_computation | async-start | bytes 8388608 | tf_op jit(solution)/shard_map/all_to_all | solution.py:512
  97.1 60.7 %all-to-all-start.1 = ((f32[16,1,2,128,128]{4,3,2,1,0:T(8,128)}), f32[16,1,2,128,128]{4,3,2,1,0:T(8,128)}, u32[]{:S(2)}, u32[]{:S(2)}) async-start(f32[16,1,2,128,128]{4,3,2,1,0:T(8,128)} %get-tuple-element.65), calls=%async_computation.1 | async-start | bytes 4194304 | tf_op jit(solution)/shard_map/all_to_all | solution.py:512
  157.8 52.3 %all-to-all-start.2 = ((f32[16,1,2,128,128]{4,3,2,1,0:T(8,128)}), f32[16,1,2,128,128]{4,3,2,1,0:T(8,128)}, u32[]{:S(2)}, u32[]{:S(2)}) async-start(f32[16,1,2,128,128]{4,3,2,1,0:T(8,128)} %get-tuple-element.69), calls=%async_computation.2 | async-start | bytes 4194304 | tf_op jit(solution)/shard_map/all_to_all | solution.py:512
  210.1 52.3 %all-to-all-start.3 = ((f32[16,1,2,128,128]{4,3,2,1,0:T(8,128)}), f32[16,1,2,128,128]{4,3,2,1,0:T(8,128)}, u32[]{:S(2)}, u32[]{:S(2)}) async-start(f32[16,1,2,128,128]{4,3,2,1,0:T(8,128)} %get-tuple-element.75), calls=%async_computation.3 | async-start | bytes 4194304 | tf_op jit(solution)/shard_map/all_to_all | solution.py:512
  320.9 96.0 %all-to-all-start.5 = ((f32[16,2,2,128,128]{4,3,2,1,0:T(8,128)}), f32[16,2,2,128,128]{4,3,2,1,0:T(8,128)}, u32[]{:S(2)}, u32[]{:S(2)}) async-start(f32[16,2,2,128,128]{4,3,2,1,0:T(8,128)} %get-tuple-element.82), calls=%async_computation.5 | async-start | bytes 8388608 | tf_op jit(solution)/shard_map/all_to_all | solution.py:512
  326.1 13.0 %copy-start = (f32[2]{0:T(128)S(1)}, f32[2]{0:T(128)}, u32[]{:S(2)}) copy-start(f32[2]{0:T(128)} %param.12) | copy-start | bytes 28
  337.6 48.2 %collective-permute-start = (f32[128,4096]{1,0:T(8,128)}, f32[128,4096]{1,0:T(8,128)}, u32[]{:S(2)}, u32[]{:S(2)}) collective-permute-start(f32[128,4096]{1,0:T(8,128)} %shard_map.117.own), channel_id=1, source_target_pairs={{0,16},{16,0},{1,17},{17,1},{2,18},{18,2},{3,19},{19,3},{4,20},{20... | collective-permute-start | bytes 6291464 | tf_op jit(solution)/shard_map/ppermute | solution.py:24
  416.9 97.9 %all-to-all-start.6 = ((f32[16,2,2,128,128]{4,3,2,1,0:T(8,128)}), f32[16,2,2,128,128]{4,3,2,1,0:T(8,128)}, u32[]{:S(2)}, u32[]{:S(2)}) async-start(f32[16,2,2,128,128]{4,3,2,1,0:T(8,128)} %get-tuple-element.87), calls=%async_computation.6 | async-start | bytes 8388608 | tf_op jit(solution)/shard_map/all_to_all | solution.py:512
  434.8 48.2 %collective-permute-start.1 = (f32[128,4096]{1,0:T(8,128)}, f32[128,4096]{1,0:T(8,128)}, u32[]{:S(2)}, u32[]{:S(2)}) collective-permute-start(f32[128,4096]{1,0:T(8,128)} %shard_map.119.own), channel_id=1, source_target_pairs={{0,16},{16,0},{1,17},{17,1},{2,18},{18,2},{3,19},{19,3},{4,20},{20... | collective-permute-start | bytes 6291464 | tf_op jit(solution)/shard_map/ppermute | solution.py:24
  567.8 46.2 %all-to-all-start.8 = ((f32[16,1,2,128,128]{4,3,2,1,0:T(8,128)}), f32[16,1,2,128,128]{4,3,2,1,0:T(8,128)}, u32[]{:S(2)}, u32[]{:S(2)}) async-start(f32[16,1,2,128,128]{4,3,2,1,0:T(8,128)} %get-tuple-element.96), calls=%async_computation.8 | async-start | bytes 4194304 | tf_op jit(solution)/shard_map/all_to_all | solution.py:512
  614.1 52.3 %all-to-all-start.9 = ((f32[16,1,2,128,128]{4,3,2,1,0:T(8,128)}), f32[16,1,2,128,128]{4,3,2,1,0:T(8,128)}, u32[]{:S(2)}, u32[]{:S(2)}) async-start(f32[16,1,2,128,128]{4,3,2,1,0:T(8,128)} %get-tuple-element.103), calls=%async_computation.9 | async-start | bytes 4194304 | tf_op jit(solution)/shard_map/all_to_all | solution.py:512
  724.8 85.0 %all-to-all-start.11 = ((f32[16,2,2,128,128]{4,3,2,1,0:T(8,128)}), f32[16,2,2,128,128]{4,3,2,1,0:T(8,128)}, u32[]{:S(2)}, u32[]{:S(2)}) async-start(f32[16,2,2,128,128]{4,3,2,1,0:T(8,128)} %get-tuple-element.111), calls=%async_computation.11 | async-start | bytes 8388608 | tf_op jit(solution)/shard_map/all_to_all | solution.py:512
  741.5 48.2 %collective-permute-start.2 = (f32[128,4096]{1,0:T(8,128)}, f32[128,4096]{1,0:T(8,128)}, u32[]{:S(2)}, u32[]{:S(2)}) collective-permute-start(f32[128,4096]{1,0:T(8,128)} %shard_map.123.own), channel_id=1, source_target_pairs={{0,16},{16,0},{1,17},{17,1},{2,18},{18,2},{3,19},{19,3},{4,20},{20... | collective-permute-start | bytes 6291464 | tf_op jit(solution)/shard_map/ppermute | solution.py:24
  821.4 47.3 %collective-permute-start.3 = (f32[128,4096]{1,0:T(8,128)}, f32[128,4096]{1,0:T(8,128)}, u32[]{:S(2)}, u32[]{:S(2)}) collective-permute-start(f32[128,4096]{1,0:T(8,128)} %shard_map.125.own), channel_id=1, source_target_pairs={{0,16},{16,0},{1,17},{17,1},{2,18},{18,2},{3,19},{19,3},{4,20},{20... | collective-permute-start | bytes 6291464 | tf_op jit(solution)/shard_map/ppermute | solution.py:24

commit v2 on v1

--- a/solution.py
+++ b/solution.py
@@ -150,6 +150,7 @@
 
 RADIX = 16
 CHUNKS = 2
+LAST_CUT = 80
 f32 = jnp.float32
 bf16 = jnp.bfloat16
 
@@ -300,11 +301,15 @@
     factor = 0.5 * jnp.exp(state)
     for iteration in range(NEWTON):
         scaled = factor * rate
-        misfit = strength * inverse_sinh(scaled) + joint * rate - locked
-        slope = strength * factor / jnp.sqrt(1.0 + scaled * scaled) + joint
+        wide = 1.0 + scaled * scaled
+        narrow = lax.rsqrt(wide)
+        bent = jnp.log(jnp.abs(scaled) + wide * narrow)
+        bent = jnp.where(scaled < 0.0, -bent, bent)
+        misfit = strength * bent + joint * rate - locked
+        slope = strength * factor * narrow + joint
         rate = rate - 0.5 * misfit / slope
     stress = locked - joint * rate
-    speed = sign * (prestress + own - stress) / eta
+    speed = (sign / eta) * (prestress + own - stress)
     state_new = state + 0.25 * (jnp.exp(-state) - jnp.abs(rate))
     return speed, rate, state_new
 
@@ -374,7 +379,7 @@
     lax.fori_loop(0, now.shape[2] // 256, group, 0)
 
 
-def spectral_kernel(has_past, half, *refs):
+def spectral_kernel(has_past, half, pieces, *refs):
     blocks = refs[:CHUNKS]
     kernel_now, past_sum, table, twist = refs[CHUNKS : CHUNKS + 4]
     rest = list(refs[CHUNKS + 4 :])
@@ -382,8 +387,8 @@
         kernel_past, spec_past = rest.pop(0), rest.pop(0)
         spec_out = None
     if half > 0:
-        rest.pop(0)
-    outs, rest = rest[:CHUNKS], rest[CHUNKS:]
+        rest = rest[len(pieces) - 1 :]
+    outs, rest = rest[: len(pieces)], rest[len(pieces) :]
     if not has_past:
         spec_out = rest.pop(0)
     held, turned, total = rest
@@ -450,14 +455,15 @@
     def wave_back(pair, carry):
         both = product(table, held, pair, 0)
         slabs = outs[0].shape[0]
-        per = inner // slabs // CHUNKS
+        per = inner // slabs
         for slab in range(slabs):
-            for chunk in range(CHUNKS):
+            for out, (row, count) in zip(outs, pieces):
+                count = count // RADIX
                 for part in range(2):
-                    first = (1 - part) * inner + (slab * CHUNKS + chunk) * per
+                    first = (1 - part) * inner + slab * per + row // RADIX
                     for odd in range(2):
-                        outs[chunk][slab, 0, part, pl.ds(2 * pair + odd, per, RADIX), :] = both[
-                            first : first + per, odd * 128 : odd * 128 + 128
+                        out[slab, 0, part, pl.ds(2 * pair + odd, count, RADIX), :] = both[
+                            first : first + count, odd * 128 : odd * 128 + 128
                         ]
         return carry
 
@@ -493,7 +499,7 @@
 
     def turn(b, carry):
         cols = pl.ds(pl.multiple_of(b * 256, 256), 256)
-        out[:, cols] = turned[cols, :].T * scale
+        out[:, cols] = turned[cols, :].T[:rows] * scale
         return carry
 
     lax.fori_loop(0, length // 256, turn, 0)
@@ -538,8 +544,8 @@
             jnp.where(is_first, 1.0, -1.0).astype(f32),
         ]
     )
-    def tiles(counts):
-        return [jax.ShapeDtypeStruct((slabs, count, 2, 128, 128), f32) for count in counts]
+    def tiles(counts, rows=128):
+        return [jax.ShapeDtypeStruct((slabs, count, 2, rows, 128), f32) for count in counts]
 
     def tile_specs(counts):
         return [pl.BlockSpec((slabs, count, 2, 128, 128), lambda *_: (0,) * 5) for count in counts]
@@ -588,20 +594,22 @@
         )(scalars, own, other, prestress, strength, state, table, twist)
         return sent, state_new
 
-    def end(chunk, own, other, state, before):
+    def end(row, own, other, state, before):
         full = jax.ShapeDtypeStruct((rows_dev, length), f32)
-        step = 32
-        parts = chunk_rows // step
-        base = chunk * parts
+        step = 16
+        parts = own.shape[0] // step
+        base = row // step
+        ahead = row % chunk_rows // step
         moving = pl.BlockSpec((step, length), lambda g: (base + g, 0))
         near = pl.BlockSpec((step, length), lambda g: (g, 0))
+        held_state = pl.BlockSpec((step, length), lambda g: (ahead + g, 0))
         moving_speed = pl.BlockSpec((1, step, length), lambda g: (0, base + g, 0))
         kept = [pl.BlockSpec(memory_space=pl.ANY)] * len(before)
         return pl.pallas_call(
             end_kernel,
             out_shape=(jax.ShapeDtypeStruct((1, rows_dev, length), f32), full, full),
             grid=(parts,),
-            in_specs=[SCALARS, near, near, moving, moving, near] + kept,
+            in_specs=[SCALARS, near, near, moving, moving, held_state] + kept,
             out_specs=(moving_speed, moving, moving),
             input_output_aliases={6 + n: n for n in range(len(before))},
             compiler_params=PARAMS,
@@ -623,10 +631,11 @@
             compiler_params=PARAMS,
         )(kernel, history)
 
-    def spectral(half, blocks, past_sum, past, before):
+    def spectral(half, blocks, past_sum, past, pieces, before):
         def block(array):
             place = half if array.shape[1] == halves else 0
-            return pl.BlockSpec((slabs, 1, 2, 128, 128), lambda *_: (0, place, 0, 0, 0))
+            shape = (slabs, 1, 2, array.shape[3], 128)
+            return pl.BlockSpec(shape, lambda *_: (0, place, 0, 0, 0))
 
         lag_spec = [
             pl.BlockSpec((1, 1, 128, length), functools.partial(lambda lag, *_: (0, lag, half, 0), lag))
@@ -637,7 +646,9 @@
         operands = list(blocks) + [kernel, past_sum, table, twist]
         in_specs = [block(b) for b in blocks]
         in_specs += [lag_spec[0], sum_spec, whole_spec(table), whole_spec(twist)]
-        out_shape = tiles([1, halves])
+        out_shape = tiles([1])
+        for row, count in pieces[1:]:
+            out_shape += tiles([halves], count)
         out_specs = [block(shape) for shape in out_shape]
         if past is not None:
             operands += [kernel, past]
@@ -647,11 +658,11 @@
             out_specs.append(spec_spec)
         aliases = {}
         if before is not None:
-            aliases = {len(operands): 1}
-            operands.append(before)
-            in_specs.append(pl.BlockSpec(memory_space=pl.ANY))
+            aliases = {len(operands) + n: 1 + n for n in range(len(before))}
+            operands += before
+            in_specs += [pl.BlockSpec(memory_space=pl.ANY)] * len(before)
         return pl.pallas_call(
-            functools.partial(spectral_kernel, past is not None, half),
+            functools.partial(spectral_kernel, past is not None, half, pieces),
             input_output_aliases=aliases,
             out_shape=out_shape,
             grid=(1,),
@@ -666,12 +677,13 @@
         )(*operands)
 
     def inverse(*blocks):
+        rows = blocks[0].shape[3]
         return pl.pallas_call(
             functools.partial(inverse_kernel, len(blocks)),
-            out_shape=rows_shape,
+            out_shape=jax.ShapeDtypeStruct((rows, length), f32),
             grid=(1,),
-            in_specs=tile_specs([b.shape[1] for b in blocks]) + [whole_spec(table), whole_spec(twist)],
-            out_specs=rows_spec,
+            in_specs=[whole_spec(b) for b in blocks] + [whole_spec(table), whole_spec(twist)],
+            out_specs=pl.BlockSpec((rows, length), lambda *_: (0, 0)),
             scratch_shapes=[held, pltpu.VMEM((length, 128), f32)],
             compiler_params=PARAMS,
         )(*blocks, table, twist)
@@ -679,9 +691,13 @@
     sent = [start(0), None]
     states = [fault_state] * CHUNKS
     past = [None] * halves
-    sums, results, waiting = None, (), None
+    sums, waiting = None, None
+    whole, cut = chunk_rows, LAST_CUT
     for step_index in range(STEPS):
         last = step_index == STEPS - 1
+        pieces = [(0, whole), (whole, cut), (whole + cut, whole - cut)]
+        if not last:
+            pieces = [(0, whole), (whole, whole)]
         first = exchanged(sent[0][0])
         if step_index == 0:
             sent[1] = start(1)
@@ -694,29 +710,35 @@
             sums = past_sums()
         near, far, sums = hold((near, sent[1][1], sums))
         far = exchanged(far)
-        outs = spectral(0, (first, near), sums[step_index], past[0], None)
+        outs = spectral(0, (first, near), sums[step_index], past[0], pieces, None)
         if step_index == 0:
-            past[0] = outs[2]
-        back, late = outs[0], outs[1]
+            past[0] = outs[-1]
+        back, late = outs[0], outs[1 : len(pieces)]
         far, back, late = hold((far, back, late))
         back = exchanged(back)
-        outs = spectral(1, (first, far), sums[step_index], past[1], late)
+        outs = spectral(1, (first, far), sums[step_index], past[1], pieces, late)
         if step_index == 0:
-            past[1] = outs[2]
-        back, more, late = hold((back, outs[0], outs[1]))
+            past[1] = outs[-1]
+        back, more, late = hold((back, outs[0], outs[1 : len(pieces)]))
         more = exchanged(more)
         more, late = hold((more, late))
-        waiting = exchanged(late)
+        waiting = exchanged(late[0])
         own = inverse(back, more)
         other = swapped(own, "side", 0)
-        if last:
-            results = end(0, own, other, states[0], results)
-            waiting, results = hold((waiting, tuple(results)))
-            own = inverse(waiting)
-            results = end(1, own, swapped(own, "side", 0), states[1], results)
-        else:
+        if not last:
             sent[0], states[0] = middle(0, own, other, states[0])
             waiting, sent[0], states[0] = hold((waiting, sent[0], states[0]))
+            continue
+        waiting, own, other, final = hold((waiting, own, other, late[1]))
+        final = exchanged(final)
+        own_near = inverse(waiting)
+        other_near = swapped(own_near, "side", 0)
+        results = end(0, own, other, states[0], ())
+        final, own_near, results = hold((final, own_near, tuple(results)))
+        own = inverse(final)
+        other = swapped(own, "side", 0)
+        results = end(whole, own_near, other_near, states[1], results)
+        results = end(whole + cut, own, other, states[1], results)
     return tuple(results)
 
 

time: 902 us -> 869 us (0.963)
  waiting for transfers between devices: 327 us -> 300 us
  Pallas kernels: 295 us -> 272 us
  starting transfers between devices: 89 us -> 105 us
    ppermute x4 -> x5, waiting for transfers between devices: 179 us -> 144 us  [swapped(): return lax.ppermute(value, axis, pairs)]
    pallas_call x2, Pallas kernels: 63 us -> 46.5 us  [middle(): pl.pallas_call(middle_kernel, out_shape=tiles(forward_cut[chunk]) + [rows...]
    all_to_all x9 -> x10, starting transfers between devices: 82.9 us -> 97 us  [exchanged(): lax.all_to_all(value, 'slab', split_axis=0, concat_axis=0, tiled=True)]
    pallas_call x2 -> x3, Pallas kernels: 40.2 us -> 27 us  [end(): pl.pallas_call(end_kernel, out_shape=(jax.ShapeDtypeStruct((1, rows_dev,...]
    all_to_all x9 -> x10, waiting for transfers between devices: 148 us -> 156 us  [exchanged(): lax.all_to_all(value, 'slab', split_axis=0, concat_axis=0, tiled=True)]
    pallas_call x4 -> x5, Pallas kernels: 45.9 us -> 52.6 us  [inverse(): pl.pallas_call(functools.partial(inverse_kernel, len(blocks)), out_shape=...]
  transfers between devices with their start and end apart: 13 -> 15, of which waited for: 10 -> 11; matrix products, arithmetic and copies ran while one was open for 0% -> 0% of each run, Pallas kernels for 28% -> 29%
where the time goes in v2:
time: 869 us; the launch traced here: 864 us
  waiting for transfers between devices  300 us (35%)
  Pallas kernels  272 us (31%)
  blocking collectives  178 us (20%)
  starting transfers between devices  105 us (12%)
    all_to_all x3, blocking collectives, exchanged(): lax.all_to_all(value, 'slab', split_axis=0, concat_axis=0, tiled=True)  178 us
    all_to_all x10, waiting for transfers between devices, exchanged(): lax.all_to_all(value, 'slab', split_axis=0, concat_axis=0, tiled=True)  156 us
    ppermute x5, waiting for transfers between devices, swapped(): return lax.ppermute(value, axis, pairs)  144 us
    pallas_call x4, Pallas kernels, spectral(): pl.pallas_call(functools.partial(spectral_kernel, past is not None, half,...  98.1 us
    all_to_all x10, starting transfers between devices, exchanged(): lax.all_to_all(value, 'slab', split_axis=0, concat_axis=0, tiled=True)  97 us
    pallas_call x5, Pallas kernels, inverse(): pl.pallas_call(functools.partial(inverse_kernel, len(blocks)), out_shape=...  52.6 us
    pallas_call x2, Pallas kernels, middle(): pl.pallas_call(middle_kernel, out_shape=tiles(forward_cut[chunk]) + [rows...  46.5 us
    pallas_call x3, Pallas kernels, end(): pl.pallas_call(end_kernel, out_shape=(jax.ShapeDtypeStruct((1, rows_dev,...  27 us
  transfers between devices with their start and end apart: 15, of which 11 were waited for; matrix products, arithmetic and copies ran while one was open for 0% of the time, Pallas kernels for 29%

profile of v2, /device:TPU:0, one launch (start us, length us, event | category | flops | bytes accessed | tf_op | source)
XLA Modules:
  0.0 864.3 jit_solution(14608745527974779165)
XLA Ops:
  0.6 11.5 %shard_map.112 = f32[16,2,2,128,128]{4,3,2,1,0:T(8,128)} custom-call(f32[1,256,4096]{2,1,0:T(8,128)} %velocity.3, bf16[512,1536]{1,0:T(8,128)(2,1)} %constant.16.clone.table.refs_4_.refs_2_.refs_1_, f32[2,16,256]{2,1,0:T(8,128)} %constant.17.clone.twist.refs_5_.refs_3_.refs_2_), custom_call_target="tpu_custom_call" | custom-call | tf_op jit(solution)/shard_map/pallas_call | solution.py:562
  19.6 11.5 %shard_map.113 = (f32[16,1,2,128,128]{4,3,2,1,0:T(8,128)}, f32[16,1,2,128,128]{4,3,2,1,0:T(8,128)}) custom-call(f32[1,256,4096]{2,1,0:T(8,128)} %velocity.3, bf16[512,1536]{1,0:T(8,128)(2,1)} %constant.16.clone.table.refs_4_.refs_2_.refs_1_, f32[2,16,256]{2,1,0:T(8,128)} %constant.17.clone.twist.refs_5_.refs_3_.refs_2_), custom_call_target="tpu_custom_call" | custom-call | tf_op jit(solution)/shard_map/pallas_call | solution.py:562
  31.1 66.1 %all-to-all-done.refs_0_ = f32[16,2,2,128,128]{4,3,2,1,0:T(8,128)} async-done(((f32[16,2,2,128,128]{4,3,2,1,0:T(8,128)}), f32[16,2,2,128,128]{4,3,2,1,0:T(8,128)}, u32[]{:S(2)}, u32[]{:S(2)}) %all-to-all-start) | async-done | bytes 4194336 | tf_op jit(solution)/shard_map/all_to_all | solution.py:518
  97.1 19.7 %all-to-all-start.1 = ((f32[16,1,2,128,128]{4,3,2,1,0:T(8,128)}), f32[16,1,2,128,128]{4,3,2,1,0:T(8,128)}, u32[]{:S(2)}, u32[]{:S(2)}) async-start(f32[16,1,2,128,128]{4,3,2,1,0:T(8,128)} %get-tuple-element.78), calls=%async_computation.1 | async-start | bytes 4194304 | tf_op jit(solution)/shard_map/all_to_all | solution.py:518
  116.8 24.8 %shard_map.114 = (f32[2,256,4096]{2,1,0:T(8,128)}, f32[2,256,4096]{2,1,0:T(8,128)}) custom-call(bf16[1,9,256,4096]{3,2,1,0:T(8,128)(2,1)} %refs_6_.3, bf16[1,8,2,256,4096]{4,3,2,1,0:T(8,128)(2,1)} %history.1), custom_call_target="tpu_custom_call" | custom-call | tf_op jit(solution)/shard_map/pallas_call | solution.py:622
  141.6 16.2 %all-to-all-done.1.refs_1_ = f32[16,1,2,128,128]{4,3,2,1,0:T(8,128)} async-done(((f32[16,1,2,128,128]{4,3,2,1,0:T(8,128)}), f32[16,1,2,128,128]{4,3,2,1,0:T(8,128)}, u32[]{:S(2)}, u32[]{:S(2)}) %all-to-all-start.1) | async-done | bytes 2097184 | tf_op jit(solution)/shard_map/all_to_all | solution.py:518
  169.1 24.5 %shard_map.115 = (f32[16,1,2,128,128]{4,3,2,1,0:T(8,128)}, f32[16,2,2,128,128]{4,3,2,1,0:T(8,128)}, bf16[2,128,4096]{2,1,0:T(8,128)(2,1)}) custom-call(f32[16,2,2,128,128]{4,3,2,1,0:T(8,128)} %all-to-all-done.refs_0_, f32[16,1,2,128,128]{4,3,2,1,0:T(8,128)} %all-to-all-done.1.refs_1_, bf16[1,9,256,4096]{3,2,1,0:T(8,128)(2,1)} %refs_6_.3, ...), custom_call_target="tpu_custom_call" | custom-call | tf_op jit(solution)/shard_map/pallas_call | solution.py:664
  193.6 16.6 %all-to-all-done.2.refs_1_ = f32[16,1,2,128,128]{4,3,2,1,0:T(8,128)} async-done(((f32[16,1,2,128,128]{4,3,2,1,0:T(8,128)}), f32[16,1,2,128,128]{4,3,2,1,0:T(8,128)}, u32[]{:S(2)}, u32[]{:S(2)}) %all-to-all-start.2) | async-done | bytes 2097184 | tf_op jit(solution)/shard_map/all_to_all | solution.py:518
  221.4 24.4 %shard_map.116 = (f32[16,1,2,128,128]{4,3,2,1,0:T(8,128)}, f32[16,2,2,128,128]{4,3,2,1,0:T(8,128)}, bf16[2,128,4096]{2,1,0:T(8,128)(2,1)}) custom-call(f32[16,2,2,128,128]{4,3,2,1,0:T(8,128)} %all-to-all-done.refs_0_, f32[16,1,2,128,128]{4,3,2,1,0:T(8,128)} %all-to-all-done.2.refs_1_, ...), custom_call_target="tpu_custom_call", output_to_operand_aliasing={{1}: (6, {})} | custom-call | tf_op jit(solution)/shard_map/pallas_call | solution.py:664
  245.9 16.6 %all-to-all-done.3.refs_0_ = f32[16,1,2,128,128]{4,3,2,1,0:T(8,128)} async-done(((f32[16,1,2,128,128]{4,3,2,1,0:T(8,128)}), f32[16,1,2,128,128]{4,3,2,1,0:T(8,128)}, u32[]{:S(2)}, u32[]{:S(2)}) %all-to-all-start.3) | async-done | bytes 2097184 | tf_op jit(solution)/shard_map/all_to_all | solution.py:518
  262.5 58.5 %all_to_all.65.refs_1_ = f32[16,1,2,128,128]{4,3,2,1,0:T(8,128)} all-to-all(f32[16,1,2,128,128]{4,3,2,1,0:T(8,128)} %get-tuple-element.93), channel_id=1, replica_groups=mesh['side'=2,'slab'=16] {'slab'}, dimensions={0} | all-to-all | bytes 4194304 | tf_op jit(solution)/shard_map/all_to_all | solution.py:518
  345.7 40.1 %collective-permute-done.other = f32[128,4096]{1,0:T(8,128)} collective-permute-done((f32[128,4096]{1,0:T(8,128)}, f32[128,4096]{1,0:T(8,128)}, u32[]{:S(2)}, u32[]{:S(2)}) %collective-permute-start) | collective-permute-done | bytes 2097184 | tf_op jit(solution)/shard_map/ppermute | solution.py:24
  385.8 22.8 %shard_map.118 = (f32[16,2,2,128,128]{4,3,2,1,0:T(8,128)}, f32[128,4096]{1,0:T(8,128)}) custom-call(f32[5]{0:T(128)} %stack.23.scalars, f32[128,4096]{1,0:T(8,128)} %shard_map.117.own, f32[128,4096]{1,0:T(8,128)} %collective-permute-done.other, f32[256,4096]{1,0:T(8,128)} %prestress.9, f32[256,4096]{1,0:T(8,128)} %strength.9, f32[256,4096]{1,0:T(8,128)} %state.2, ...), custom_call_target="tpu_custom_call" | custom-call | tf_op jit(solution)/shard_map/pallas_call | solution.py:577
  408.6 14.7 %all-to-all-start.6 = ((f32[16,2,2,128,128]{4,3,2,1,0:T(8,128)}), f32[16,2,2,128,128]{4,3,2,1,0:T(8,128)}, u32[]{:S(2)}, u32[]{:S(2)}) async-start(f32[16,2,2,128,128]{4,3,2,1,0:T(8,128)} %get-tuple-element.100), calls=%async_computation.6 | async-start | bytes 8388608 | tf_op jit(solution)/shard_map/all_to_all | solution.py:518
  436.3 46.7 %collective-permute-done.1.other = f32[128,4096]{1,0:T(8,128)} collective-permute-done((f32[128,4096]{1,0:T(8,128)}, f32[128,4096]{1,0:T(8,128)}, u32[]{:S(2)}, u32[]{:S(2)}) %collective-permute-start.1) | collective-permute-done | bytes 2097184 | tf_op jit(solution)/shard_map/ppermute | solution.py:24
  483.0 23.7 %shard_map.120 = (f32[16,1,2,128,128]{4,3,2,1,0:T(8,128)}, f32[16,1,2,128,128]{4,3,2,1,0:T(8,128)}, f32[128,4096]{1,0:T(8,128)}) custom-call(f32[5]{0:T(128)} %stack.23.scalars, f32[128,4096]{1,0:T(8,128)} %shard_map.119.own, f32[128,4096]{1,0:T(8,128)} %collective-permute-done.1.other, f32[256,4096]{1,0:T(8,128)} %prestress.9, f32[256,4096]{1,0:T(8,128)} %strength.9, ...), custom_call_target="tpu_custom_call" | custom-call | tf_op jit(solution)/shard_map/pallas_call | solution.py:577
  506.7 61.1 %all_to_all.66.refs_1_ = f32[16,1,2,128,128]{4,3,2,1,0:T(8,128)} all-to-all(f32[16,1,2,128,128]{4,3,2,1,0:T(8,128)} %get-tuple-element.106), channel_id=1, replica_groups=mesh['side'=2,'slab'=16] {'slab'}, dimensions={0} | all-to-all | bytes 4194304 | tf_op jit(solution)/shard_map/all_to_all | solution.py:518
  573.0 24.6 %shard_map.121 = (f32[16,1,2,128,128]{4,3,2,1,0:T(8,128)}, f32[16,2,2,80,128]{4,3,2,1,0:T(8,128)}, f32[16,2,2,48,128]{4,3,2,1,0:T(8,128)}) custom-call(f32[16,2,2,128,128]{4,3,2,1,0:T(8,128)} %all-to-all-done.6.refs_0_, f32[16,1,2,128,128]{4,3,2,1,0:T(8,128)} %all_to_all.66.refs_1_, bf16[1,9,256,4096]{3,2,1,0:T(8,128)(2,1)} %refs_6_.3, ...), custom_call_target="tpu_custom_call" | custom-call | tf_op jit(solution)/shard_map/pallas_call | solution.py:664
  597.6 16.5 %all-to-all-done.8.refs_1_ = f32[16,1,2,128,128]{4,3,2,1,0:T(8,128)} async-done(((f32[16,1,2,128,128]{4,3,2,1,0:T(8,128)}), f32[16,1,2,128,128]{4,3,2,1,0:T(8,128)}, u32[]{:S(2)}, u32[]{:S(2)}) %all-to-all-start.8) | async-done | bytes 2097184 | tf_op jit(solution)/shard_map/all_to_all | solution.py:518
  625.3 24.6 %shard_map.122 = (f32[16,1,2,128,128]{4,3,2,1,0:T(8,128)}, f32[16,2,2,80,128]{4,3,2,1,0:T(8,128)}, f32[16,2,2,48,128]{4,3,2,1,0:T(8,128)}) custom-call(f32[16,2,2,128,128]{4,3,2,1,0:T(8,128)} %all-to-all-done.6.refs_0_, f32[16,1,2,128,128]{4,3,2,1,0:T(8,128)} %all-to-all-done.8.refs_1_, ...), custom_call_target="tpu_custom_call", output_to_operand_aliasing={{1}: (8, {}), {2}: (9, {})} | custom-call | tf_op jit(solution)/shard_map/pallas_call | solution.py:664
  649.9 16.4 %all-to-all-done.9.refs_0_ = f32[16,1,2,128,128]{4,3,2,1,0:T(8,128)} async-done(((f32[16,1,2,128,128]{4,3,2,1,0:T(8,128)}), f32[16,1,2,128,128]{4,3,2,1,0:T(8,128)}, u32[]{:S(2)}, u32[]{:S(2)}) %all-to-all-start.9) | async-done | bytes 2097184 | tf_op jit(solution)/shard_map/all_to_all | solution.py:518
  666.3 58.5 %all_to_all.67.refs_1_ = f32[16,1,2,128,128]{4,3,2,1,0:T(8,128)} all-to-all(f32[16,1,2,128,128]{4,3,2,1,0:T(8,128)} %get-tuple-element.125), channel_id=1, replica_groups=mesh['side'=2,'slab'=16] {'slab'}, dimensions={0} | all-to-all | bytes 4194304 | tf_op jit(solution)/shard_map/all_to_all | solution.py:518
  743.0 46.7 %collective-permute-done.2.other = f32[128,4096]{1,0:T(8,128)} collective-permute-done((f32[128,4096]{1,0:T(8,128)}, f32[128,4096]{1,0:T(8,128)}, u32[]{:S(2)}, u32[]{:S(2)}) %collective-permute-start.2) | collective-permute-done | bytes 2097184 | tf_op jit(solution)/shard_map/ppermute | solution.py:24
  806.7 12.5 %shard_map.125 = (f32[1,256,4096]{2,1,0:T(8,128)}, f32[256,4096]{1,0:T(8,128)}, f32[256,4096]{1,0:T(8,128)}) custom-call(f32[5]{0:T(128)} %stack.23.scalars, f32[128,4096]{1,0:T(8,128)} %shard_map.123.own, f32[128,4096]{1,0:T(8,128)} %collective-permute-done.2.other, f32[256,4096]{1,0:T(8,128)} %prestress.9, f32[256,4096]{1,0:T(8,128)} %strength.9, ...), custom_call_target="tpu_custom_call" | custom-call | tf_op jit(solution)/shard_map/pallas_call | solution.py:608
  (34 shorter events, 159.0 us)
Async XLA Ops:
  12.1 85.0 %all-to-all-start = ((f32[16,2,2,128,128]{4,3,2,1,0:T(8,128)}), f32[16,2,2,128,128]{4,3,2,1,0:T(8,128)}, u32[]{:S(2)}, u32[]{:S(2)}) async-start(f32[16,2,2,128,128]{4,3,2,1,0:T(8,128)} %shard_map.112), calls=%async_computation | async-start | bytes 8388608 | tf_op jit(solution)/shard_map/all_to_all | solution.py:518
  97.1 60.7 %all-to-all-start.1 = ((f32[16,1,2,128,128]{4,3,2,1,0:T(8,128)}), f32[16,1,2,128,128]{4,3,2,1,0:T(8,128)}, u32[]{:S(2)}, u32[]{:S(2)}) async-start(f32[16,1,2,128,128]{4,3,2,1,0:T(8,128)} %get-tuple-element.78), calls=%async_computation.1 | async-start | bytes 4194304 | tf_op jit(solution)/shard_map/all_to_all | solution.py:518
  157.8 52.3 %all-to-all-start.2 = ((f32[16,1,2,128,128]{4,3,2,1,0:T(8,128)}), f32[16,1,2,128,128]{4,3,2,1,0:T(8,128)}, u32[]{:S(2)}, u32[]{:S(2)}) async-start(f32[16,1,2,128,128]{4,3,2,1,0:T(8,128)} %get-tuple-element.82), calls=%async_computation.2 | async-start | bytes 4194304 | tf_op jit(solution)/shard_map/all_to_all | solution.py:518
  210.1 52.3 %all-to-all-start.3 = ((f32[16,1,2,128,128]{4,3,2,1,0:T(8,128)}), f32[16,1,2,128,128]{4,3,2,1,0:T(8,128)}, u32[]{:S(2)}, u32[]{:S(2)}) async-start(f32[16,1,2,128,128]{4,3,2,1,0:T(8,128)} %get-tuple-element.88), calls=%async_computation.3 | async-start | bytes 4194304 | tf_op jit(solution)/shard_map/all_to_all | solution.py:518
  320.9 87.7 %all-to-all-start.5 = ((f32[16,2,2,128,128]{4,3,2,1,0:T(8,128)}), f32[16,2,2,128,128]{4,3,2,1,0:T(8,128)}, u32[]{:S(2)}, u32[]{:S(2)}) async-start(f32[16,2,2,128,128]{4,3,2,1,0:T(8,128)} %get-tuple-element.95), calls=%async_computation.5 | async-start | bytes 8388608 | tf_op jit(solution)/shard_map/all_to_all | solution.py:518
  326.1 13.0 %copy-start.2 = (f32[2]{0:T(128)S(1)}, f32[2]{0:T(128)}, u32[]{:S(2)}) copy-start(f32[2]{0:T(128)} %param.12) | copy-start | bytes 28
  337.6 48.2 %collective-permute-start = (f32[128,4096]{1,0:T(8,128)}, f32[128,4096]{1,0:T(8,128)}, u32[]{:S(2)}, u32[]{:S(2)}) collective-permute-start(f32[128,4096]{1,0:T(8,128)} %shard_map.117.own), channel_id=1, source_target_pairs={{0,16},{16,0},{1,17},{17,1},{2,18},{18,2},{3,19},{19,3},{4,20},{20... | collective-permute-start | bytes 6291464 | tf_op jit(solution)/shard_map/ppermute | solution.py:24
  408.6 98.1 %all-to-all-start.6 = ((f32[16,2,2,128,128]{4,3,2,1,0:T(8,128)}), f32[16,2,2,128,128]{4,3,2,1,0:T(8,128)}, u32[]{:S(2)}, u32[]{:S(2)}) async-start(f32[16,2,2,128,128]{4,3,2,1,0:T(8,128)} %get-tuple-element.100), calls=%async_computation.6 | async-start | bytes 8388608 | tf_op jit(solution)/shard_map/all_to_all | solution.py:518
  434.8 48.2 %collective-permute-start.1 = (f32[128,4096]{1,0:T(8,128)}, f32[128,4096]{1,0:T(8,128)}, u32[]{:S(2)}, u32[]{:S(2)}) collective-permute-start(f32[128,4096]{1,0:T(8,128)} %shard_map.119.own), channel_id=1, source_target_pairs={{0,16},{16,0},{1,17},{17,1},{2,18},{18,2},{3,19},{19,3},{4,20},{20... | collective-permute-start | bytes 6291464 | tf_op jit(solution)/shard_map/ppermute | solution.py:24
  567.8 46.2 %all-to-all-start.8 = ((f32[16,1,2,128,128]{4,3,2,1,0:T(8,128)}), f32[16,1,2,128,128]{4,3,2,1,0:T(8,128)}, u32[]{:S(2)}, u32[]{:S(2)}) async-start(f32[16,1,2,128,128]{4,3,2,1,0:T(8,128)} %get-tuple-element.109), calls=%async_computation.8 | async-start | bytes 4194304 | tf_op jit(solution)/shard_map/all_to_all | solution.py:518
  614.0 52.3 %all-to-all-start.9 = ((f32[16,1,2,128,128]{4,3,2,1,0:T(8,128)}), f32[16,1,2,128,128]{4,3,2,1,0:T(8,128)}, u32[]{:S(2)}, u32[]{:S(2)}) async-start(f32[16,1,2,128,128]{4,3,2,1,0:T(8,128)} %get-tuple-element.117), calls=%async_computation.9 | async-start | bytes 4194304 | tf_op jit(solution)/shard_map/all_to_all | solution.py:518
  724.8 64.9 %all-to-all-start.11 = ((f32[16,2,2,80,128]{4,3,2,1,0:T(8,128)}), f32[16,2,2,80,128]{4,3,2,1,0:T(8,128)}, u32[]{:S(2)}, u32[]{:S(2)}) async-start(f32[16,2,2,80,128]{4,3,2,1,0:T(8,128)} %get-tuple-element.128), calls=%async_computation.11 | async-start | bytes 5242880 | tf_op jit(solution)/shard_map/all_to_all | solution.py:518
  741.5 48.2 %collective-permute-start.2 = (f32[128,4096]{1,0:T(8,128)}, f32[128,4096]{1,0:T(8,128)}, u32[]{:S(2)}, u32[]{:S(2)}) collective-permute-start(f32[128,4096]{1,0:T(8,128)} %shard_map.123.own), channel_id=1, source_target_pairs={{0,16},{16,0},{1,17},{17,1},{2,18},{18,2},{3,19},{19,3},{4,20},{20... | collective-permute-start | bytes 6291464 | tf_op jit(solution)/shard_map/ppermute | solution.py:24
  789.7 37.6 %all-to-all-start.12 = ((f32[16,2,2,48,128]{4,3,2,1,0:T(8,128)}), f32[16,2,2,48,128]{4,3,2,1,0:T(8,128)S(1)}, u32[]{:S(2)}, u32[]{:S(2)}) async-start(f32[16,2,2,48,128]{4,3,2,1,0:T(8,128)} %get-tuple-element.132), calls=%async_computation.12 | async-start | bytes 3145728 | tf_op jit(solution)/shard_map/all_to_all | solution.py:518
  805.2 33.3 %collective-permute-start.4 = (f32[80,4096]{1,0:T(8,128)}, f32[80,4096]{1,0:T(8,128)}, u32[]{:S(2)}, u32[]{:S(2)}) collective-permute-start(f32[80,4096]{1,0:T(8,128)} %shard_map.124.own), channel_id=1, source_target_pairs={{0,16},{16,0},{1,17},{17,1},{2,18},{18,2},{3,19},{19,3},{4,20},{20... | collective-permute-start | bytes 3932168 | tf_op jit(solution)/shard_map/ppermute | solution.py:24
  827.3 1.2 copy-start
  836.9 20.6 %collective-permute-start.3 = (f32[48,4096]{1,0:T(8,128)}, f32[48,4096]{1,0:T(8,128)S(1)}, u32[]{:S(2)}, u32[]{:S(2)}) collective-permute-start(f32[48,4096]{1,0:T(8,128)} %shard_map.126.own), channel_id=1, source_target_pairs={{0,16},{16,0},{1,17},{17,1},{2,18},{18,2},{3,19},{19,3},{4,20},{20... | collective-permute-start | bytes 2359304 | tf_op jit(solution)/shard_map/ppermute | solution.py:24
  857.6 0.9 copy-start.1

commit v3 on v2

--- a/solution.py
+++ b/solution.py
@@ -8,6 +8,7 @@
 from jax.experimental import pallas as pl
 from jax.experimental.pallas import tpu as pltpu
 from jax.sharding import PartitionSpec as P
+
 
 NX = 4096
 NZ = 4096
@@ -99,7 +100,7 @@
     turned = jnp.swapaxes(
         lax.all_to_all(moved, "slab", split_axis=3, concat_axis=2, tiled=True)[:, :, :, 0, :], 2, 3
     )
-    field_real, unused = transform_last(turned[:, 0], turned[:, 1], 1.0, True)
+    field_real, _ = transform_last(turned[:, 0], turned[:, 1], 1.0, True)
     return field_real * scale
 
 
@@ -120,7 +121,7 @@
     speed = velocity[0]
     state_now = fault_state
     rate = jnp.zeros_like(prestress)
-    for step_index in range(STEPS):
+    for _ in range(STEPS):
         spec_now = to_spectrum(speed)
         total = kernel_now * spec_now.astype(jnp.float32) + jnp.einsum(
             "lzx,lczx->czx", lag_kernel[1:], lag_history, preferred_element_type=jnp.float32
@@ -133,7 +134,7 @@
         locked = prestress + coupled
         friction_rate = locked / (eta_joint + strength)
         factor = 0.5 * jnp.exp(state_now)
-        for iteration in range(NEWTON):
+        for _ in range(NEWTON):
             scaled = factor * friction_rate
             misfit = strength * inverse_sinh(scaled) + eta_joint * friction_rate - locked
             slope = strength * factor / jnp.sqrt(1.0 + scaled * scaled) + eta_joint
@@ -258,7 +259,22 @@
     return (refs[0], half) if len(refs) == 1 else (refs[half], 0)
 
 
-def forward_rows(rows_ref, table, twist, outs, held):
+def store_ring(place, spread, both, outs, pair, lead, first_part, row):
+    inner = both.shape[0] // 2
+    per = inner // RADIX
+    spread[...] = both
+    for n in range(RADIX):
+        target = lax.rem(place[0] + n, RADIX)
+        for part in range(2):
+            base = (part if first_part == 0 else 1 - part) * inner
+            rows = pl.ds(pl.multiple_of(base + target * per + row, 8), 8)
+            for odd in range(2):
+                outs[n][lead, part, pl.ds(2 * pair + odd, 8, RADIX), :] = spread[
+                    rows, odd * 128 : odd * 128 + 128
+                ]
+
+
+def forward_rows(rows_ref, table, twist, place, outs, held, spread):
     rows, length = rows_ref.shape
     inner = length // RADIX
 
@@ -274,15 +290,19 @@
 
     def wave(pair, carry):
         both = product(table, held, pair, 0)
+        if len(outs) == RADIX:
+            for half in range(2):
+                store_ring(place, spread, both, outs, pair, half, 0, half * 8)
+            return carry
         slabs, halves = outs[0].shape[0], 2
         per = inner // slabs // halves
         for slab in range(slabs):
             for half in range(halves):
-                out, place = picked(outs, half)
+                out, spot = picked(outs, half)
                 for part in range(2):
                     first = part * inner + (slab * halves + half) * per
                     for odd in range(2):
-                        out[slab, place, part, pl.ds(2 * pair + odd, per, RADIX), :] = both[
+                        out[slab, spot, part, pl.ds(2 * pair + odd, per, RADIX), :] = both[
                             first : first + per, odd * 128 : odd * 128 + 128
                         ]
         return carry
@@ -290,8 +310,8 @@
     lax.fori_loop(0, RADIX // 2, wave, 0)
 
 
-def start_kernel(velocity, table, twist, *refs):
-    forward_rows(velocity.at[0], table, twist, refs[:-1], refs[-1])
+def start_kernel(place, velocity, table, twist, *refs):
+    forward_rows(velocity.at[0], table, twist, place, refs[:-2], *refs[-2:])
 
 
 def friction(scalars, own, other, prestress, strength, state):
@@ -299,7 +319,7 @@
     locked = prestress + (weight_own * own + weight_other * other)
     rate = locked / (joint + strength)
     factor = 0.5 * jnp.exp(state)
-    for iteration in range(NEWTON):
+    for _ in range(NEWTON):
         scaled = factor * rate
         wide = 1.0 + scaled * scaled
         narrow = lax.rsqrt(wide)
@@ -314,15 +334,15 @@
     return speed, rate, state_new
 
 
-def middle_kernel(scalars, own, other, prestress, strength, state, table, twist, *refs):
-    outs = refs[:-3]
-    state_out, held, speed_held = refs[-3:]
+def middle_kernel(place, scalars, own, other, prestress, strength, state, table, twist, *refs):
+    outs = refs[:-4]
+    state_out, held, spread, speed_held = refs[-4:]
 
     def group(g, carry):
         at = pl.ds(pl.multiple_of(g * 8, 8), 8)
         for lane in range(0, own.shape[1], 1024):
             cols = pl.ds(lane, 1024)
-            speed, rate, state_new = friction(
+            speed, _, state_new = friction(
                 scalars,
                 own[at, cols],
                 other[at, cols],
@@ -335,7 +355,7 @@
         return carry
 
     lax.fori_loop(0, own.shape[0] // 8, group, 0)
-    forward_rows(speed_held, table, twist, outs, held)
+    forward_rows(speed_held, table, twist, place, outs, held, spread)
 
 
 def end_kernel(scalars, own, other, prestress, strength, state, *refs):
@@ -380,32 +400,34 @@
 
 
 def spectral_kernel(has_past, half, pieces, *refs):
-    blocks = refs[:CHUNKS]
-    kernel_now, past_sum, table, twist = refs[CHUNKS : CHUNKS + 4]
-    rest = list(refs[CHUNKS + 4 :])
+    place, ring, block = refs[0], refs[1 : RADIX + 1], refs[RADIX + 1]
+    kernel_now, past_sum, table, twist, twist_ring = refs[RADIX + 2 : RADIX + 7]
+    rest = list(refs[RADIX + 7 :])
     if has_past:
         kernel_past, spec_past = rest.pop(0), rest.pop(0)
         spec_out = None
     if half > 0:
         rest = rest[len(pieces) - 1 :]
+    ring_out = []
+    if half == 0:
+        ring_out, rest = rest[:RADIX], rest[RADIX:]
+        pieces = pieces[1:]
     outs, rest = rest[: len(pieces)], rest[len(pieces) :]
     if not has_past:
         spec_out = rest.pop(0)
-    held, turned, total = rest
-    rows = blocks[0].shape[3]
+    held, turned, total, spread = rest
+    rows = block.shape[3]
     inner = RADIX * 16
     length = total.shape[2]
 
     def group(g, carry):
         at = pl.ds(pl.multiple_of(g * 16, 16), 16)
-        for chunk in range(CHUNKS):
-            values = [
-                (blocks[chunk][n, 0, 0, at, :], blocks[chunk][n, 0, 1, at, :])
-                for n in range(RADIX)
-            ]
-            lane = chunk * 128
-            for k, value in enumerate(sixteen(values, -1)):
-                store_split(held, k, g, lane, *twisted(value, twist, k, lane, -1))
+        values = [(ring[n][0, 0, at, :], ring[n][0, 1, at, :]) for n in range(RADIX)]
+        for k, value in enumerate(sixteen(values, 1)):
+            store_split(held, k, g, 0, *twisted(value, twist_ring, k, 0, -1))
+        values = [(block[n, 0, 0, at, :], block[n, 0, 1, at, :]) for n in range(RADIX)]
+        for k, value in enumerate(sixteen(values, -1)):
+            store_split(held, k, g, 128, *twisted(value, twist, k, 128, -1))
         return carry
 
     lax.fori_loop(0, rows // 16, group, 0)
@@ -454,6 +476,8 @@
 
     def wave_back(pair, carry):
         both = product(table, held, pair, 0)
+        if half == 0:
+            store_ring(place, spread, both, ring_out, pair, 0, 1, 0)
         slabs = outs[0].shape[0]
         per = inner // slabs
         for slab in range(slabs):
@@ -472,17 +496,24 @@
 
 def inverse_kernel(count, *refs):
     blocks = refs[:count]
-    table, twist, out, held, turned = refs[count:]
+    ring = blocks[:RADIX] if count > RADIX else None
+    table, twist, twist_ring, out, held, turned = refs[count:]
     rows, length = out.shape
     inner = length // RADIX
 
     def group(g, carry):
         at = pl.ds(pl.multiple_of(g * 16, 16), 16)
         for half in range(inner // 128):
-            block, place = picked(blocks, half)
-            values = [(block[n, place, 0, at, :], block[n, place, 1, at, :]) for n in range(RADIX)]
-            for k, value in enumerate(sixteen(values, 1)):
-                real, imag = twisted(value, twist, k, half * 128, 1)
+            sign, turn = 1, twist
+            if ring is not None and half == 0:
+                values = [(ring[n][0, 0, at, :], ring[n][0, 1, at, :]) for n in range(RADIX)]
+                sign, turn = -1, twist_ring
+            else:
+                block = blocks[-1]
+                spot = 0 if ring is not None else half
+                values = [(block[n, spot, 0, at, :], block[n, spot, 1, at, :]) for n in range(RADIX)]
+            for k, value in enumerate(sixteen(values, sign)):
+                real, imag = twisted(value, turn, k, half * 128, 1)
                 store_split(held, k, g, half * 128, imag, real)
         return carry
 
@@ -510,8 +541,16 @@
     return pl.BlockSpec(array.shape, lambda *_: zeros)
 
 
-PARAMS = pltpu.CompilerParams(vmem_limit_bytes=62 * 1024 * 1024)
+PARAMS = pltpu.CompilerParams(vmem_limit_bytes=67043328)
 SCALARS = pl.BlockSpec(memory_space=pltpu.SMEM)
+
+
+def ringed(blocks):
+    count = lax.axis_size("slab")
+    return [blocks[0]] + [
+        lax.ppermute(blocks[n], "slab", [(source, (source + n) % count) for source in range(count)])
+        for n in range(1, count)
+    ]
 
 
 def exchanged(value):
@@ -544,13 +583,20 @@
             jnp.where(is_first, 1.0, -1.0).astype(f32),
         ]
     )
+
     def tiles(counts, rows=128):
         return [jax.ShapeDtypeStruct((slabs, count, 2, rows, 128), f32) for count in counts]
 
-    def tile_specs(counts):
-        return [pl.BlockSpec((slabs, count, 2, 128, 128), lambda *_: (0,) * 5) for count in counts]
-
-    forward_cut = [[2], [1, 1]]
+    def ring_tiles(count):
+        return [jax.ShapeDtypeStruct((count, 2, 128, 128), f32)] * slabs
+
+    def forward_shapes(chunk):
+        shapes = ring_tiles(halves) if chunk == 0 else tiles([1, 1])
+        return shapes, [whole_spec(shape) for shape in shapes]
+
+    me = lax.axis_index("slab")
+    place = jnp.reshape(me, (1,)).astype(jnp.int32)
+    spread = pltpu.VMEM((2 * inner, 2 * 128), f32)
     held = pltpu.VMEM((RADIX // 2, 256, 4 * inner), bf16)
     rows_shape = jax.ShapeDtypeStruct((chunk_rows, length), f32)
     rows_spec = pl.BlockSpec((chunk_rows, length), lambda *_: (0, 0))
@@ -559,26 +605,30 @@
         return pl.BlockSpec((chunk_rows, length), lambda *_: (chunk, 0))
 
     def start(chunk):
+        shapes, specs = forward_shapes(chunk)
         return pl.pallas_call(
             start_kernel,
-            out_shape=tiles(forward_cut[chunk]),
+            out_shape=shapes,
             grid=(1,),
             in_specs=[
+                SCALARS,
                 pl.BlockSpec((1, chunk_rows, length), lambda *_: (0, chunk, 0)),
                 whole_spec(table),
                 whole_spec(twist),
             ],
-            out_specs=tile_specs(forward_cut[chunk]),
-            scratch_shapes=[held],
+            out_specs=specs,
+            scratch_shapes=[held, spread],
             compiler_params=PARAMS,
-        )(velocity, table, twist)
+        )(place, velocity, table, twist)
 
     def middle(chunk, own, other, state):
+        shapes, specs = forward_shapes(chunk)
         *sent, state_new = pl.pallas_call(
             middle_kernel,
-            out_shape=tiles(forward_cut[chunk]) + [rows_shape],
+            out_shape=shapes + [rows_shape],
             grid=(1,),
             in_specs=[
+                SCALARS,
                 SCALARS,
                 rows_spec,
                 rows_spec,
@@ -588,10 +638,10 @@
                 whole_spec(table),
                 whole_spec(twist),
             ],
-            out_specs=tile_specs(forward_cut[chunk]) + [rows_spec],
-            scratch_shapes=[held, pltpu.VMEM((chunk_rows, length), f32)],
+            out_specs=specs + [rows_spec],
+            scratch_shapes=[held, spread, pltpu.VMEM((chunk_rows, length), f32)],
             compiler_params=PARAMS,
-        )(scalars, own, other, prestress, strength, state, table, twist)
+        )(place, scalars, own, other, prestress, strength, state, table, twist)
         return sent, state_new
 
     def end(row, own, other, state, before):
@@ -631,7 +681,7 @@
             compiler_params=PARAMS,
         )(kernel, history)
 
-    def spectral(half, blocks, past_sum, past, pieces, before):
+    def spectral(half, ring, near, past_sum, past, pieces, before):
         def block(array):
             place = half if array.shape[1] == halves else 0
             shape = (slabs, 1, 2, array.shape[3], 128)
@@ -643,13 +693,18 @@
         ]
         sum_spec = pl.BlockSpec((2, 128, length), lambda *_: (0, half, 0))
         spec_spec = pl.BlockSpec((2, 128, length), lambda *_: (0, 0, 0))
-        operands = list(blocks) + [kernel, past_sum, table, twist]
-        in_specs = [block(b) for b in blocks]
-        in_specs += [lag_spec[0], sum_spec, whole_spec(table), whole_spec(twist)]
-        out_shape = tiles([1])
+        ring_spec = pl.BlockSpec((1, 2, 128, 128), lambda *_: (half, 0, 0, 0))
+        operands = [place, *ring, near, kernel, past_sum, table, twist, twist_ring]
+        in_specs = [SCALARS] + [ring_spec] * slabs + [block(near), lag_spec[0], sum_spec]
+        in_specs += [whole_spec(table), whole_spec(twist), whole_spec(twist_ring)]
+        out_shape = tiles([1]) if half else []
         for row, count in pieces[1:]:
             out_shape += tiles([halves], count)
         out_specs = [block(shape) for shape in out_shape]
+        if half == 0:
+            shapes = ring_tiles(1)
+            out_shape = shapes + out_shape
+            out_specs = [whole_spec(shape) for shape in shapes] + out_specs
         if past is not None:
             operands += [kernel, past]
             in_specs += [lag_spec[1], spec_spec]
@@ -672,62 +727,69 @@
                 held,
                 pltpu.VMEM((2, length, 128), f32),
                 pltpu.VMEM((2, 128, length), f32),
+                spread,
             ],
             compiler_params=PARAMS,
         )(*operands)
 
     def inverse(*blocks):
-        rows = blocks[0].shape[3]
+        rows = blocks[-1].shape[3]
         return pl.pallas_call(
             functools.partial(inverse_kernel, len(blocks)),
             out_shape=jax.ShapeDtypeStruct((rows, length), f32),
             grid=(1,),
-            in_specs=[whole_spec(b) for b in blocks] + [whole_spec(table), whole_spec(twist)],
+            in_specs=[whole_spec(b) for b in (*blocks, table, twist, twist_ring)],
             out_specs=pl.BlockSpec((rows, length), lambda *_: (0, 0)),
             scratch_shapes=[held, pltpu.VMEM((length, 128), f32)],
             compiler_params=PARAMS,
-        )(*blocks, table, twist)
+        )(*blocks, table, twist, twist_ring)
+
     hold = lax.optimization_barrier
-    sent = [start(0), None]
     states = [fault_state] * CHUNKS
     past = [None] * halves
     sums, waiting = None, None
     whole, cut = chunk_rows, LAST_CUT
+    sent = [start(0), None]
     for step_index in range(STEPS):
         last = step_index == STEPS - 1
         pieces = [(0, whole), (whole, cut), (whole + cut, whole - cut)]
         if not last:
             pieces = [(0, whole), (whole, whole)]
-        first = exchanged(sent[0][0])
+        ring = ringed(sent[0])
         if step_index == 0:
             sent[1] = start(1)
+            sent[1], shift = hold((tuple(sent[1]), me))
+            turn = lax.broadcasted_iota(jnp.int32, (RADIX, inner), 0) * (
+                lax.broadcasted_iota(jnp.int32, (RADIX, inner), 1) + inner * shift
+            )
+            turn = (turn % length).astype(f32) * (2.0 * math.pi / length)
+            twist_ring = jnp.stack([jnp.cos(turn), jnp.sin(turn)])
         else:
             own = inverse(waiting)
             sent[1], states[1] = middle(1, own, swapped(own, "side", 0), states[1])
-        first, sent[1], states[1] = hold((first, sent[1], states[1]))
         near = exchanged(sent[1][0])
         if step_index == 0:
             sums = past_sums()
         near, far, sums = hold((near, sent[1][1], sums))
         far = exchanged(far)
-        outs = spectral(0, (first, near), sums[step_index], past[0], pieces, None)
+        outs = spectral(0, ring, near, sums[step_index], past[0], pieces, None)
         if step_index == 0:
             past[0] = outs[-1]
-        back, late = outs[0], outs[1 : len(pieces)]
-        far, back, late = hold((far, back, late))
-        back = exchanged(back)
-        outs = spectral(1, (first, far), sums[step_index], past[1], pieces, late)
+        late = outs[slabs : slabs + len(pieces) - 1]
+        back = ringed(outs[:slabs])
+        far, late = hold((far, list(late)))
+        outs = spectral(1, ring, far, sums[step_index], past[1], pieces, late)
         if step_index == 0:
             past[1] = outs[-1]
-        back, more, late = hold((back, outs[0], outs[1 : len(pieces)]))
+        more, late = outs[0], outs[1 : len(pieces)]
         more = exchanged(more)
-        more, late = hold((more, late))
+        more, late = hold((more, list(late)))
         waiting = exchanged(late[0])
-        own = inverse(back, more)
+        own = inverse(*back, more)
         other = swapped(own, "side", 0)
         if not last:
             sent[0], states[0] = middle(0, own, other, states[0])
-            waiting, sent[0], states[0] = hold((waiting, sent[0], states[0]))
+        if not last:
             continue
         waiting, own, other, final = hold((waiting, own, other, late[1]))
         final = exchanged(final)

time: 869 us -> 1190 us (1.37)
  starting transfers between devices: 105 us -> 253 us
  waiting for transfers between devices: 300 us -> 390 us
  blocking collectives: 178 us -> 256 us
    ppermute x0 -> x60, waiting for transfers between devices: none -> 221 us  [ringed(): lax.ppermute(blocks[n], 'slab', [(source, (source + n) % count) for sourc...]
    ppermute x0 -> x60, starting transfers between devices: none -> 212 us  [ringed(): lax.ppermute(blocks[n], 'slab', [(source, (source + n) % count) for sourc...]
    all_to_all x10 -> x5, waiting for transfers between devices: 156 us -> 24.4 us  [exchanged(): lax.all_to_all(value, 'slab', split_axis=0, concat_axis=0, tiled=True)]
    all_to_all x3 -> x4, blocking collectives: 178 us -> 256 us  [exchanged(): lax.all_to_all(value, 'slab', split_axis=0, concat_axis=0, tiled=True)]
    all_to_all x10 -> x5, starting transfers between devices: 97 us -> 34.1 us  [exchanged(): lax.all_to_all(value, 'slab', split_axis=0, concat_axis=0, tiled=True)]
  transfers between devices with their start and end apart: 15 -> 70, of which waited for: 11 -> 30; matrix products, arithmetic and copies ran while one was open for 0% -> 0% of each run, Pallas kernels for 29% -> 15%
where the time goes in v3:
time: 1190 us; the launch traced here: 1180 us
  waiting for transfers between devices  390 us (33%)
  Pallas kernels  276 us (23%)
  blocking collectives  256 us (22%)
  starting transfers between devices  253 us (21%)
    all_to_all x4, blocking collectives, exchanged(): lax.all_to_all(value, 'slab', split_axis=0, concat_axis=0, tiled=True)  256 us
    ppermute x60, waiting for transfers between devices, ringed(): lax.ppermute(blocks[n], 'slab', [(source, (source + n) % count) for sourc...  221 us
    ppermute x60, starting transfers between devices, ringed(): lax.ppermute(blocks[n], 'slab', [(source, (source + n) % count) for sourc...  212 us
    ppermute x5, waiting for transfers between devices, swapped(): return lax.ppermute(value, axis, pairs)  145 us
    pallas_call x4, Pallas kernels, spectral(): pl.pallas_call(functools.partial(spectral_kernel, past is not None, half,...  98.9 us
    pallas_call x5, Pallas kernels, inverse(): pl.pallas_call(functools.partial(inverse_kernel, len(blocks)), out_shape=...  52.9 us
    pallas_call x2, Pallas kernels, middle(): pl.pallas_call(middle_kernel, out_shape=shapes + [rows_shape], grid=(1,),...  48.3 us
    all_to_all x5, starting transfers between devices, exchanged(): lax.all_to_all(value, 'slab', split_axis=0, concat_axis=0, tiled=True)  34.1 us
  transfers between devices with their start and end apart: 70, of which 30 were waited for; matrix products, arithmetic and copies ran while one was open for 0% of the time, Pallas kernels for 15%

profile of v3, /device:TPU:0, one launch (start us, length us, event | category | flops | bytes accessed | tf_op | source)
XLA Modules:
  0.0 1184.4 jit_solution(3258009730666072180)
XLA Ops:
  19.6 24.8 %shard_map.114 = (f32[2,256,4096]{2,1,0:T(8,128)}, f32[2,256,4096]{2,1,0:T(8,128)}) custom-call(bf16[1,9,256,4096]{3,2,1,0:T(8,128)(2,1)} %refs_23_.3, bf16[1,8,2,256,4096]{4,3,2,1,0:T(8,128)(2,1)} %history.1), custom_call_target="tpu_custom_call" | custom-call | tf_op jit(solution)/shard_map/pallas_call | solution.py:672
  44.3 16.3 %all-to-all-done.refs_17_ = f32[16,1,2,128,128]{4,3,2,1,0:T(8,128)} async-done(((f32[16,1,2,128,128]{4,3,2,1,0:T(8,128)}), f32[16,1,2,128,128]{4,3,2,1,0:T(8,128)}, u32[]{:S(2)}, u32[]{:S(2)}) %all-to-all-start) | async-done | bytes 2097184 | tf_op jit(solution)/shard_map/all_to_all | solution.py:557
  90.5 26.3 %collective-permute-done.refs_2_ = f32[2,2,128,128]{3,2,1,0:T(8,128)} collective-permute-done((f32[2,2,128,128]{3,2,1,0:T(8,128)}, f32[2,2,128,128]{3,2,1,0:T(8,128)}, u32[]{:S(2)}, u32[]{:S(2)}) %collective-permute-start) | collective-permute-done | bytes 262176 | tf_op jit(solution)/shard_map/ppermute | solution.py:551
  118.0 13.0 %collective-permute-start.6 = (f32[2,2,128,128]{3,2,1,0:T(8,128)}, f32[2,2,128,128]{3,2,1,0:T(8,128)}, u32[]{:S(2)}, u32[]{:S(2)}) collective-permute-start(f32[2,2,128,128]{3,2,1,0:T(8,128)} %get-tuple-element.127), channel_id=1, source_target_pairs={{0,7},{1,8},{2,9},{3,10},{4,11},{5,12},{6,13},{7,14},{8,15},{9,0},... | collective-permute-start | bytes 786440 | tf_op jit(solution)/shard_map/ppermute | solution.py:551
  130.9 22.4 %collective-permute-start.8 = (f32[2,2,128,128]{3,2,1,0:T(8,128)}, f32[2,2,128,128]{3,2,1,0:T(8,128)}, u32[]{:S(2)}, u32[]{:S(2)}) collective-permute-start(f32[2,2,128,128]{3,2,1,0:T(8,128)} %get-tuple-element.129), channel_id=1, source_target_pairs={{0,9},{1,10},{2,11},{3,12},{4,13},{5,14},{6,15},{7,0},{8,1},{9,2},... | collective-permute-start | bytes 786440 | tf_op jit(solution)/shard_map/ppermute | solution.py:551
  153.4 15.7 %collective-permute-done.4.refs_6_ = f32[2,2,128,128]{3,2,1,0:T(8,128)} collective-permute-done((f32[2,2,128,128]{3,2,1,0:T(8,128)}, f32[2,2,128,128]{3,2,1,0:T(8,128)}, u32[]{:S(2)}, u32[]{:S(2)}) %collective-permute-start.4) | collective-permute-done | bytes 262176 | tf_op jit(solution)/shard_map/ppermute | solution.py:551
  216.6 24.6 %shard_map.115 = (f32[1,2,128,128]{3,2,1,0:T(8,128)}, f32[1,2,128,128]{3,2,1,0:T(8,128)}, f32[1,2,128,128]{3,2,1,0:T(8,128)}, f32[1,2,128,128]{3,2,1,0:T(8,128)}...) custom-call(s32[1]{0:T(128)} %bitcast.7.place.refs_0_, ...), custom_call_target="tpu_custom_call" | custom-call | tf_op jit(solution)/shard_map/pallas_call | solution.py:719
  241.2 24.5 %shard_map.116 = (f32[16,1,2,128,128]{4,3,2,1,0:T(8,128)}, f32[16,2,2,128,128]{4,3,2,1,0:T(8,128)}, bf16[2,128,4096]{2,1,0:T(8,128)(2,1)}) custom-call(s32[1]{0:T(128)} %bitcast.7.place.refs_0_, f32[2,2,128,128]{3,2,1,0:T(8,128)} %get-tuple-element.120.refs_1_, f32[2,2,128,128]{3,2,1,0:T(8,128)} %collective-permute-done.refs_2_, ...), custom_call_target="tpu_custom_call", output_to_operand_aliasing={{1}: (23, {})} | custom-call | tf_op jit(solution)/shard_map/pallas_call | solution.py:719
  265.7 53.6 %all_to_all.45.refs_16_ = f32[16,1,2,128,128]{4,3,2,1,0:T(8,128)} all-to-all(f32[16,1,2,128,128]{4,3,2,1,0:T(8,128)} %get-tuple-element.165), channel_id=1, replica_groups=mesh['side'=2,'slab'=16] {'slab'}, dimensions={0} | all-to-all | bytes 4194304 | tf_op jit(solution)/shard_map/all_to_all | solution.py:557
  319.3 97.1 %all_to_all.46.refs_0_ = f32[16,2,2,128,128]{4,3,2,1,0:T(8,128)} all-to-all(f32[16,2,2,128,128]{4,3,2,1,0:T(8,128)S(1)} %copy-done), channel_id=1, replica_groups=mesh['side'=2,'slab'=16] {'slab'}, dimensions={0} | all-to-all | bytes 8388608 | tf_op jit(solution)/shard_map/all_to_all | solution.py:557
  436.2 40.5 %collective-permute-done.46.other = f32[128,4096]{1,0:T(8,128)} collective-permute-done((f32[128,4096]{1,0:T(8,128)}, f32[128,4096]{1,0:T(8,128)}, u32[]{:S(2)}, u32[]{:S(2)}) %collective-permute-start.46) | collective-permute-done | bytes 2097184 | tf_op jit(solution)/shard_map/ppermute | solution.py:25
  476.7 23.6 %shard_map.120 = (f32[16,1,2,128,128]{4,3,2,1,0:T(8,128)}, f32[16,1,2,128,128]{4,3,2,1,0:T(8,128)}, f32[128,4096]{1,0:T(8,128)}) custom-call(s32[1]{0:T(128)} %bitcast.7.place.refs_0_, f32[5]{0:T(128)} %stack.28.scalars, f32[128,4096]{1,0:T(8,128)} %shard_map.119.own, f32[128,4096]{1,0:T(8,128)} %collective-permute-done.46.other, f32[256,4096]{1,0:T(8,128)} %prestress.9, ...), custom_call_target="tpu_custom_call" | custom-call | tf_op jit(solution)/shard_map/pallas_call | solution.py:626
  500.2 52.0 %all_to_all.47.refs_17_ = f32[16,1,2,128,128]{4,3,2,1,0:T(8,128)} all-to-all(f32[16,1,2,128,128]{4,3,2,1,0:T(8,128)} %get-tuple-element.185), channel_id=1, replica_groups=mesh['side'=2,'slab'=16] {'slab'}, dimensions={0} | all-to-all | bytes 4194304 | tf_op jit(solution)/shard_map/all_to_all | solution.py:557
  563.6 36.2 %collective-permute-done.15.refs_1_ = f32[1,2,128,128]{3,2,1,0:T(8,128)} collective-permute-done((f32[1,2,128,128]{3,2,1,0:T(8,128)S(1)}, f32[1,2,128,128]{3,2,1,0:T(8,128)}, u32[]{:S(2)}, u32[]{:S(2)}) %collective-permute-start.15) | collective-permute-done | bytes 131104 | tf_op jit(solution)/shard_map/ppermute | solution.py:551
  601.0 14.3 %collective-permute-start.21 = (f32[1,2,128,128]{3,2,1,0:T(8,128)S(1)}, f32[1,2,128,128]{3,2,1,0:T(8,128)}, u32[]{:S(2)}, u32[]{:S(2)}) collective-permute-start(f32[1,2,128,128]{3,2,1,0:T(8,128)S(1)} %copy-done.9), channel_id=1, source_target_pairs={{0,7},{1,8},{2,9},{3,10},{4,11},{5,12},{6,13},{7,14},{8,15},{9,0},... | collective-permute-start | bytes 393224 | tf_op jit(solution)/shard_map/ppermute | solution.py:551
  667.2 47.0 %collective-permute-done.30.other = f32[128,4096]{1,0:T(8,128)} collective-permute-done((f32[128,4096]{1,0:T(8,128)}, f32[128,4096]{1,0:T(8,128)}, u32[]{:S(2)}, u32[]{:S(2)}) %collective-permute-start.30) | collective-permute-done | bytes 2097184 | tf_op jit(solution)/shard_map/ppermute | solution.py:25
  714.2 24.8 %shard_map.118 = (f32[2,2,128,128]{3,2,1,0:T(8,128)}, f32[2,2,128,128]{3,2,1,0:T(8,128)}, f32[2,2,128,128]{3,2,1,0:T(8,128)}, f32[2,2,128,128]{3,2,1,0:T(8,128)}...) custom-call(s32[1]{0:T(128)} %bitcast.7.place.refs_0_, ...), custom_call_target="tpu_custom_call" | custom-call | tf_op jit(solution)/shard_map/pallas_call | solution.py:626
  759.1 36.3 %collective-permute-done.35.refs_6_ = f32[2,2,128,128]{3,2,1,0:T(8,128)} collective-permute-done((f32[2,2,128,128]{3,2,1,0:T(8,128)}, f32[2,2,128,128]{3,2,1,0:T(8,128)}, u32[]{:S(2)}, u32[]{:S(2)}) %collective-permute-start.35) | collective-permute-done | bytes 262176 | tf_op jit(solution)/shard_map/ppermute | solution.py:551
  836.5 25.1 %shard_map.121 = (f32[1,2,128,128]{3,2,1,0:T(8,128)}, f32[1,2,128,128]{3,2,1,0:T(8,128)}, f32[1,2,128,128]{3,2,1,0:T(8,128)}, f32[1,2,128,128]{3,2,1,0:T(8,128)}...) custom-call(s32[1]{0:T(128)} %bitcast.7.place.refs_0_, ...), custom_call_target="tpu_custom_call" | custom-call | tf_op jit(solution)/shard_map/pallas_call | solution.py:719
  861.6 24.7 %shard_map.122 = (f32[16,1,2,128,128]{4,3,2,1,0:T(8,128)}, f32[16,2,2,80,128]{4,3,2,1,0:T(8,128)}, f32[16,2,2,48,128]{4,3,2,1,0:T(8,128)}) custom-call(s32[1]{0:T(128)} %bitcast.7.place.refs_0_, f32[2,2,128,128]{3,2,1,0:T(8,128)} %get-tuple-element.168.refs_1_, ...), custom_call_target="tpu_custom_call", output_to_operand_aliasing={{1}: (25, {}), {2}: (26, {})} | custom-call | tf_op jit(solution)/shard_map/pallas_call | solution.py:719
  886.3 53.2 %all_to_all.48.refs_16_ = f32[16,1,2,128,128]{4,3,2,1,0:T(8,128)} all-to-all(f32[16,1,2,128,128]{4,3,2,1,0:T(8,128)} %get-tuple-element.198), channel_id=1, replica_groups=mesh['side'=2,'slab'=16] {'slab'}, dimensions={0} | all-to-all | bytes 4194304 | tf_op jit(solution)/shard_map/all_to_all | solution.py:557
  950.9 44.7 %collective-permute-done.47.refs_1_ = f32[1,2,128,128]{3,2,1,0:T(8,128)} collective-permute-done((f32[1,2,128,128]{3,2,1,0:T(8,128)S(1)}, f32[1,2,128,128]{3,2,1,0:T(8,128)}, u32[]{:S(2)}, u32[]{:S(2)}) %collective-permute-start.47) | collective-permute-done | bytes 131104 | tf_op jit(solution)/shard_map/ppermute | solution.py:551
  996.7 17.0 %collective-permute-start.53 = (f32[1,2,128,128]{3,2,1,0:T(8,128)S(1)}, f32[1,2,128,128]{3,2,1,0:T(8,128)}, u32[]{:S(2)}, u32[]{:S(2)}) collective-permute-start(f32[1,2,128,128]{3,2,1,0:T(8,128)S(1)} %copy-done.24), channel_id=1, source_target_pairs={{0,7},{1,8},{2,9},{3,10},{4,11},{5,12},{6,13},{7,14},{8,15},{9,0},... | collective-permute-start | bytes 393224 | tf_op jit(solution)/shard_map/ppermute | solution.py:551
  1065.7 47.0 %collective-permute-done.62.other = f32[128,4096]{1,0:T(8,128)} collective-permute-done((f32[128,4096]{1,0:T(8,128)}, f32[128,4096]{1,0:T(8,128)}, u32[]{:S(2)}, u32[]{:S(2)}) %collective-permute-start.62) | collective-permute-done | bytes 2097184 | tf_op jit(solution)/shard_map/ppermute | solution.py:25
  (204 shorter events, 373.8 us)
Async XLA Ops:
  12.1 48.5 %all-to-all-start = ((f32[16,1,2,128,128]{4,3,2,1,0:T(8,128)}), f32[16,1,2,128,128]{4,3,2,1,0:T(8,128)}, u32[]{:S(2)}, u32[]{:S(2)}) async-start(f32[16,1,2,128,128]{4,3,2,1,0:T(8,128)} %get-tuple-element.138), calls=%async_computation | async-start | bytes 4194304 | tf_op jit(solution)/shard_map/all_to_all | solution.py:557
  60.6 180.6 %all-to-all-start.1 = ((f32[16,1,2,128,128]{4,3,2,1,0:T(8,128)}), f32[16,1,2,128,128]{4,3,2,1,0:T(8,128)}, u32[]{:S(2)}, u32[]{:S(2)}) async-start(f32[16,1,2,128,128]{4,3,2,1,0:T(8,128)} %get-tuple-element.161), calls=%async_computation.1 | async-start | bytes 4194304 | tf_op jit(solution)/shard_map/all_to_all | solution.py:557
  90.3 78.8 %collective-permute-start.4 = (f32[2,2,128,128]{3,2,1,0:T(8,128)}, f32[2,2,128,128]{3,2,1,0:T(8,128)}, u32[]{:S(2)}, u32[]{:S(2)}) collective-permute-start(f32[2,2,128,128]{3,2,1,0:T(8,128)} %get-tuple-element.125), channel_id=1, source_target_pairs={{0,5},{1,6},{2,7},{3,8},{4,9},{5,10},{6,11},{7,12},{8,13},{9,14},{... | collective-permute-start | bytes 786440 | tf_op jit(solution)/shard_map/ppermute | solution.py:551
  116.8 53.5 %collective-permute-start.5 = (f32[2,2,128,128]{3,2,1,0:T(8,128)}, f32[2,2,128,128]{3,2,1,0:T(8,128)}, u32[]{:S(2)}, u32[]{:S(2)}) collective-permute-start(f32[2,2,128,128]{3,2,1,0:T(8,128)} %get-tuple-element.126), channel_id=1, source_target_pairs={{0,6},{1,7},{2,8},{3,9},{4,10},{5,11},{6,12},{7,13},{8,14},{9,15},... | collective-permute-start | bytes 786440 | tf_op jit(solution)/shard_map/ppermute | solution.py:551
  118.0 58.9 %collective-permute-start.6 = (f32[2,2,128,128]{3,2,1,0:T(8,128)}, f32[2,2,128,128]{3,2,1,0:T(8,128)}, u32[]{:S(2)}, u32[]{:S(2)}) collective-permute-start(f32[2,2,128,128]{3,2,1,0:T(8,128)} %get-tuple-element.127), channel_id=1, source_target_pairs={{0,7},{1,8},{2,9},{3,10},{4,11},{5,12},{6,13},{7,14},{8,15},{9,0},... | collective-permute-start | bytes 786440 | tf_op jit(solution)/shard_map/ppermute | solution.py:551
  130.9 58.5 %collective-permute-start.7 = (f32[2,2,128,128]{3,2,1,0:T(8,128)}, f32[2,2,128,128]{3,2,1,0:T(8,128)}, u32[]{:S(2)}, u32[]{:S(2)}) collective-permute-start(f32[2,2,128,128]{3,2,1,0:T(8,128)} %get-tuple-element.128), channel_id=1, source_target_pairs={{0,8},{1,9},{2,10},{3,11},{4,12},{5,13},{6,14},{7,15},{8,0},{9,1},... | collective-permute-start | bytes 786440 | tf_op jit(solution)/shard_map/ppermute | solution.py:551
  130.9 62.8 %collective-permute-start.8 = (f32[2,2,128,128]{3,2,1,0:T(8,128)}, f32[2,2,128,128]{3,2,1,0:T(8,128)}, u32[]{:S(2)}, u32[]{:S(2)}) collective-permute-start(f32[2,2,128,128]{3,2,1,0:T(8,128)} %get-tuple-element.129), channel_id=1, source_target_pairs={{0,9},{1,10},{2,11},{3,12},{4,13},{5,14},{6,15},{7,0},{8,1},{9,2},... | collective-permute-start | bytes 786440 | tf_op jit(solution)/shard_map/ppermute | solution.py:551
  427.8 48.8 %collective-permute-start.46 = (f32[128,4096]{1,0:T(8,128)}, f32[128,4096]{1,0:T(8,128)}, u32[]{:S(2)}, u32[]{:S(2)}) collective-permute-start(f32[128,4096]{1,0:T(8,128)} %shard_map.119.own), channel_id=1, source_target_pairs={{0,16},{16,0},{1,17},{17,1},{2,18},{18,2},{3,19},{19,3},{4,20},{20... | collective-permute-start | bytes 6291464 | tf_op jit(solution)/shard_map/ppermute | solution.py:25
  552.4 309.2 %all-to-all-start.5 = ((f32[16,1,2,128,128]{4,3,2,1,0:T(8,128)}), f32[16,1,2,128,128]{4,3,2,1,0:T(8,128)}, u32[]{:S(2)}, u32[]{:S(2)}) async-start(f32[16,1,2,128,128]{4,3,2,1,0:T(8,128)} %get-tuple-element.188), calls=%async_computation.5 | async-start | bytes 4194304 | tf_op jit(solution)/shard_map/all_to_all | solution.py:557
  559.8 55.5 %collective-permute-start.17 = (f32[1,2,128,128]{3,2,1,0:T(8,128)S(1)}, f32[1,2,128,128]{3,2,1,0:T(8,128)}, u32[]{:S(2)}, u32[]{:S(2)}) collective-permute-start(f32[1,2,128,128]{3,2,1,0:T(8,128)S(1)} %copy-done.18), channel_id=1, source_target_pairs={{0,3},{1,4},{2,5},{3,6},{4,7},{5,8},{6,9},{7,10},{8,11},{9,12},{10... | collective-permute-start | bytes 393224 | tf_op jit(solution)/shard_map/ppermute | solution.py:551
  562.0 54.0 %collective-permute-start.18 = (f32[1,2,128,128]{3,2,1,0:T(8,128)S(1)}, f32[1,2,128,128]{3,2,1,0:T(8,128)}, u32[]{:S(2)}, u32[]{:S(2)}) collective-permute-start(f32[1,2,128,128]{3,2,1,0:T(8,128)S(1)} %copy-done.15), channel_id=1, source_target_pairs={{0,4},{1,5},{2,6},{3,7},{4,8},{5,9},{6,10},{7,11},{8,12},{9,13},{1... | collective-permute-start | bytes 393224 | tf_op jit(solution)/shard_map/ppermute | solution.py:551
  563.5 67.7 %collective-permute-start.19 = (f32[1,2,128,128]{3,2,1,0:T(8,128)S(1)}, f32[1,2,128,128]{3,2,1,0:T(8,128)}, u32[]{:S(2)}, u32[]{:S(2)}) collective-permute-start(f32[1,2,128,128]{3,2,1,0:T(8,128)S(1)} %copy-done.12), channel_id=1, source_target_pairs={{0,5},{1,6},{2,7},{3,8},{4,9},{5,10},{6,11},{7,12},{8,13},{9,14},{... | collective-permute-start | bytes 393224 | tf_op jit(solution)/shard_map/ppermute | solution.py:551
  665.7 48.5 %collective-permute-start.30 = (f32[128,4096]{1,0:T(8,128)}, f32[128,4096]{1,0:T(8,128)}, u32[]{:S(2)}, u32[]{:S(2)}) collective-permute-start(f32[128,4096]{1,0:T(8,128)} %shard_map.117.own), channel_id=1, source_target_pairs={{0,16},{16,0},{1,17},{17,1},{2,18},{18,2},{3,19},{19,3},{4,20},{20... | collective-permute-start | bytes 6291464 | tf_op jit(solution)/shard_map/ppermute | solution.py:25
  744.2 51.2 %collective-permute-start.35 = (f32[2,2,128,128]{3,2,1,0:T(8,128)}, f32[2,2,128,128]{3,2,1,0:T(8,128)}, u32[]{:S(2)}, u32[]{:S(2)}) collective-permute-start(f32[2,2,128,128]{3,2,1,0:T(8,128)} %get-tuple-element.173), channel_id=1, source_target_pairs={{0,5},{1,6},{2,7},{3,8},{4,9},{5,10},{6,11},{7,12},{8,13},{9,14},{... | collective-permute-start | bytes 786440 | tf_op jit(solution)/shard_map/ppermute | solution.py:551
  751.4 48.9 %collective-permute-start.37 = (f32[2,2,128,128]{3,2,1,0:T(8,128)}, f32[2,2,128,128]{3,2,1,0:T(8,128)}, u32[]{:S(2)}, u32[]{:S(2)}) collective-permute-start(f32[2,2,128,128]{3,2,1,0:T(8,128)} %get-tuple-element.175), channel_id=1, source_target_pairs={{0,7},{1,8},{2,9},{3,10},{4,11},{5,12},{6,13},{7,14},{8,15},{9,0},... | collective-permute-start | bytes 786440 | tf_op jit(solution)/shard_map/ppermute | solution.py:551
  754.9 54.4 %collective-permute-start.38 = (f32[2,2,128,128]{3,2,1,0:T(8,128)}, f32[2,2,128,128]{3,2,1,0:T(8,128)}, u32[]{:S(2)}, u32[]{:S(2)}) collective-permute-start(f32[2,2,128,128]{3,2,1,0:T(8,128)} %get-tuple-element.176), channel_id=1, source_target_pairs={{0,8},{1,9},{2,10},{3,11},{4,12},{5,13},{6,14},{7,15},{8,0},{9,1},... | collective-permute-start | bytes 786440 | tf_op jit(solution)/shard_map/ppermute | solution.py:551
  755.3 58.2 %collective-permute-start.39 = (f32[2,2,128,128]{3,2,1,0:T(8,128)}, f32[2,2,128,128]{3,2,1,0:T(8,128)}, u32[]{:S(2)}, u32[]{:S(2)}) collective-permute-start(f32[2,2,128,128]{3,2,1,0:T(8,128)} %get-tuple-element.177), channel_id=1, source_target_pairs={{0,9},{1,10},{2,11},{3,12},{4,13},{5,14},{6,15},{7,0},{8,1},{9,2},... | collective-permute-start | bytes 786440 | tf_op jit(solution)/shard_map/ppermute | solution.py:551
  939.7 173.0 %all-to-all-start.7 = ((f32[16,2,2,80,128]{4,3,2,1,0:T(8,128)}), f32[16,2,2,80,128]{4,3,2,1,0:T(8,128)}, u32[]{:S(2)}, u32[]{:S(2)}) async-start(f32[16,2,2,80,128]{4,3,2,1,0:T(8,128)} %get-tuple-element.201), calls=%async_computation.7 | async-start | bytes 5242880 | tf_op jit(solution)/shard_map/all_to_all | solution.py:557
  945.0 50.5 %collective-permute-start.47 = (f32[1,2,128,128]{3,2,1,0:T(8,128)S(1)}, f32[1,2,128,128]{3,2,1,0:T(8,128)}, u32[]{:S(2)}, u32[]{:S(2)}) collective-permute-start(f32[1,2,128,128]{3,2,1,0:T(8,128)S(1)} %copy-done.30), channel_id=1, source_target_pairs={{0,1},{1,2},{2,3},{3,4},{4,5},{5,6},{6,7},{7,8},{8,9},{9,10},{10,1... | collective-permute-start | bytes 393224 | tf_op jit(solution)/shard_map/ppermute | solution.py:551
  945.4 51.3 %collective-permute-start.48 = (f32[1,2,128,128]{3,2,1,0:T(8,128)S(1)}, f32[1,2,128,128]{3,2,1,0:T(8,128)}, u32[]{:S(2)}, u32[]{:S(2)}) collective-permute-start(f32[1,2,128,128]{3,2,1,0:T(8,128)S(1)} %copy-done.29), channel_id=1, source_target_pairs={{0,2},{1,3},{2,4},{3,5},{4,6},{5,7},{6,8},{7,9},{8,10},{9,11},{10,... | collective-permute-start | bytes 393224 | tf_op jit(solution)/shard_map/ppermute | solution.py:551
  947.1 66.7 %collective-permute-start.49 = (f32[1,2,128,128]{3,2,1,0:T(8,128)S(1)}, f32[1,2,128,128]{3,2,1,0:T(8,128)}, u32[]{:S(2)}, u32[]{:S(2)}) collective-permute-start(f32[1,2,128,128]{3,2,1,0:T(8,128)S(1)} %copy-done.28), channel_id=1, source_target_pairs={{0,3},{1,4},{2,5},{3,6},{4,7},{5,8},{6,9},{7,10},{8,11},{9,12},{10... | collective-permute-start | bytes 393224 | tf_op jit(solution)/shard_map/ppermute | solution.py:551
  949.3 65.2 %collective-permute-start.50 = (f32[1,2,128,128]{3,2,1,0:T(8,128)S(1)}, f32[1,2,128,128]{3,2,1,0:T(8,128)}, u32[]{:S(2)}, u32[]{:S(2)}) collective-permute-start(f32[1,2,128,128]{3,2,1,0:T(8,128)S(1)} %copy-done.27), channel_id=1, source_target_pairs={{0,4},{1,5},{2,6},{3,7},{4,8},{5,9},{6,10},{7,11},{8,12},{9,13},{1... | collective-permute-start | bytes 393224 | tf_op jit(solution)/shard_map/ppermute | solution.py:551
  950.8 78.9 %collective-permute-start.51 = (f32[1,2,128,128]{3,2,1,0:T(8,128)S(1)}, f32[1,2,128,128]{3,2,1,0:T(8,128)}, u32[]{:S(2)}, u32[]{:S(2)}) collective-permute-start(f32[1,2,128,128]{3,2,1,0:T(8,128)S(1)} %copy-done.26), channel_id=1, source_target_pairs={{0,5},{1,6},{2,7},{3,8},{4,9},{5,10},{6,11},{7,12},{8,13},{9,14},{... | collective-permute-start | bytes 393224 | tf_op jit(solution)/shard_map/ppermute | solution.py:551
  1064.2 48.5 %collective-permute-start.62 = (f32[128,4096]{1,0:T(8,128)}, f32[128,4096]{1,0:T(8,128)}, u32[]{:S(2)}, u32[]{:S(2)}) collective-permute-start(f32[128,4096]{1,0:T(8,128)} %shard_map.123.own), channel_id=1, source_target_pairs={{0,16},{16,0},{1,17},{17,1},{2,18},{18,2},{3,19},{19,3},{4,20},{20... | collective-permute-start | bytes 6291464 | tf_op jit(solution)/shard_map/ppermute | solution.py:25
  (77 other events, 2855.2 us)

commit v4 on v3

--- a/solution.py
+++ b/solution.py
@@ -399,10 +399,10 @@
     lax.fori_loop(0, now.shape[2] // 256, group, 0)
 
 
-def spectral_kernel(has_past, half, pieces, *refs):
-    place, ring, block = refs[0], refs[1 : RADIX + 1], refs[RADIX + 1]
-    kernel_now, past_sum, table, twist, twist_ring = refs[RADIX + 2 : RADIX + 7]
-    rest = list(refs[RADIX + 7 :])
+def spectral_kernel(count, has_past, half, pieces, *refs):
+    place, ring, block = refs[0], refs[1 : count + 1], refs[count + 1]
+    kernel_now, past_sum, table, twist, twist_ring = refs[count + 2 : count + 7]
+    rest = list(refs[count + 7 :])
     if has_past:
         kernel_past, spec_past = rest.pop(0), rest.pop(0)
         spec_out = None
@@ -422,9 +422,14 @@
 
     def group(g, carry):
         at = pl.ds(pl.multiple_of(g * 16, 16), 16)
-        values = [(ring[n][0, 0, at, :], ring[n][0, 1, at, :]) for n in range(RADIX)]
-        for k, value in enumerate(sixteen(values, 1)):
-            store_split(held, k, g, 0, *twisted(value, twist_ring, k, 0, -1))
+        if count == 1:
+            values = [(ring[0][n, 0, 0, at, :], ring[0][n, 0, 1, at, :]) for n in range(RADIX)]
+            sign, turn = -1, twist
+        else:
+            values = [(ring[n][0, 0, at, :], ring[n][0, 1, at, :]) for n in range(RADIX)]
+            sign, turn = 1, twist_ring
+        for k, value in enumerate(sixteen(values, sign)):
+            store_split(held, k, g, 0, *twisted(value, turn, k, 0, -1))
         values = [(block[n, 0, 0, at, :], block[n, 0, 1, at, :]) for n in range(RADIX)]
         for k, value in enumerate(sixteen(values, -1)):
             store_split(held, k, g, 128, *twisted(value, twist, k, 128, -1))
@@ -590,8 +595,8 @@
     def ring_tiles(count):
         return [jax.ShapeDtypeStruct((count, 2, 128, 128), f32)] * slabs
 
-    def forward_shapes(chunk):
-        shapes = ring_tiles(halves) if chunk == 0 else tiles([1, 1])
+    def forward_shapes(chunk, ring):
+        shapes = ring_tiles(halves) if ring else tiles([[halves], [1, 1]][chunk])
         return shapes, [whole_spec(shape) for shape in shapes]
 
     me = lax.axis_index("slab")
@@ -605,7 +610,7 @@
         return pl.BlockSpec((chunk_rows, length), lambda *_: (chunk, 0))
 
     def start(chunk):
-        shapes, specs = forward_shapes(chunk)
+        shapes, specs = forward_shapes(chunk, chunk == 0)
         return pl.pallas_call(
             start_kernel,
             out_shape=shapes,
@@ -622,7 +627,7 @@
         )(place, velocity, table, twist)
 
     def middle(chunk, own, other, state):
-        shapes, specs = forward_shapes(chunk)
+        shapes, specs = forward_shapes(chunk, False)
         *sent, state_new = pl.pallas_call(
             middle_kernel,
             out_shape=shapes + [rows_shape],
@@ -695,7 +700,8 @@
         spec_spec = pl.BlockSpec((2, 128, length), lambda *_: (0, 0, 0))
         ring_spec = pl.BlockSpec((1, 2, 128, 128), lambda *_: (half, 0, 0, 0))
         operands = [place, *ring, near, kernel, past_sum, table, twist, twist_ring]
-        in_specs = [SCALARS] + [ring_spec] * slabs + [block(near), lag_spec[0], sum_spec]
+        in_specs = [SCALARS] + ([ring_spec] * slabs if len(ring) > 1 else [block(ring[0])])
+        in_specs += [block(near), lag_spec[0], sum_spec]
         in_specs += [whole_spec(table), whole_spec(twist), whole_spec(twist_ring)]
         out_shape = tiles([1]) if half else []
         for row, count in pieces[1:]:
@@ -717,7 +723,7 @@
             operands += before
             in_specs += [pl.BlockSpec(memory_space=pl.ANY)] * len(before)
         return pl.pallas_call(
-            functools.partial(spectral_kernel, past is not None, half, pieces),
+            functools.partial(spectral_kernel, len(ring), past is not None, half, pieces),
             input_output_aliases=aliases,
             out_shape=out_shape,
             grid=(1,),
@@ -755,7 +761,7 @@
         pieces = [(0, whole), (whole, cut), (whole + cut, whole - cut)]
         if not last:
             pieces = [(0, whole), (whole, whole)]
-        ring = ringed(sent[0])
+        ring = ringed(sent[0]) if step_index == 0 else [exchanged(sent[0][0])]
         if step_index == 0:
             sent[1] = start(1)
             sent[1], shift = hold((tuple(sent[1]), me))
@@ -767,6 +773,7 @@
         else:
             own = inverse(waiting)
             sent[1], states[1] = middle(1, own, swapped(own, "side", 0), states[1])
+            ring, sent[1], states[1] = hold((ring, sent[1], states[1]))
         near = exchanged(sent[1][0])
         if step_index == 0:
             sums = past_sums()
@@ -790,6 +797,7 @@
         if not last:
             sent[0], states[0] = middle(0, own, other, states[0])
         if not last:
+            waiting, sent[0], states[0] = hold((waiting, sent[0], states[0]))
             continue
         waiting, own, other, final = hold((waiting, own, other, late[1]))
         final = exchanged(final)

time: 1190 us -> 1080 us (0.908)
  blocking collectives: 256 us -> 173 us
  starting transfers between devices: 253 us -> 227 us
    all_to_all x4 -> x3, blocking collectives: 256 us -> 173 us  [exchanged(): lax.all_to_all(value, 'slab', split_axis=0, concat_axis=0, tiled=True)]
    ppermute x60 -> x45, starting transfers between devices: 212 us -> 175 us  [ringed(): lax.ppermute(blocks[n], 'slab', [(source, (source + n) % count) for sourc...]
    ppermute x60 -> x45, waiting for transfers between devices: 221 us -> 205 us  [ringed(): lax.ppermute(blocks[n], 'slab', [(source, (source + n) % count) for sourc...]
    all_to_all x5 -> x7, waiting for transfers between devices: 24.4 us -> 40.4 us  [exchanged(): lax.all_to_all(value, 'slab', split_axis=0, concat_axis=0, tiled=True)]
    all_to_all x5 -> x7, starting transfers between devices: 34.1 us -> 44 us  [exchanged(): lax.all_to_all(value, 'slab', split_axis=0, concat_axis=0, tiled=True)]
  transfers between devices with their start and end apart: 70 -> 57, of which waited for: 30 -> 25; matrix products, arithmetic and copies ran while one was open for 0% -> 0% of each run, Pallas kernels for 15% -> 19%
where the time goes in v4:
time: 1080 us; the launch traced here: 1070 us
  waiting for transfers between devices  389 us (36%)
  Pallas kernels  274 us (25%)
  starting transfers between devices  227 us (21%)
  blocking collectives  173 us (16%)
    ppermute x45, waiting for transfers between devices, ringed(): lax.ppermute(blocks[n], 'slab', [(source, (source + n) % count) for sourc...  205 us
    ppermute x45, starting transfers between devices, ringed(): lax.ppermute(blocks[n], 'slab', [(source, (source + n) % count) for sourc...  175 us
    all_to_all x3, blocking collectives, exchanged(): lax.all_to_all(value, 'slab', split_axis=0, concat_axis=0, tiled=True)  173 us
    ppermute x5, waiting for transfers between devices, swapped(): return lax.ppermute(value, axis, pairs)  144 us
    pallas_call x4, Pallas kernels, spectral(): pl.pallas_call(functools.partial(spectral_kernel, len(ring), past is not...  98.7 us
    pallas_call x5, Pallas kernels, inverse(): pl.pallas_call(functools.partial(inverse_kernel, len(blocks)), out_shape=...  52.9 us
    pallas_call x2, Pallas kernels, middle(): pl.pallas_call(middle_kernel, out_shape=shapes + [rows_shape], grid=(1,),...  46.4 us
    all_to_all x7, starting transfers between devices, exchanged(): lax.all_to_all(value, 'slab', split_axis=0, concat_axis=0, tiled=True)  44 us
  transfers between devices with their start and end apart: 57, of which 25 were waited for; matrix products, arithmetic and copies ran while one was open for 0% of the time, Pallas kernels for 19%

profile of v4, /device:TPU:0, one launch (start us, length us, event | category | flops | bytes accessed | tf_op | source)
XLA Modules:
  0.0 1071.8 jit_solution(11462185679475389446)
XLA Ops:
  19.6 24.8 %shard_map.114 = (f32[2,256,4096]{2,1,0:T(8,128)}, f32[2,256,4096]{2,1,0:T(8,128)}) custom-call(bf16[1,9,256,4096]{3,2,1,0:T(8,128)(2,1)} %refs_8_.3, bf16[1,8,2,256,4096]{4,3,2,1,0:T(8,128)(2,1)} %history.1), custom_call_target="tpu_custom_call" | custom-call | tf_op jit(solution)/shard_map/pallas_call | solution.py:677
  44.3 16.3 %all-to-all-done.refs_17_ = f32[16,1,2,128,128]{4,3,2,1,0:T(8,128)} async-done(((f32[16,1,2,128,128]{4,3,2,1,0:T(8,128)}), f32[16,1,2,128,128]{4,3,2,1,0:T(8,128)}, u32[]{:S(2)}, u32[]{:S(2)}) %all-to-all-start) | async-done | bytes 2097184 | tf_op jit(solution)/shard_map/all_to_all | solution.py:562
  90.5 26.3 %collective-permute-done.refs_2_ = f32[2,2,128,128]{3,2,1,0:T(8,128)} collective-permute-done((f32[2,2,128,128]{3,2,1,0:T(8,128)}, f32[2,2,128,128]{3,2,1,0:T(8,128)}, u32[]{:S(2)}, u32[]{:S(2)}) %collective-permute-start) | collective-permute-done | bytes 262176 | tf_op jit(solution)/shard_map/ppermute | solution.py:556
  118.0 13.0 %collective-permute-start.6 = (f32[2,2,128,128]{3,2,1,0:T(8,128)}, f32[2,2,128,128]{3,2,1,0:T(8,128)}, u32[]{:S(2)}, u32[]{:S(2)}) collective-permute-start(f32[2,2,128,128]{3,2,1,0:T(8,128)} %get-tuple-element.119), channel_id=1, source_target_pairs={{0,7},{1,8},{2,9},{3,10},{4,11},{5,12},{6,13},{7,14},{8,15},{9,0},... | collective-permute-start | bytes 786440 | tf_op jit(solution)/shard_map/ppermute | solution.py:556
  130.9 22.4 %collective-permute-start.8 = (f32[2,2,128,128]{3,2,1,0:T(8,128)}, f32[2,2,128,128]{3,2,1,0:T(8,128)}, u32[]{:S(2)}, u32[]{:S(2)}) collective-permute-start(f32[2,2,128,128]{3,2,1,0:T(8,128)} %get-tuple-element.121), channel_id=1, source_target_pairs={{0,9},{1,10},{2,11},{3,12},{4,13},{5,14},{6,15},{7,0},{8,1},{9,2},... | collective-permute-start | bytes 786440 | tf_op jit(solution)/shard_map/ppermute | solution.py:556
  153.4 15.7 %collective-permute-done.4.refs_6_ = f32[2,2,128,128]{3,2,1,0:T(8,128)} collective-permute-done((f32[2,2,128,128]{3,2,1,0:T(8,128)}, f32[2,2,128,128]{3,2,1,0:T(8,128)}, u32[]{:S(2)}, u32[]{:S(2)}) %collective-permute-start.4) | collective-permute-done | bytes 262176 | tf_op jit(solution)/shard_map/ppermute | solution.py:556
  216.6 24.6 %shard_map.115 = (f32[1,2,128,128]{3,2,1,0:T(8,128)}, f32[1,2,128,128]{3,2,1,0:T(8,128)}, f32[1,2,128,128]{3,2,1,0:T(8,128)}, f32[1,2,128,128]{3,2,1,0:T(8,128)}...) custom-call(s32[1]{0:T(128)} %bitcast.7.place.refs_0_, ...), custom_call_target="tpu_custom_call" | custom-call | tf_op jit(solution)/shard_map/pallas_call | solution.py:725
  241.2 24.5 %shard_map.116 = (f32[16,1,2,128,128]{4,3,2,1,0:T(8,128)}, f32[16,2,2,128,128]{4,3,2,1,0:T(8,128)}, bf16[2,128,4096]{2,1,0:T(8,128)(2,1)}) custom-call(s32[1]{0:T(128)} %bitcast.7.place.refs_0_, f32[2,2,128,128]{3,2,1,0:T(8,128)} %get-tuple-element.112.refs_1_, f32[2,2,128,128]{3,2,1,0:T(8,128)} %collective-permute-done.refs_2_, ...), custom_call_target="tpu_custom_call", output_to_operand_aliasing={{1}: (23, {})} | custom-call | tf_op jit(solution)/shard_map/pallas_call | solution.py:725
  265.7 53.3 %all_to_all.50.refs_16_ = f32[16,1,2,128,128]{4,3,2,1,0:T(8,128)} all-to-all(f32[16,1,2,128,128]{4,3,2,1,0:T(8,128)} %get-tuple-element.141), channel_id=1, replica_groups=mesh['side'=2,'slab'=16] {'slab'}, dimensions={0} | all-to-all | bytes 4194304 | tf_op jit(solution)/shard_map/all_to_all | solution.py:562
  330.4 69.9 %collective-permute-done.15.refs_1_ = f32[1,2,128,128]{3,2,1,0:T(8,128)} collective-permute-done((f32[1,2,128,128]{3,2,1,0:T(8,128)S(1)}, f32[1,2,128,128]{3,2,1,0:T(8,128)}, u32[]{:S(2)}, u32[]{:S(2)}) %collective-permute-start.15) | collective-permute-done | bytes 131104 | tf_op jit(solution)/shard_map/ppermute | solution.py:556
  401.5 25.4 %collective-permute-start.21 = (f32[1,2,128,128]{3,2,1,0:T(8,128)S(1)}, f32[1,2,128,128]{3,2,1,0:T(8,128)}, u32[]{:S(2)}, u32[]{:S(2)}) collective-permute-start(f32[1,2,128,128]{3,2,1,0:T(8,128)S(1)} %copy-done.15), channel_id=1, source_target_pairs={{0,7},{1,8},{2,9},{3,10},{4,11},{5,12},{6,13},{7,14},{8,15},{9,0},... | collective-permute-start | bytes 393224 | tf_op jit(solution)/shard_map/ppermute | solution.py:556
  429.9 13.0 %collective-permute-done.19.refs_5_ = f32[1,2,128,128]{3,2,1,0:T(8,128)} collective-permute-done((f32[1,2,128,128]{3,2,1,0:T(8,128)S(1)}, f32[1,2,128,128]{3,2,1,0:T(8,128)}, u32[]{:S(2)}, u32[]{:S(2)}) %collective-permute-start.19) | collective-permute-done | bytes 131104 | tf_op jit(solution)/shard_map/ppermute | solution.py:556
  485.6 40.1 %collective-permute-done.30.other = f32[128,4096]{1,0:T(8,128)} collective-permute-done((f32[128,4096]{1,0:T(8,128)}, f32[128,4096]{1,0:T(8,128)}, u32[]{:S(2)}, u32[]{:S(2)}) %collective-permute-start.30) | collective-permute-done | bytes 2097184 | tf_op jit(solution)/shard_map/ppermute | solution.py:25
  525.8 22.8 %shard_map.118 = (f32[16,2,2,128,128]{4,3,2,1,0:T(8,128)}, f32[128,4096]{1,0:T(8,128)}) custom-call(s32[1]{0:T(128)} %bitcast.7.place.refs_0_, f32[5]{0:T(128)} %stack.28.scalars, f32[128,4096]{1,0:T(8,128)} %shard_map.117.own, f32[128,4096]{1,0:T(8,128)} %collective-permute-done.30.other, f32[256,4096]{1,0:T(8,128)} %prestress.9, f32[256,4096]{1,0:T(8,128)} %strength.9, ...), custom_call_target="tpu_custom_call" | custom-call | tf_op jit(solution)/shard_map/pallas_call | solution.py:631
  566.3 46.6 %collective-permute-done.31.other = f32[128,4096]{1,0:T(8,128)} collective-permute-done((f32[128,4096]{1,0:T(8,128)}, f32[128,4096]{1,0:T(8,128)}, u32[]{:S(2)}, u32[]{:S(2)}) %collective-permute-start.31) | collective-permute-done | bytes 2097184 | tf_op jit(solution)/shard_map/ppermute | solution.py:25
  612.9 23.6 %shard_map.120 = (f32[16,1,2,128,128]{4,3,2,1,0:T(8,128)}, f32[16,1,2,128,128]{4,3,2,1,0:T(8,128)}, f32[128,4096]{1,0:T(8,128)}) custom-call(s32[1]{0:T(128)} %bitcast.7.place.refs_0_, f32[5]{0:T(128)} %stack.28.scalars, f32[128,4096]{1,0:T(8,128)} %shard_map.119.own, f32[128,4096]{1,0:T(8,128)} %collective-permute-done.31.other, f32[256,4096]{1,0:T(8,128)} %prestress.9, ...), custom_call_target="tpu_custom_call" | custom-call | tf_op jit(solution)/shard_map/pallas_call | solution.py:631
  636.5 61.2 %all_to_all.51.refs_2_ = f32[16,1,2,128,128]{4,3,2,1,0:T(8,128)} all-to-all(f32[16,1,2,128,128]{4,3,2,1,0:T(8,128)} %get-tuple-element.169), channel_id=1, replica_groups=mesh['side'=2,'slab'=16] {'slab'}, dimensions={0} | all-to-all | bytes 4194304 | tf_op jit(solution)/shard_map/all_to_all | solution.py:562
  702.9 25.0 %shard_map.121 = (f32[1,2,128,128]{3,2,1,0:T(8,128)}, f32[1,2,128,128]{3,2,1,0:T(8,128)}, f32[1,2,128,128]{3,2,1,0:T(8,128)}, f32[1,2,128,128]{3,2,1,0:T(8,128)}...) custom-call(s32[1]{0:T(128)} %bitcast.7.place.refs_0_, ...), custom_call_target="tpu_custom_call" | custom-call | tf_op jit(solution)/shard_map/pallas_call | solution.py:725
  728.0 16.0 %all-to-all-done.6.refs_2_ = f32[16,1,2,128,128]{4,3,2,1,0:T(8,128)} async-done(((f32[16,1,2,128,128]{4,3,2,1,0:T(8,128)}), f32[16,1,2,128,128]{4,3,2,1,0:T(8,128)}, u32[]{:S(2)}, u32[]{:S(2)}) %all-to-all-start.6) | async-done | bytes 2097184 | tf_op jit(solution)/shard_map/all_to_all | solution.py:562
  744.0 24.6 %shard_map.122 = (f32[16,1,2,128,128]{4,3,2,1,0:T(8,128)}, f32[16,2,2,80,128]{4,3,2,1,0:T(8,128)}, f32[16,2,2,48,128]{4,3,2,1,0:T(8,128)}) custom-call(s32[1]{0:T(128)} %bitcast.7.place.refs_0_, f32[16,2,2,128,128]{4,3,2,1,0:T(8,128)} %all-to-all-done.4.refs_1_, ...), custom_call_target="tpu_custom_call", output_to_operand_aliasing={{1}: (10, {}), {2}: (11, {})} | custom-call | tf_op jit(solution)/shard_map/pallas_call | solution.py:725
  768.5 58.5 %all_to_all.52.refs_16_ = f32[16,1,2,128,128]{4,3,2,1,0:T(8,128)} all-to-all(f32[16,1,2,128,128]{4,3,2,1,0:T(8,128)} %get-tuple-element.182), channel_id=1, replica_groups=mesh['side'=2,'slab'=16] {'slab'}, dimensions={0} | all-to-all | bytes 4194304 | tf_op jit(solution)/shard_map/all_to_all | solution.py:562
  838.4 44.7 %collective-permute-done.32.refs_1_ = f32[1,2,128,128]{3,2,1,0:T(8,128)} collective-permute-done((f32[1,2,128,128]{3,2,1,0:T(8,128)S(1)}, f32[1,2,128,128]{3,2,1,0:T(8,128)}, u32[]{:S(2)}, u32[]{:S(2)}) %collective-permute-start.32) | collective-permute-done | bytes 131104 | tf_op jit(solution)/shard_map/ppermute | solution.py:556
  884.2 17.0 %collective-permute-start.38 = (f32[1,2,128,128]{3,2,1,0:T(8,128)S(1)}, f32[1,2,128,128]{3,2,1,0:T(8,128)}, u32[]{:S(2)}, u32[]{:S(2)}) collective-permute-start(f32[1,2,128,128]{3,2,1,0:T(8,128)S(1)} %copy-done.18), channel_id=1, source_target_pairs={{0,7},{1,8},{2,9},{3,10},{4,11},{5,12},{6,13},{7,14},{8,15},{9,0},... | collective-permute-start | bytes 393224 | tf_op jit(solution)/shard_map/ppermute | solution.py:556
  953.1 47.0 %collective-permute-done.47.other = f32[128,4096]{1,0:T(8,128)} collective-permute-done((f32[128,4096]{1,0:T(8,128)}, f32[128,4096]{1,0:T(8,128)}, u32[]{:S(2)}, u32[]{:S(2)}) %collective-permute-start.47) | collective-permute-done | bytes 2097184 | tf_op jit(solution)/shard_map/ppermute | solution.py:25
  (175 shorter events, 309.6 us)
Async XLA Ops:
  12.1 48.5 %all-to-all-start = ((f32[16,1,2,128,128]{4,3,2,1,0:T(8,128)}), f32[16,1,2,128,128]{4,3,2,1,0:T(8,128)}, u32[]{:S(2)}, u32[]{:S(2)}) async-start(f32[16,1,2,128,128]{4,3,2,1,0:T(8,128)} %get-tuple-element.130), calls=%async_computation | async-start | bytes 4194304 | tf_op jit(solution)/shard_map/all_to_all | solution.py:562
  60.6 180.6 %all-to-all-start.1 = ((f32[16,1,2,128,128]{4,3,2,1,0:T(8,128)}), f32[16,1,2,128,128]{4,3,2,1,0:T(8,128)}, u32[]{:S(2)}, u32[]{:S(2)}) async-start(f32[16,1,2,128,128]{4,3,2,1,0:T(8,128)} %get-tuple-element.134), calls=%async_computation.1 | async-start | bytes 4194304 | tf_op jit(solution)/shard_map/all_to_all | solution.py:562
  90.3 78.8 %collective-permute-start.4 = (f32[2,2,128,128]{3,2,1,0:T(8,128)}, f32[2,2,128,128]{3,2,1,0:T(8,128)}, u32[]{:S(2)}, u32[]{:S(2)}) collective-permute-start(f32[2,2,128,128]{3,2,1,0:T(8,128)} %get-tuple-element.117), channel_id=1, source_target_pairs={{0,5},{1,6},{2,7},{3,8},{4,9},{5,10},{6,11},{7,12},{8,13},{9,14},{... | collective-permute-start | bytes 786440 | tf_op jit(solution)/shard_map/ppermute | solution.py:556
  116.8 53.5 %collective-permute-start.5 = (f32[2,2,128,128]{3,2,1,0:T(8,128)}, f32[2,2,128,128]{3,2,1,0:T(8,128)}, u32[]{:S(2)}, u32[]{:S(2)}) collective-permute-start(f32[2,2,128,128]{3,2,1,0:T(8,128)} %get-tuple-element.118), channel_id=1, source_target_pairs={{0,6},{1,7},{2,8},{3,9},{4,10},{5,11},{6,12},{7,13},{8,14},{9,15},... | collective-permute-start | bytes 786440 | tf_op jit(solution)/shard_map/ppermute | solution.py:556
  118.0 58.9 %collective-permute-start.6 = (f32[2,2,128,128]{3,2,1,0:T(8,128)}, f32[2,2,128,128]{3,2,1,0:T(8,128)}, u32[]{:S(2)}, u32[]{:S(2)}) collective-permute-start(f32[2,2,128,128]{3,2,1,0:T(8,128)} %get-tuple-element.119), channel_id=1, source_target_pairs={{0,7},{1,8},{2,9},{3,10},{4,11},{5,12},{6,13},{7,14},{8,15},{9,0},... | collective-permute-start | bytes 786440 | tf_op jit(solution)/shard_map/ppermute | solution.py:556
  130.9 58.5 %collective-permute-start.7 = (f32[2,2,128,128]{3,2,1,0:T(8,128)}, f32[2,2,128,128]{3,2,1,0:T(8,128)}, u32[]{:S(2)}, u32[]{:S(2)}) collective-permute-start(f32[2,2,128,128]{3,2,1,0:T(8,128)} %get-tuple-element.120), channel_id=1, source_target_pairs={{0,8},{1,9},{2,10},{3,11},{4,12},{5,13},{6,14},{7,15},{8,0},{9,1},... | collective-permute-start | bytes 786440 | tf_op jit(solution)/shard_map/ppermute | solution.py:556
  130.9 62.8 %collective-permute-start.8 = (f32[2,2,128,128]{3,2,1,0:T(8,128)}, f32[2,2,128,128]{3,2,1,0:T(8,128)}, u32[]{:S(2)}, u32[]{:S(2)}) collective-permute-start(f32[2,2,128,128]{3,2,1,0:T(8,128)} %get-tuple-element.121), channel_id=1, source_target_pairs={{0,9},{1,10},{2,11},{3,12},{4,13},{5,14},{6,15},{7,0},{8,1},{9,2},... | collective-permute-start | bytes 786440 | tf_op jit(solution)/shard_map/ppermute | solution.py:556
  319.1 229.5 %all-to-all-start.3 = ((f32[16,2,2,128,128]{4,3,2,1,0:T(8,128)}), f32[16,2,2,128,128]{4,3,2,1,0:T(8,128)}, u32[]{:S(2)}, u32[]{:S(2)}) async-start(f32[16,2,2,128,128]{4,3,2,1,0:T(8,128)} %get-tuple-element.143), calls=%async_computation.3 | async-start | bytes 8388608 | tf_op jit(solution)/shard_map/all_to_all | solution.py:562
  324.5 75.8 %collective-permute-start.15 = (f32[1,2,128,128]{3,2,1,0:T(8,128)S(1)}, f32[1,2,128,128]{3,2,1,0:T(8,128)}, u32[]{:S(2)}, u32[]{:S(2)}) collective-permute-start(f32[1,2,128,128]{3,2,1,0:T(8,128)S(1)} %copy-done.27), channel_id=1, source_target_pairs={{0,1},{1,2},{2,3},{3,4},{4,5},{5,6},{6,7},{7,8},{8,9},{9,10},{10,1... | collective-permute-start | bytes 393224 | tf_op jit(solution)/shard_map/ppermute | solution.py:556
  324.9 76.6 %collective-permute-start.16 = (f32[1,2,128,128]{3,2,1,0:T(8,128)S(1)}, f32[1,2,128,128]{3,2,1,0:T(8,128)}, u32[]{:S(2)}, u32[]{:S(2)}) collective-permute-start(f32[1,2,128,128]{3,2,1,0:T(8,128)S(1)} %copy-done.25), channel_id=1, source_target_pairs={{0,2},{1,3},{2,4},{3,5},{4,6},{5,7},{6,8},{7,9},{8,10},{9,11},{10,... | collective-permute-start | bytes 393224 | tf_op jit(solution)/shard_map/ppermute | solution.py:556
  326.5 100.3 %collective-permute-start.17 = (f32[1,2,128,128]{3,2,1,0:T(8,128)S(1)}, f32[1,2,128,128]{3,2,1,0:T(8,128)}, u32[]{:S(2)}, u32[]{:S(2)}) collective-permute-start(f32[1,2,128,128]{3,2,1,0:T(8,128)S(1)} %copy-done.23), channel_id=1, source_target_pairs={{0,3},{1,4},{2,5},{3,6},{4,7},{5,8},{6,9},{7,10},{8,11},{9,12},{10... | collective-permute-start | bytes 393224 | tf_op jit(solution)/shard_map/ppermute | solution.py:556
  328.8 98.8 %collective-permute-start.18 = (f32[1,2,128,128]{3,2,1,0:T(8,128)S(1)}, f32[1,2,128,128]{3,2,1,0:T(8,128)}, u32[]{:S(2)}, u32[]{:S(2)}) collective-permute-start(f32[1,2,128,128]{3,2,1,0:T(8,128)S(1)} %copy-done.21), channel_id=1, source_target_pairs={{0,4},{1,5},{2,6},{3,7},{4,8},{5,9},{6,10},{7,11},{8,12},{9,13},{1... | collective-permute-start | bytes 393224 | tf_op jit(solution)/shard_map/ppermute | solution.py:556
  330.3 112.6 %collective-permute-start.19 = (f32[1,2,128,128]{3,2,1,0:T(8,128)S(1)}, f32[1,2,128,128]{3,2,1,0:T(8,128)}, u32[]{:S(2)}, u32[]{:S(2)}) collective-permute-start(f32[1,2,128,128]{3,2,1,0:T(8,128)S(1)} %copy-done.19), channel_id=1, source_target_pairs={{0,5},{1,6},{2,7},{3,8},{4,9},{5,10},{6,11},{7,12},{8,13},{9,14},{... | collective-permute-start | bytes 393224 | tf_op jit(solution)/shard_map/ppermute | solution.py:556
  477.3 48.5 %collective-permute-start.30 = (f32[128,4096]{1,0:T(8,128)}, f32[128,4096]{1,0:T(8,128)}, u32[]{:S(2)}, u32[]{:S(2)}) collective-permute-start(f32[128,4096]{1,0:T(8,128)} %shard_map.117.own), channel_id=1, source_target_pairs={{0,16},{16,0},{1,17},{17,1},{2,18},{18,2},{3,19},{19,3},{4,20},{20... | collective-permute-start | bytes 6291464 | tf_op jit(solution)/shard_map/ppermute | solution.py:25
  548.6 87.9 %all-to-all-start.4 = ((f32[16,2,2,128,128]{4,3,2,1,0:T(8,128)}), f32[16,2,2,128,128]{4,3,2,1,0:T(8,128)}, u32[]{:S(2)}, u32[]{:S(2)}) async-start(f32[16,2,2,128,128]{4,3,2,1,0:T(8,128)} %get-tuple-element.163), calls=%async_computation.4 | async-start | bytes 8388608 | tf_op jit(solution)/shard_map/all_to_all | solution.py:562
  564.8 48.1 %collective-permute-start.31 = (f32[128,4096]{1,0:T(8,128)}, f32[128,4096]{1,0:T(8,128)}, u32[]{:S(2)}, u32[]{:S(2)}) collective-permute-start(f32[128,4096]{1,0:T(8,128)} %shard_map.119.own), channel_id=1, source_target_pairs={{0,16},{16,0},{1,17},{17,1},{2,18},{18,2},{3,19},{19,3},{4,20},{20... | collective-permute-start | bytes 6291464 | tf_op jit(solution)/shard_map/ppermute | solution.py:25
  697.7 46.2 %all-to-all-start.6 = ((f32[16,1,2,128,128]{4,3,2,1,0:T(8,128)}), f32[16,1,2,128,128]{4,3,2,1,0:T(8,128)}, u32[]{:S(2)}, u32[]{:S(2)}) async-start(f32[16,1,2,128,128]{4,3,2,1,0:T(8,128)} %get-tuple-element.172), calls=%async_computation.6 | async-start | bytes 4194304 | tf_op jit(solution)/shard_map/all_to_all | solution.py:562
  827.1 173.0 %all-to-all-start.8 = ((f32[16,2,2,80,128]{4,3,2,1,0:T(8,128)}), f32[16,2,2,80,128]{4,3,2,1,0:T(8,128)}, u32[]{:S(2)}, u32[]{:S(2)}) async-start(f32[16,2,2,80,128]{4,3,2,1,0:T(8,128)} %get-tuple-element.185), calls=%async_computation.8 | async-start | bytes 5242880 | tf_op jit(solution)/shard_map/all_to_all | solution.py:562
  832.5 50.5 %collective-permute-start.32 = (f32[1,2,128,128]{3,2,1,0:T(8,128)S(1)}, f32[1,2,128,128]{3,2,1,0:T(8,128)}, u32[]{:S(2)}, u32[]{:S(2)}) collective-permute-start(f32[1,2,128,128]{3,2,1,0:T(8,128)S(1)} %copy-done.29), channel_id=1, source_target_pairs={{0,1},{1,2},{2,3},{3,4},{4,5},{5,6},{6,7},{7,8},{8,9},{9,10},{10,1... | collective-permute-start | bytes 393224 | tf_op jit(solution)/shard_map/ppermute | solution.py:556
  832.9 51.3 %collective-permute-start.33 = (f32[1,2,128,128]{3,2,1,0:T(8,128)S(1)}, f32[1,2,128,128]{3,2,1,0:T(8,128)}, u32[]{:S(2)}, u32[]{:S(2)}) collective-permute-start(f32[1,2,128,128]{3,2,1,0:T(8,128)S(1)} %copy-done.28), channel_id=1, source_target_pairs={{0,2},{1,3},{2,4},{3,5},{4,6},{5,7},{6,8},{7,9},{8,10},{9,11},{10,... | collective-permute-start | bytes 393224 | tf_op jit(solution)/shard_map/ppermute | solution.py:556
  834.5 66.7 %collective-permute-start.34 = (f32[1,2,128,128]{3,2,1,0:T(8,128)S(1)}, f32[1,2,128,128]{3,2,1,0:T(8,128)}, u32[]{:S(2)}, u32[]{:S(2)}) collective-permute-start(f32[1,2,128,128]{3,2,1,0:T(8,128)S(1)} %copy-done.26), channel_id=1, source_target_pairs={{0,3},{1,4},{2,5},{3,6},{4,7},{5,8},{6,9},{7,10},{8,11},{9,12},{10... | collective-permute-start | bytes 393224 | tf_op jit(solution)/shard_map/ppermute | solution.py:556
  836.8 65.2 %collective-permute-start.35 = (f32[1,2,128,128]{3,2,1,0:T(8,128)S(1)}, f32[1,2,128,128]{3,2,1,0:T(8,128)}, u32[]{:S(2)}, u32[]{:S(2)}) collective-permute-start(f32[1,2,128,128]{3,2,1,0:T(8,128)S(1)} %copy-done.24), channel_id=1, source_target_pairs={{0,4},{1,5},{2,6},{3,7},{4,8},{5,9},{6,10},{7,11},{8,12},{9,13},{1... | collective-permute-start | bytes 393224 | tf_op jit(solution)/shard_map/ppermute | solution.py:556
  838.2 78.9 %collective-permute-start.36 = (f32[1,2,128,128]{3,2,1,0:T(8,128)S(1)}, f32[1,2,128,128]{3,2,1,0:T(8,128)}, u32[]{:S(2)}, u32[]{:S(2)}) collective-permute-start(f32[1,2,128,128]{3,2,1,0:T(8,128)S(1)} %copy-done.22), channel_id=1, source_target_pairs={{0,5},{1,6},{2,7},{3,8},{4,9},{5,10},{6,11},{7,12},{8,13},{9,14},{... | collective-permute-start | bytes 393224 | tf_op jit(solution)/shard_map/ppermute | solution.py:556
  951.7 48.5 %collective-permute-start.47 = (f32[128,4096]{1,0:T(8,128)}, f32[128,4096]{1,0:T(8,128)}, u32[]{:S(2)}, u32[]{:S(2)}) collective-permute-start(f32[128,4096]{1,0:T(8,128)} %shard_map.123.own), channel_id=1, source_target_pairs={{0,16},{16,0},{1,17},{17,1},{2,18},{18,2},{3,19},{19,3},{4,20},{20... | collective-permute-start | bytes 6291464 | tf_op jit(solution)/shard_map/ppermute | solution.py:25
  (63 other events, 2922.8 us)

commit v5 on v4

--- a/solution.py
+++ b/solution.py
@@ -255,10 +255,6 @@
     )
 
 
-def picked(refs, half):
-    return (refs[0], half) if len(refs) == 1 else (refs[half], 0)
-
-
 def store_ring(place, spread, both, outs, pair, lead, first_part, row):
     inner = both.shape[0] // 2
     per = inner // RADIX
@@ -290,15 +286,16 @@
 
     def wave(pair, carry):
         both = product(table, held, pair, 0)
-        if len(outs) == RADIX:
-            for half in range(2):
-                store_ring(place, spread, both, outs, pair, half, 0, half * 8)
-            return carry
-        slabs, halves = outs[0].shape[0], 2
+        if len(outs) >= RADIX:
+            for half in range(outs[0].shape[0]):
+                store_ring(place, spread, both, outs[:RADIX], pair, half, 0, half * 8)
+            if len(outs) == RADIX:
+                return carry
+        slabs, halves = outs[-1].shape[0], 2
         per = inner // slabs // halves
         for slab in range(slabs):
-            for half in range(halves):
-                out, spot = picked(outs, half)
+            for half in range(halves - outs[-1].shape[1], halves):
+                out, spot = outs[-1], half - halves + outs[-1].shape[1]
                 for part in range(2):
                     first = part * inner + (slab * halves + half) * per
                     for odd in range(2):
@@ -399,40 +396,38 @@
     lax.fori_loop(0, now.shape[2] // 256, group, 0)
 
 
-def spectral_kernel(count, has_past, half, pieces, *refs):
-    place, ring, block = refs[0], refs[1 : count + 1], refs[count + 1]
-    kernel_now, past_sum, table, twist, twist_ring = refs[count + 2 : count + 7]
-    rest = list(refs[count + 7 :])
+def spectral_kernel(counts, has_past, half, pieces, *refs):
+    count = 1 + sum(counts)
+    place, arrived = refs[0], (refs[1 : 1 + counts[0]], refs[1 + counts[0] : count])
+    kernel_now, past_sum, table, twist, twist_ring = refs[count : count + 5]
+    rest = list(refs[count + 5 :])
     if has_past:
         kernel_past, spec_past = rest.pop(0), rest.pop(0)
         spec_out = None
     if half > 0:
         rest = rest[len(pieces) - 1 :]
-    ring_out = []
-    if half == 0:
-        ring_out, rest = rest[:RADIX], rest[RADIX:]
-        pieces = pieces[1:]
+    ring_out, rest = rest[:RADIX], rest[RADIX:]
+    pieces = pieces[1:]
     outs, rest = rest[: len(pieces)], rest[len(pieces) :]
     if not has_past:
         spec_out = rest.pop(0)
     held, turned, total, spread = rest
-    rows = block.shape[3]
+    rows = 128
     inner = RADIX * 16
     length = total.shape[2]
 
     def group(g, carry):
         at = pl.ds(pl.multiple_of(g * 16, 16), 16)
-        if count == 1:
-            values = [(ring[0][n, 0, 0, at, :], ring[0][n, 0, 1, at, :]) for n in range(RADIX)]
-            sign, turn = -1, twist
-        else:
-            values = [(ring[n][0, 0, at, :], ring[n][0, 1, at, :]) for n in range(RADIX)]
-            sign, turn = 1, twist_ring
-        for k, value in enumerate(sixteen(values, sign)):
-            store_split(held, k, g, 0, *twisted(value, turn, k, 0, -1))
-        values = [(block[n, 0, 0, at, :], block[n, 0, 1, at, :]) for n in range(RADIX)]
-        for k, value in enumerate(sixteen(values, -1)):
-            store_split(held, k, g, 128, *twisted(value, twist, k, 128, -1))
+        for chunk, tile in enumerate(arrived):
+            if len(tile) == 1:
+                values = [(tile[0][n, 0, 0, at, :], tile[0][n, 0, 1, at, :]) for n in range(RADIX)]
+                sign, turn = -1, twist
+            else:
+                values = [(tile[n][0, 0, at, :], tile[n][0, 1, at, :]) for n in range(RADIX)]
+                sign, turn = 1, twist_ring
+            lane = chunk * 128
+            for k, value in enumerate(sixteen(values, sign)):
+                store_split(held, k, g, lane, *twisted(value, turn, k, lane, -1))
         return carry
 
     lax.fori_loop(0, rows // 16, group, 0)
@@ -481,8 +476,7 @@
 
     def wave_back(pair, carry):
         both = product(table, held, pair, 0)
-        if half == 0:
-            store_ring(place, spread, both, ring_out, pair, 0, 1, 0)
+        store_ring(place, spread, both, ring_out, pair, 0, 1, 0)
         slabs = outs[0].shape[0]
         per = inner // slabs
         for slab in range(slabs):
@@ -501,7 +495,7 @@
 
 def inverse_kernel(count, *refs):
     blocks = refs[:count]
-    ring = blocks[:RADIX] if count > RADIX else None
+    ring = blocks if count > 1 else None
     table, twist, twist_ring, out, held, turned = refs[count:]
     rows, length = out.shape
     inner = length // RADIX
@@ -510,13 +504,13 @@
         at = pl.ds(pl.multiple_of(g * 16, 16), 16)
         for half in range(inner // 128):
             sign, turn = 1, twist
-            if ring is not None and half == 0:
-                values = [(ring[n][0, 0, at, :], ring[n][0, 1, at, :]) for n in range(RADIX)]
+            if ring is not None:
+                tile = ring[half * RADIX : half * RADIX + RADIX]
+                values = [(tile[n][0, 0, at, :], tile[n][0, 1, at, :]) for n in range(RADIX)]
                 sign, turn = -1, twist_ring
             else:
-                block = blocks[-1]
-                spot = 0 if ring is not None else half
-                values = [(block[n, spot, 0, at, :], block[n, spot, 1, at, :]) for n in range(RADIX)]
+                block = blocks[0]
+                values = [(block[n, half, 0, at, :], block[n, half, 1, at, :]) for n in range(RADIX)]
             for k, value in enumerate(sixteen(values, sign)):
                 real, imag = twisted(value, turn, k, half * 128, 1)
                 store_split(held, k, g, half * 128, imag, real)
@@ -550,12 +544,27 @@
 SCALARS = pl.BlockSpec(memory_space=pltpu.SMEM)
 
 
+def is_light(distance, count):
+    return min(distance, count - distance) * 3 <= count
+
+
 def ringed(blocks):
     count = lax.axis_size("slab")
-    return [blocks[0]] + [
-        lax.ppermute(blocks[n], "slab", [(source, (source + n) % count) for source in range(count)])
-        for n in range(1, count)
-    ]
+    moved = [blocks[0]]
+    for n in range(1, count):
+        pairs = [(source, (source + n) % count) for source in range(count)]
+        moved.append(lax.ppermute(blocks[n], "slab", pairs))
+    return moved
+
+
+def after_light(arrived, then):
+    count = len(arrived)
+    light = [n for n in range(1, count) if is_light(n, count)]
+    held = lax.optimization_barrier((tuple(arrived[n] for n in light), *then))
+    arrived = list(arrived)
+    for n, value in zip(light, held[0]):
+        arrived[n] = value
+    return (arrived, *held[1:])
 
 
 def exchanged(value):
@@ -596,7 +605,9 @@
         return [jax.ShapeDtypeStruct((count, 2, 128, 128), f32)] * slabs
 
     def forward_shapes(chunk, ring):
-        shapes = ring_tiles(halves) if ring else tiles([[halves], [1, 1]][chunk])
+        shapes = ring_tiles(1) + tiles([1])
+        if chunk == 0:
+            shapes = ring_tiles(halves) if ring else tiles([halves])
         return shapes, [whole_spec(shape) for shape in shapes]
 
     me = lax.axis_index("slab")
@@ -698,19 +709,23 @@
         ]
         sum_spec = pl.BlockSpec((2, 128, length), lambda *_: (0, half, 0))
         spec_spec = pl.BlockSpec((2, 128, length), lambda *_: (0, 0, 0))
-        ring_spec = pl.BlockSpec((1, 2, 128, 128), lambda *_: (half, 0, 0, 0))
-        operands = [place, *ring, near, kernel, past_sum, table, twist, twist_ring]
-        in_specs = [SCALARS] + ([ring_spec] * slabs if len(ring) > 1 else [block(ring[0])])
-        in_specs += [block(near), lag_spec[0], sum_spec]
+
+        def arrived(tile):
+            if len(tile) == 1:
+                return [block(tile[0])]
+            spot = half if tile[0].shape[0] == halves else 0
+            return [pl.BlockSpec((1, 2, 128, 128), lambda *_: (spot, 0, 0, 0))] * slabs
+
+        operands = [place, *ring, *near, kernel, past_sum, table, twist, twist_ring]
+        in_specs = [SCALARS] + arrived(ring) + arrived(near) + [lag_spec[0], sum_spec]
         in_specs += [whole_spec(table), whole_spec(twist), whole_spec(twist_ring)]
-        out_shape = tiles([1]) if half else []
+        out_shape = []
         for row, count in pieces[1:]:
             out_shape += tiles([halves], count)
         out_specs = [block(shape) for shape in out_shape]
-        if half == 0:
-            shapes = ring_tiles(1)
-            out_shape = shapes + out_shape
-            out_specs = [whole_spec(shape) for shape in shapes] + out_specs
+        shapes = ring_tiles(1)
+        out_shape = shapes + out_shape
+        out_specs = [whole_spec(shape) for shape in shapes] + out_specs
         if past is not None:
             operands += [kernel, past]
             in_specs += [lag_spec[1], spec_spec]
@@ -719,11 +734,13 @@
             out_specs.append(spec_spec)
         aliases = {}
         if before is not None:
-            aliases = {len(operands) + n: 1 + n for n in range(len(before))}
+            aliases = {len(operands) + n: slabs + n for n in range(len(before))}
             operands += before
             in_specs += [pl.BlockSpec(memory_space=pl.ANY)] * len(before)
         return pl.pallas_call(
-            functools.partial(spectral_kernel, len(ring), past is not None, half, pieces),
+            functools.partial(
+                spectral_kernel, (len(ring), len(near)), past is not None, half, pieces
+            ),
             input_output_aliases=aliases,
             out_shape=out_shape,
             grid=(1,),
@@ -739,7 +756,7 @@
         )(*operands)
 
     def inverse(*blocks):
-        rows = blocks[-1].shape[3]
+        rows = blocks[0].shape[-2]
         return pl.pallas_call(
             functools.partial(inverse_kernel, len(blocks)),
             out_shape=jax.ShapeDtypeStruct((rows, length), f32),
@@ -773,11 +790,10 @@
         else:
             own = inverse(waiting)
             sent[1], states[1] = middle(1, own, swapped(own, "side", 0), states[1])
-            ring, sent[1], states[1] = hold((ring, sent[1], states[1]))
-        near = exchanged(sent[1][0])
+        near = ringed(sent[1][:slabs])
         if step_index == 0:
             sums = past_sums()
-        near, far, sums = hold((near, sent[1][1], sums))
+        near, far, sums = after_light(near, (sent[1][slabs], sums))
         far = exchanged(far)
         outs = spectral(0, ring, near, sums[step_index], past[0], pieces, None)
         if step_index == 0:
@@ -785,14 +801,14 @@
         late = outs[slabs : slabs + len(pieces) - 1]
         back = ringed(outs[:slabs])
         far, late = hold((far, list(late)))
-        outs = spectral(1, ring, far, sums[step_index], past[1], pieces, late)
+        outs = spectral(1, ring, [far], sums[step_index], past[1], pieces, late)
         if step_index == 0:
             past[1] = outs[-1]
-        more, late = outs[0], outs[1 : len(pieces)]
-        more = exchanged(more)
-        more, late = hold((more, list(late)))
+        late = outs[slabs : slabs + len(pieces) - 1]
+        more = ringed(outs[:slabs])
+        more, late = after_light(more, (list(late),))
         waiting = exchanged(late[0])
-        own = inverse(*back, more)
+        own = inverse(*back, *more)
         other = swapped(own, "side", 0)
         if not last:
             sent[0], states[0] = middle(0, own, other, states[0])

time: 1080 us -> 1120 us (1.037)
  blocking collectives: 173 us -> 0 us
  waiting for transfers between devices: 389 us -> 522 us
  starting transfers between devices: 227 us -> 316 us
    all_to_all x3 -> x0, blocking collectives: 173 us -> none  [exchanged(): lax.all_to_all(value, 'slab', split_axis=0, concat_axis=0, tiled=True)]
    ppermute x45 -> x105, waiting for transfers between devices: 205 us -> 371 us  [ringed(): moved.append(lax.ppermute(blocks[n], 'slab', pairs))]
    ppermute x45 -> x105, starting transfers between devices: 175 us -> 263 us  [ringed(): moved.append(lax.ppermute(blocks[n], 'slab', pairs))]
    all_to_all x7 -> x6, waiting for transfers between devices: 40.4 us -> 8.11 us  [exchanged(): lax.all_to_all(value, 'slab', split_axis=0, concat_axis=0, tiled=True)]
    all_to_all x7 -> x6, starting transfers between devices: 44 us -> 44.9 us  [exchanged(): lax.all_to_all(value, 'slab', split_axis=0, concat_axis=0, tiled=True)]
  transfers between devices with their start and end apart: 57 -> 116, of which waited for: 25 -> 44; matrix products, arithmetic and copies ran while one was open for 0% -> 0% of each run, Pallas kernels for 19% -> 18%
where the time goes in v5:
time: 1120 us
  waiting for transfers between devices  522 us (47%)
  starting transfers between devices  316 us (28%)
  Pallas kernels  274 us (24%)
    ppermute x105, waiting for transfers between devices, ringed(): moved.append(lax.ppermute(blocks[n], 'slab', pairs))  371 us
    ppermute x105, starting transfers between devices, ringed(): moved.append(lax.ppermute(blocks[n], 'slab', pairs))  263 us
    ppermute x5, waiting for transfers between devices, swapped(): return lax.ppermute(value, axis, pairs)  143 us
    pallas_call x4, Pallas kernels, spectral(): pl.pallas_call(functools.partial(spectral_kernel, (len(ring), len(near)),...  99.3 us
    pallas_call x5, Pallas kernels, inverse(): pl.pallas_call(functools.partial(inverse_kernel, len(blocks)), out_shape=...  52.7 us
    pallas_call x2, Pallas kernels, middle(): pl.pallas_call(middle_kernel, out_shape=shapes + [rows_shape], grid=(1,),...  46.3 us
    all_to_all x6, starting transfers between devices, exchanged(): lax.all_to_all(value, 'slab', split_axis=0, concat_axis=0, tiled=True)  44.9 us
    pallas_call x3, Pallas kernels, end(): pl.pallas_call(end_kernel, out_shape=(jax.ShapeDtypeStruct((1, rows_dev,...  27 us
  transfers between devices with their start and end apart: 116, of which 44 were waited for; matrix products, arithmetic and copies ran while one was open for 0% of the time, Pallas kernels for 18%

profile of v5, /device:TPU:0, one launch (start us, length us, event | category | flops | bytes accessed | tf_op | source)
XLA Modules:
  0.0 1121.0 jit_solution(15948419481742878288)
XLA Ops:
  0.6 11.6 %shard_map.113 = (f32[1,2,128,128]{3,2,1,0:T(8,128)}, f32[1,2,128,128]{3,2,1,0:T(8,128)}, f32[1,2,128,128]{3,2,1,0:T(8,128)}, f32[1,2,128,128]{3,2,1,0:T(8,128)}...) custom-call(s32[1]{0:T(128)} %bitcast.7.place.refs_0_, ...), custom_call_target="tpu_custom_call" | custom-call | tf_op jit(solution)/shard_map/pallas_call | solution.py:625
  34.6 24.8 %shard_map.114 = (f32[2,256,4096]{2,1,0:T(8,128)}, f32[2,256,4096]{2,1,0:T(8,128)}) custom-call(bf16[1,9,256,4096]{3,2,1,0:T(8,128)(2,1)} %refs_8_.1, bf16[1,8,2,256,4096]{4,3,2,1,0:T(8,128)(2,1)} %history.1), custom_call_target="tpu_custom_call" | custom-call | tf_op jit(solution)/shard_map/pallas_call | solution.py:688
  77.8 12.7 %shard_map.112 = (f32[2,2,128,128]{3,2,1,0:T(8,128)}, f32[2,2,128,128]{3,2,1,0:T(8,128)}, f32[2,2,128,128]{3,2,1,0:T(8,128)}, f32[2,2,128,128]{3,2,1,0:T(8,128)}...) custom-call(s32[1]{0:T(128)} %bitcast.7.place.refs_0_, ...), custom_call_target="tpu_custom_call" | custom-call | tf_op jit(solution)/shard_map/pallas_call | solution.py:625
  90.5 41.5 %collective-permute-done.25.refs_23_ = f32[1,2,128,128]{3,2,1,0:T(8,128)} collective-permute-done((f32[1,2,128,128]{3,2,1,0:T(8,128)}, f32[1,2,128,128]{3,2,1,0:T(8,128)}, u32[]{:S(2)}, u32[]{:S(2)}) %collective-permute-start.25) | collective-permute-done | bytes 131104 | tf_op jit(solution)/shard_map/ppermute | solution.py:556
  136.8 19.9 %collective-permute-start.3 = (f32[2,2,128,128]{3,2,1,0:T(8,128)}, f32[2,2,128,128]{3,2,1,0:T(8,128)}, u32[]{:S(2)}, u32[]{:S(2)}) collective-permute-start(f32[2,2,128,128]{3,2,1,0:T(8,128)} %get-tuple-element.223), channel_id=1, source_target_pairs={{0,4},{1,5},{2,6},{3,7},{4,8},{5,9},{6,10},{7,11},{8,12},{9,13},{1... | collective-permute-start | bytes 786440 | tf_op jit(solution)/shard_map/ppermute | solution.py:556
  163.8 31.7 %collective-permute-done.4.refs_6_ = f32[2,2,128,128]{3,2,1,0:T(8,128)} collective-permute-done((f32[2,2,128,128]{3,2,1,0:T(8,128)}, f32[2,2,128,128]{3,2,1,0:T(8,128)}, u32[]{:S(2)}, u32[]{:S(2)}) %collective-permute-start.4) | collective-permute-done | bytes 262176 | tf_op jit(solution)/shard_map/ppermute | solution.py:556
  243.4 24.5 %shard_map.115 = (f32[1,2,128,128]{3,2,1,0:T(8,128)}, f32[1,2,128,128]{3,2,1,0:T(8,128)}, f32[1,2,128,128]{3,2,1,0:T(8,128)}, f32[1,2,128,128]{3,2,1,0:T(8,128)}...) custom-call(s32[1]{0:T(128)} %bitcast.7.place.refs_0_, ...), custom_call_target="tpu_custom_call" | custom-call | tf_op jit(solution)/shard_map/pallas_call | solution.py:740
  267.9 24.7 %shard_map.116 = (f32[1,2,128,128]{3,2,1,0:T(8,128)}, f32[1,2,128,128]{3,2,1,0:T(8,128)}, f32[1,2,128,128]{3,2,1,0:T(8,128)}, f32[1,2,128,128]{3,2,1,0:T(8,128)}...) custom-call(s32[1]{0:T(128)} %bitcast.7.place.refs_0_, ...), custom_call_target="tpu_custom_call", output_to_operand_aliasing={{16}: (23, {})} | custom-call | tf_op jit(solution)/shard_map/pallas_call | solution.py:740
  331.6 69.9 %collective-permute-done.40.refs_1_ = f32[1,2,128,128]{3,2,1,0:T(8,128)} collective-permute-done((f32[1,2,128,128]{3,2,1,0:T(8,128)S(1)}, f32[1,2,128,128]{3,2,1,0:T(8,128)}, u32[]{:S(2)}, u32[]{:S(2)}) %collective-permute-start.40) | collective-permute-done | bytes 131104 | tf_op jit(solution)/shard_map/ppermute | solution.py:556
  402.7 25.4 %collective-permute-start.46 = (f32[1,2,128,128]{3,2,1,0:T(8,128)S(1)}, f32[1,2,128,128]{3,2,1,0:T(8,128)}, u32[]{:S(2)}, u32[]{:S(2)}) collective-permute-start(f32[1,2,128,128]{3,2,1,0:T(8,128)S(1)} %copy-done.26), channel_id=1, source_target_pairs={{0,7},{1,8},{2,9},{3,10},{4,11},{5,12},{6,13},{7,14},{8,15},{9,0},... | collective-permute-start | bytes 393224 | tf_op jit(solution)/shard_map/ppermute | solution.py:556
  431.1 13.0 %collective-permute-done.44.refs_5_ = f32[1,2,128,128]{3,2,1,0:T(8,128)} collective-permute-done((f32[1,2,128,128]{3,2,1,0:T(8,128)S(1)}, f32[1,2,128,128]{3,2,1,0:T(8,128)}, u32[]{:S(2)}, u32[]{:S(2)}) %collective-permute-start.44) | collective-permute-done | bytes 131104 | tf_op jit(solution)/shard_map/ppermute | solution.py:556
  486.1 11.5 %shard_map.117.own = f32[128,4096]{1,0:T(8,128)} custom-call(f32[1,2,128,128]{3,2,1,0:T(8,128)} %get-tuple-element.299.refs_0_, f32[1,2,128,128]{3,2,1,0:T(8,128)} %collective-permute-done.40.refs_1_, f32[1,2,128,128]{3,2,1,0:T(8,128)} %collective-permute-done.41.refs_2_, f32[1,2,128,128]{3,2,1,0:T(8,128)} %collective-permute-done.42.refs_3_, ...), custom_call_target="tpu_custom_call" | custom-call | tf_op jit(solution)/shard_map/pallas_call | solution.py:760
  506.0 38.9 %collective-permute-done.60.other = f32[128,4096]{1,0:T(8,128)} collective-permute-done((f32[128,4096]{1,0:T(8,128)}, f32[128,4096]{1,0:T(8,128)}, u32[]{:S(2)}, u32[]{:S(2)}) %collective-permute-start.60) | collective-permute-done | bytes 2097184 | tf_op jit(solution)/shard_map/ppermute | solution.py:25
  544.9 22.8 %shard_map.118 = (f32[16,2,2,128,128]{4,3,2,1,0:T(8,128)}, f32[128,4096]{1,0:T(8,128)}) custom-call(s32[1]{0:T(128)} %bitcast.7.place.refs_0_, f32[5]{0:T(128)} %stack.28.scalars, f32[128,4096]{1,0:T(8,128)} %shard_map.117.own, f32[128,4096]{1,0:T(8,128)} %collective-permute-done.60.other, f32[256,4096]{1,0:T(8,128)} %prestress.9, f32[256,4096]{1,0:T(8,128)} %strength.9, ...), custom_call_target="tpu_custom_call" | custom-call | tf_op jit(solution)/shard_map/pallas_call | solution.py:642
  567.7 12.1 %all-to-all-start.2 = ((f32[16,2,2,128,128]{4,3,2,1,0:T(8,128)}), f32[16,2,2,128,128]{4,3,2,1,0:T(8,128)}, u32[]{:S(2)}, u32[]{:S(2)}) async-start(f32[16,2,2,128,128]{4,3,2,1,0:T(8,128)} %get-tuple-element.333), calls=%async_computation.2 | async-start | bytes 8388608 | tf_op jit(solution)/shard_map/all_to_all | solution.py:571
  592.8 46.7 %collective-permute-done.61.other = f32[128,4096]{1,0:T(8,128)} collective-permute-done((f32[128,4096]{1,0:T(8,128)}, f32[128,4096]{1,0:T(8,128)}, u32[]{:S(2)}, u32[]{:S(2)}) %collective-permute-start.61) | collective-permute-done | bytes 2097184 | tf_op jit(solution)/shard_map/ppermute | solution.py:25
  639.4 23.5 %shard_map.120 = (f32[1,2,128,128]{3,2,1,0:T(8,128)}, f32[1,2,128,128]{3,2,1,0:T(8,128)}, f32[1,2,128,128]{3,2,1,0:T(8,128)}, f32[1,2,128,128]{3,2,1,0:T(8,128)}...) custom-call(s32[1]{0:T(128)} %bitcast.7.place.refs_0_, ...), custom_call_target="tpu_custom_call" | custom-call | tf_op jit(solution)/shard_map/pallas_call | solution.py:642
  711.9 54.2 %collective-permute-done.72.refs_8_ = f32[1,2,128,128]{3,2,1,0:T(8,128)} collective-permute-done((f32[1,2,128,128]{3,2,1,0:T(8,128)S(1)}, f32[1,2,128,128]{3,2,1,0:T(8,128)}, u32[]{:S(2)}, u32[]{:S(2)}) %collective-permute-start.72) | collective-permute-done | bytes 131104 | tf_op jit(solution)/shard_map/ppermute | solution.py:556
  769.4 24.9 %shard_map.121 = (f32[1,2,128,128]{3,2,1,0:T(8,128)}, f32[1,2,128,128]{3,2,1,0:T(8,128)}, f32[1,2,128,128]{3,2,1,0:T(8,128)}, f32[1,2,128,128]{3,2,1,0:T(8,128)}...) custom-call(s32[1]{0:T(128)} %bitcast.7.place.refs_0_, ...), custom_call_target="tpu_custom_call" | custom-call | tf_op jit(solution)/shard_map/pallas_call | solution.py:740
  794.3 25.1 %shard_map.122 = (f32[1,2,128,128]{3,2,1,0:T(8,128)}, f32[1,2,128,128]{3,2,1,0:T(8,128)}, f32[1,2,128,128]{3,2,1,0:T(8,128)}, f32[1,2,128,128]{3,2,1,0:T(8,128)}...) custom-call(s32[1]{0:T(128)} %bitcast.7.place.refs_0_, ...), custom_call_target="tpu_custom_call", output_to_operand_aliasing={{16}: (10, {}), {17}: (11, {})} | custom-call | tf_op jit(solution)/shard_map/pallas_call | solution.py:740
  865.0 65.4 %collective-permute-done.102.refs_22_ = f32[1,2,128,128]{3,2,1,0:T(8,128)} collective-permute-done((f32[1,2,128,128]{3,2,1,0:T(8,128)S(1)}, f32[1,2,128,128]{3,2,1,0:T(8,128)}, u32[]{:S(2)}, u32[]{:S(2)}) %collective-permute-start.102) | collective-permute-done | bytes 131104 | tf_op jit(solution)/shard_map/ppermute | solution.py:556
  989.6 11.6 %shard_map.123.own = f32[128,4096]{1,0:T(8,128)} custom-call(f32[1,2,128,128]{3,2,1,0:T(8,128)} %get-tuple-element.385.refs_0_, f32[1,2,128,128]{3,2,1,0:T(8,128)} %collective-permute-done.87.refs_1_, f32[1,2,128,128]{3,2,1,0:T(8,128)} %collective-permute-done.88.refs_2_, f32[1,2,128,128]{3,2,1,0:T(8,128)} %collective-permute-done.89.refs_3_, ...), custom_call_target="tpu_custom_call" | custom-call | tf_op jit(solution)/shard_map/pallas_call | solution.py:760
  1002.7 47.0 %collective-permute-done.107.other = f32[128,4096]{1,0:T(8,128)} collective-permute-done((f32[128,4096]{1,0:T(8,128)}, f32[128,4096]{1,0:T(8,128)}, u32[]{:S(2)}, u32[]{:S(2)}) %collective-permute-start.107) | collective-permute-done | bytes 2097184 | tf_op jit(solution)/shard_map/ppermute | solution.py:25
  1065.4 12.5 %shard_map.125 = (f32[1,256,4096]{2,1,0:T(8,128)}, f32[256,4096]{1,0:T(8,128)}, f32[256,4096]{1,0:T(8,128)}) custom-call(f32[5]{0:T(128)} %stack.28.scalars, f32[128,4096]{1,0:T(8,128)} %shard_map.123.own, f32[128,4096]{1,0:T(8,128)} %collective-permute-done.107.other, f32[256,4096]{1,0:T(8,128)} %prestress.9, f32[256,4096]{1,0:T(8,128)} %strength.9, ...), custom_call_target="tpu_custom_call" | custom-call | tf_op jit(solution)/shard_map/pallas_call | solution.py:674
  (320 shorter events, 418.7 us)
Async XLA Ops:
  59.4 208.5 %all-to-all-start = ((f32[16,1,2,128,128]{4,3,2,1,0:T(8,128)}), f32[16,1,2,128,128]{4,3,2,1,0:T(8,128)}, u32[]{:S(2)}, u32[]{:S(2)}) async-start(f32[16,1,2,128,128]{4,3,2,1,0:T(8,128)} %get-tuple-element.265), calls=%async_computation | async-start | bytes 4194304 | tf_op jit(solution)/shard_map/all_to_all | solution.py:571
  68.8 63.2 %collective-permute-start.25 = (f32[1,2,128,128]{3,2,1,0:T(8,128)}, f32[1,2,128,128]{3,2,1,0:T(8,128)}, u32[]{:S(2)}, u32[]{:S(2)}) collective-permute-start(f32[1,2,128,128]{3,2,1,0:T(8,128)} %get-tuple-element.272), channel_id=1, source_target_pairs={{0,6},{1,7},{2,8},{3,9},{4,10},{5,11},{6,12},{7,13},{8,14},{9,15},... | collective-permute-start | bytes 393224 | tf_op jit(solution)/shard_map/ppermute | solution.py:556
  71.6 62.6 %collective-permute-start.26 = (f32[1,2,128,128]{3,2,1,0:T(8,128)}, f32[1,2,128,128]{3,2,1,0:T(8,128)}, u32[]{:S(2)}, u32[]{:S(2)}) collective-permute-start(f32[1,2,128,128]{3,2,1,0:T(8,128)} %get-tuple-element.273), channel_id=1, source_target_pairs={{0,7},{1,8},{2,9},{3,10},{4,11},{5,12},{6,13},{7,14},{8,15},{9,0},... | collective-permute-start | bytes 393224 | tf_op jit(solution)/shard_map/ppermute | solution.py:556
  73.4 61.9 %collective-permute-start.27 = (f32[1,2,128,128]{3,2,1,0:T(8,128)}, f32[1,2,128,128]{3,2,1,0:T(8,128)}, u32[]{:S(2)}, u32[]{:S(2)}) collective-permute-start(f32[1,2,128,128]{3,2,1,0:T(8,128)} %get-tuple-element.274), channel_id=1, source_target_pairs={{0,8},{1,9},{2,10},{3,11},{4,12},{5,13},{6,14},{7,15},{8,0},{9,1},... | collective-permute-start | bytes 393224 | tf_op jit(solution)/shard_map/ppermute | solution.py:556
  74.0 62.9 %collective-permute-start.28 = (f32[1,2,128,128]{3,2,1,0:T(8,128)}, f32[1,2,128,128]{3,2,1,0:T(8,128)}, u32[]{:S(2)}, u32[]{:S(2)}) collective-permute-start(f32[1,2,128,128]{3,2,1,0:T(8,128)} %get-tuple-element.275), channel_id=1, source_target_pairs={{0,9},{1,10},{2,11},{3,12},{4,13},{5,14},{6,15},{7,0},{8,1},{9,2},... | collective-permute-start | bytes 393224 | tf_op jit(solution)/shard_map/ppermute | solution.py:556
  76.3 80.4 %collective-permute-start.29 = (f32[1,2,128,128]{3,2,1,0:T(8,128)}, f32[1,2,128,128]{3,2,1,0:T(8,128)}, u32[]{:S(2)}, u32[]{:S(2)}) collective-permute-start(f32[1,2,128,128]{3,2,1,0:T(8,128)} %get-tuple-element.276), channel_id=1, source_target_pairs={{0,10},{1,11},{2,12},{3,13},{4,14},{5,15},{6,0},{7,1},{8,2},{9,3},... | collective-permute-start | bytes 393224 | tf_op jit(solution)/shard_map/ppermute | solution.py:556
  163.8 61.9 %collective-permute-start.8 = (f32[2,2,128,128]{3,2,1,0:T(8,128)}, f32[2,2,128,128]{3,2,1,0:T(8,128)}, u32[]{:S(2)}, u32[]{:S(2)}) collective-permute-start(f32[2,2,128,128]{3,2,1,0:T(8,128)} %get-tuple-element.228), channel_id=1, source_target_pairs={{0,9},{1,10},{2,11},{3,12},{4,13},{5,14},{6,15},{7,0},{8,1},{9,2},... | collective-permute-start | bytes 786440 | tf_op jit(solution)/shard_map/ppermute | solution.py:556
  319.5 248.2 %all-to-all-start.1 = ((f32[16,2,2,128,128]{4,3,2,1,0:T(8,128)}), f32[16,2,2,128,128]{4,3,2,1,0:T(8,128)}, u32[]{:S(2)}, u32[]{:S(2)}) async-start(f32[16,2,2,128,128]{4,3,2,1,0:T(8,128)} %get-tuple-element.298), calls=%async_computation.1 | async-start | bytes 8388608 | tf_op jit(solution)/shard_map/all_to_all | solution.py:571
  325.7 75.8 %collective-permute-start.40 = (f32[1,2,128,128]{3,2,1,0:T(8,128)S(1)}, f32[1,2,128,128]{3,2,1,0:T(8,128)}, u32[]{:S(2)}, u32[]{:S(2)}) collective-permute-start(f32[1,2,128,128]{3,2,1,0:T(8,128)S(1)} %copy-done.34), channel_id=1, source_target_pairs={{0,1},{1,2},{2,3},{3,4},{4,5},{5,6},{6,7},{7,8},{8,9},{9,10},{10,1... | collective-permute-start | bytes 393224 | tf_op jit(solution)/shard_map/ppermute | solution.py:556
  326.1 76.6 %collective-permute-start.41 = (f32[1,2,128,128]{3,2,1,0:T(8,128)S(1)}, f32[1,2,128,128]{3,2,1,0:T(8,128)}, u32[]{:S(2)}, u32[]{:S(2)}) collective-permute-start(f32[1,2,128,128]{3,2,1,0:T(8,128)S(1)} %copy-done.33), channel_id=1, source_target_pairs={{0,2},{1,3},{2,4},{3,5},{4,6},{5,7},{6,8},{7,9},{8,10},{9,11},{10,... | collective-permute-start | bytes 393224 | tf_op jit(solution)/shard_map/ppermute | solution.py:556
  327.8 100.3 %collective-permute-start.42 = (f32[1,2,128,128]{3,2,1,0:T(8,128)S(1)}, f32[1,2,128,128]{3,2,1,0:T(8,128)}, u32[]{:S(2)}, u32[]{:S(2)}) collective-permute-start(f32[1,2,128,128]{3,2,1,0:T(8,128)S(1)} %copy-done.32), channel_id=1, source_target_pairs={{0,3},{1,4},{2,5},{3,6},{4,7},{5,8},{6,9},{7,10},{8,11},{9,12},{10... | collective-permute-start | bytes 393224 | tf_op jit(solution)/shard_map/ppermute | solution.py:556
  330.0 98.8 %collective-permute-start.43 = (f32[1,2,128,128]{3,2,1,0:T(8,128)S(1)}, f32[1,2,128,128]{3,2,1,0:T(8,128)}, u32[]{:S(2)}, u32[]{:S(2)}) collective-permute-start(f32[1,2,128,128]{3,2,1,0:T(8,128)S(1)} %copy-done.31), channel_id=1, source_target_pairs={{0,4},{1,5},{2,6},{3,7},{4,8},{5,9},{6,10},{7,11},{8,12},{9,13},{1... | collective-permute-start | bytes 393224 | tf_op jit(solution)/shard_map/ppermute | solution.py:556
  331.5 112.6 %collective-permute-start.44 = (f32[1,2,128,128]{3,2,1,0:T(8,128)S(1)}, f32[1,2,128,128]{3,2,1,0:T(8,128)}, u32[]{:S(2)}, u32[]{:S(2)}) collective-permute-start(f32[1,2,128,128]{3,2,1,0:T(8,128)S(1)} %copy-done.30), channel_id=1, source_target_pairs={{0,5},{1,6},{2,7},{3,8},{4,9},{5,10},{6,11},{7,12},{8,13},{9,14},{... | collective-permute-start | bytes 393224 | tf_op jit(solution)/shard_map/ppermute | solution.py:556
  567.7 129.0 %all-to-all-start.2 = ((f32[16,2,2,128,128]{4,3,2,1,0:T(8,128)}), f32[16,2,2,128,128]{4,3,2,1,0:T(8,128)}, u32[]{:S(2)}, u32[]{:S(2)}) async-start(f32[16,2,2,128,128]{4,3,2,1,0:T(8,128)} %get-tuple-element.333), calls=%async_computation.2 | async-start | bytes 8388608 | tf_op jit(solution)/shard_map/all_to_all | solution.py:571
  696.7 97.6 %all-to-all-start.3 = ((f32[16,1,2,128,128]{4,3,2,1,0:T(8,128)}), f32[16,1,2,128,128]{4,3,2,1,0:T(8,128)}, u32[]{:S(2)}, u32[]{:S(2)}) async-start(f32[16,1,2,128,128]{4,3,2,1,0:T(8,128)} %get-tuple-element.347), calls=%async_computation.3 | async-start | bytes 4194304 | tf_op jit(solution)/shard_map/all_to_all | solution.py:571
  702.9 63.2 %collective-permute-start.72 = (f32[1,2,128,128]{3,2,1,0:T(8,128)S(1)}, f32[1,2,128,128]{3,2,1,0:T(8,128)}, u32[]{:S(2)}, u32[]{:S(2)}) collective-permute-start(f32[1,2,128,128]{3,2,1,0:T(8,128)S(1)} %copy-done.43), channel_id=1, source_target_pairs={{0,6},{1,7},{2,8},{3,9},{4,10},{5,11},{6,12},{7,13},{8,14},{9,15},... | collective-permute-start | bytes 393224 | tf_op jit(solution)/shard_map/ppermute | solution.py:556
  705.7 62.5 %collective-permute-start.73 = (f32[1,2,128,128]{3,2,1,0:T(8,128)S(1)}, f32[1,2,128,128]{3,2,1,0:T(8,128)}, u32[]{:S(2)}, u32[]{:S(2)}) collective-permute-start(f32[1,2,128,128]{3,2,1,0:T(8,128)S(1)} %copy-done.42), channel_id=1, source_target_pairs={{0,7},{1,8},{2,9},{3,10},{4,11},{5,12},{6,13},{7,14},{8,15},{9,0},... | collective-permute-start | bytes 393224 | tf_op jit(solution)/shard_map/ppermute | solution.py:556
  707.5 61.9 %collective-permute-start.74 = (f32[1,2,128,128]{3,2,1,0:T(8,128)S(1)}, f32[1,2,128,128]{3,2,1,0:T(8,128)}, u32[]{:S(2)}, u32[]{:S(2)}) collective-permute-start(f32[1,2,128,128]{3,2,1,0:T(8,128)S(1)} %copy-done.41), channel_id=1, source_target_pairs={{0,8},{1,9},{2,10},{3,11},{4,12},{5,13},{6,14},{7,15},{8,0},{9,1},... | collective-permute-start | bytes 393224 | tf_op jit(solution)/shard_map/ppermute | solution.py:556
  849.2 200.5 %all-to-all-start.4 = ((f32[16,2,2,80,128]{4,3,2,1,0:T(8,128)}), f32[16,2,2,80,128]{4,3,2,1,0:T(8,128)}, u32[]{:S(2)}, u32[]{:S(2)}) async-start(f32[16,2,2,80,128]{4,3,2,1,0:T(8,128)} %get-tuple-element.384), calls=%async_computation.4 | async-start | bytes 5242880 | tf_op jit(solution)/shard_map/all_to_all | solution.py:571
  855.9 74.5 %collective-permute-start.102 = (f32[1,2,128,128]{3,2,1,0:T(8,128)S(1)}, f32[1,2,128,128]{3,2,1,0:T(8,128)}, u32[]{:S(2)}, u32[]{:S(2)}) collective-permute-start(f32[1,2,128,128]{3,2,1,0:T(8,128)S(1)} %copy-done.44), channel_id=1, source_target_pairs={{0,6},{1,7},{2,8},{3,9},{4,10},{5,11},{6,12},{7,13},{8,14},{9,15},... | collective-permute-start | bytes 393224 | tf_op jit(solution)/shard_map/ppermute | solution.py:556
  858.8 73.8 %collective-permute-start.103 = (f32[1,2,128,128]{3,2,1,0:T(8,128)S(1)}, f32[1,2,128,128]{3,2,1,0:T(8,128)}, u32[]{:S(2)}, u32[]{:S(2)}) collective-permute-start(f32[1,2,128,128]{3,2,1,0:T(8,128)S(1)} %copy-done.40), channel_id=1, source_target_pairs={{0,7},{1,8},{2,9},{3,10},{4,11},{5,12},{6,13},{7,14},{8,15},{9,0},... | collective-permute-start | bytes 393224 | tf_op jit(solution)/shard_map/ppermute | solution.py:556
  860.6 73.1 %collective-permute-start.104 = (f32[1,2,128,128]{3,2,1,0:T(8,128)S(1)}, f32[1,2,128,128]{3,2,1,0:T(8,128)}, u32[]{:S(2)}, u32[]{:S(2)}) collective-permute-start(f32[1,2,128,128]{3,2,1,0:T(8,128)S(1)} %copy-done.37), channel_id=1, source_target_pairs={{0,8},{1,9},{2,10},{3,11},{4,12},{5,13},{6,14},{7,15},{8,0},{9,1},... | collective-permute-start | bytes 393224 | tf_op jit(solution)/shard_map/ppermute | solution.py:556
  861.2 74.0 %collective-permute-start.105 = (f32[1,2,128,128]{3,2,1,0:T(8,128)S(1)}, f32[1,2,128,128]{3,2,1,0:T(8,128)}, u32[]{:S(2)}, u32[]{:S(2)}) collective-permute-start(f32[1,2,128,128]{3,2,1,0:T(8,128)S(1)} %copy-done.36), channel_id=1, source_target_pairs={{0,9},{1,10},{2,11},{3,12},{4,13},{5,14},{6,15},{7,0},{8,1},{9,2},... | collective-permute-start | bytes 393224 | tf_op jit(solution)/shard_map/ppermute | solution.py:556
  863.5 79.0 %collective-permute-start.106 = (f32[1,2,128,128]{3,2,1,0:T(8,128)S(1)}, f32[1,2,128,128]{3,2,1,0:T(8,128)}, u32[]{:S(2)}, u32[]{:S(2)}) collective-permute-start(f32[1,2,128,128]{3,2,1,0:T(8,128)S(1)} %copy-done.35), channel_id=1, source_target_pairs={{0,10},{1,11},{2,12},{3,13},{4,14},{5,15},{6,0},{7,1},{8,2},{9,3},... | collective-permute-start | bytes 393224 | tf_op jit(solution)/shard_map/ppermute | solution.py:556
  (137 other events, 5740.3 us)

commit v6 on v5

--- a/solution.py
+++ b/solution.py
@@ -557,14 +557,28 @@
     return moved
 
 
-def after_light(arrived, then):
+def after_first(arrived, then):
     count = len(arrived)
-    light = [n for n in range(1, count) if is_light(n, count)]
-    held = lax.optimization_barrier((tuple(arrived[n] for n in light), *then))
+    first = [n for n in range(1, count) if not is_light(n, count)]
+    held = lax.optimization_barrier((tuple(arrived[n] for n in first), *then))
     arrived = list(arrived)
-    for n, value in zip(light, held[0]):
+    for n, value in zip(first, held[0]):
         arrived[n] = value
     return (arrived, *held[1:])
+
+
+def tick_kernel(before, after):
+    for n in range(before.shape[0]):
+        after[n] = before[n]
+
+
+def ticked(scalars):
+    return pl.pallas_call(
+        tick_kernel,
+        out_shape=jax.ShapeDtypeStruct(scalars.shape, scalars.dtype),
+        in_specs=[SCALARS],
+        out_specs=SCALARS,
+    )(scalars)
 
 
 def exchanged(value):
@@ -637,7 +651,7 @@
             compiler_params=PARAMS,
         )(place, velocity, table, twist)
 
-    def middle(chunk, own, other, state):
+    def middle(scalars, chunk, own, other, state):
         shapes, specs = forward_shapes(chunk, False)
         *sent, state_new = pl.pallas_call(
             middle_kernel,
@@ -660,7 +674,7 @@
         )(place, scalars, own, other, prestress, strength, state, table, twist)
         return sent, state_new
 
-    def end(row, own, other, state, before):
+    def end(scalars, row, own, other, state, before):
         full = jax.ShapeDtypeStruct((rows_dev, length), f32)
         step = 16
         parts = own.shape[0] // step
@@ -789,11 +803,13 @@
             twist_ring = jnp.stack([jnp.cos(turn), jnp.sin(turn)])
         else:
             own = inverse(waiting)
-            sent[1], states[1] = middle(1, own, swapped(own, "side", 0), states[1])
+            sent[1], states[1] = middle(scalars, 1, own, swapped(own, "side", 0), states[1])
         near = ringed(sent[1][:slabs])
         if step_index == 0:
             sums = past_sums()
-        near, far, sums = after_light(near, (sent[1][slabs], sums))
+        else:
+            scalars = ticked(scalars)
+        near, far, sums = after_first(near, (sent[1][slabs], sums))
         far = exchanged(far)
         outs = spectral(0, ring, near, sums[step_index], past[0], pieces, None)
         if step_index == 0:
@@ -806,12 +822,13 @@
             past[1] = outs[-1]
         late = outs[slabs : slabs + len(pieces) - 1]
         more = ringed(outs[:slabs])
-        more, late = after_light(more, (list(late),))
+        scalars = ticked(scalars)
+        more, late = after_first(more, (list(late),))
         waiting = exchanged(late[0])
         own = inverse(*back, *more)
         other = swapped(own, "side", 0)
         if not last:
-            sent[0], states[0] = middle(0, own, other, states[0])
+            sent[0], states[0] = middle(scalars, 0, own, other, states[0])
         if not last:
             waiting, sent[0], states[0] = hold((waiting, sent[0], states[0]))
             continue
@@ -819,12 +836,12 @@
         final = exchanged(final)
         own_near = inverse(waiting)
         other_near = swapped(own_near, "side", 0)
-        results = end(0, own, other, states[0], ())
+        results = end(scalars, 0, own, other, states[0], ())
         final, own_near, results = hold((final, own_near, tuple(results)))
         own = inverse(final)
         other = swapped(own, "side", 0)
-        results = end(whole, own_near, other_near, states[1], results)
-        results = end(whole + cut, own, other, states[1], results)
+        results = end(scalars, whole, own_near, other_near, states[1], results)
+        results = end(scalars, whole + cut, own, other, states[1], results)
     return tuple(results)
 
 

time: 1120 us -> 1120 us (level)
  starting transfers between devices: 316 us -> 298 us
    ppermute x105, starting transfers between devices: 263 us -> 240 us  [ringed(): moved.append(lax.ppermute(blocks[n], 'slab', pairs))]
  transfers between devices with their start and end apart: 116 -> 116, of which waited for: 44 -> 48; matrix products, arithmetic and copies ran while one was open for 0% -> 0% of each run, Pallas kernels for 18% -> 19%
where the time goes in v6:
time: 1120 us; the launch traced here: 1110 us
  waiting for transfers between devices  529 us (47%)
  starting transfers between devices  298 us (27%)
  Pallas kernels  278 us (25%)
    ppermute x105, waiting for transfers between devices, ringed(): moved.append(lax.ppermute(blocks[n], 'slab', pairs))  380 us
    ppermute x105, starting transfers between devices, ringed(): moved.append(lax.ppermute(blocks[n], 'slab', pairs))  240 us
    ppermute x5, waiting for transfers between devices, swapped(): return lax.ppermute(value, axis, pairs)  143 us
    pallas_call x4, Pallas kernels, spectral(): pl.pallas_call(functools.partial(spectral_kernel, (len(ring), len(near)),...  99.3 us
    pallas_call x5, Pallas kernels, inverse(): pl.pallas_call(functools.partial(inverse_kernel, len(blocks)), out_shape=...  52.7 us
    all_to_all x6, starting transfers between devices, exchanged(): lax.all_to_all(value, 'slab', split_axis=0, concat_axis=0, tiled=True)  50 us
    pallas_call x2, Pallas kernels, middle(): pl.pallas_call(middle_kernel, out_shape=shapes + [rows_shape], grid=(1,),...  46.4 us
    pallas_call x3, Pallas kernels, end(): pl.pallas_call(end_kernel, out_shape=(jax.ShapeDtypeStruct((1, rows_dev,...  27 us
  transfers between devices with their start and end apart: 116, of which 48 were waited for; matrix products, arithmetic and copies ran while one was open for 0% of the time, Pallas kernels for 19%

profile of v6, /device:TPU:0, one launch (start us, length us, event | category | flops | bytes accessed | tf_op | source)
XLA Modules:
  0.0 1113.8 jit_solution(6596840561989367287)
XLA Ops:
  22.4 24.8 %shard_map.117 = (f32[2,256,4096]{2,1,0:T(8,128)}, f32[2,256,4096]{2,1,0:T(8,128)}) custom-call(bf16[1,9,256,4096]{3,2,1,0:T(8,128)(2,1)} %refs_8_.1, bf16[1,8,2,256,4096]{4,3,2,1,0:T(8,128)(2,1)} %history.1), custom_call_target="tpu_custom_call" | custom-call | tf_op jit(solution)/shard_map/pallas_call | solution.py:702
  57.8 36.2 %collective-permute-done.20.refs_18_ = f32[1,2,128,128]{3,2,1,0:T(8,128)} collective-permute-done((f32[1,2,128,128]{3,2,1,0:T(8,128)S(1)}, f32[1,2,128,128]{3,2,1,0:T(8,128)}, u32[]{:S(2)}, u32[]{:S(2)}) %collective-permute-start.20) | collective-permute-done | bytes 131104 | tf_op jit(solution)/shard_map/ppermute | solution.py:556
  95.1 18.0 %collective-permute-start.26 = (f32[1,2,128,128]{3,2,1,0:T(8,128)}, f32[1,2,128,128]{3,2,1,0:T(8,128)}, u32[]{:S(2)}, u32[]{:S(2)}) collective-permute-start(f32[1,2,128,128]{3,2,1,0:T(8,128)} %get-tuple-element.253), channel_id=1, source_target_pairs={{0,12},{1,13},{2,14},{3,15},{4,0},{5,1},{6,2},{7,3},{8,4},{9,5},{1... | collective-permute-start | bytes 393224 | tf_op jit(solution)/shard_map/ppermute | solution.py:556
  121.0 12.8 %shard_map.115 = (f32[2,2,128,128]{3,2,1,0:T(8,128)}, f32[2,2,128,128]{3,2,1,0:T(8,128)}, f32[2,2,128,128]{3,2,1,0:T(8,128)}, f32[2,2,128,128]{3,2,1,0:T(8,128)}...) custom-call(s32[1]{0:T(128)} %bitcast.7.place.refs_0_, ...), custom_call_target="tpu_custom_call" | custom-call | tf_op jit(solution)/shard_map/pallas_call | solution.py:639
  151.3 19.6 %collective-permute-start.3 = (f32[2,2,128,128]{3,2,1,0:T(8,128)}, f32[2,2,128,128]{3,2,1,0:T(8,128)}, u32[]{:S(2)}, u32[]{:S(2)}) collective-permute-start(f32[2,2,128,128]{3,2,1,0:T(8,128)} %get-tuple-element.203), channel_id=1, source_target_pairs={{0,4},{1,5},{2,6},{3,7},{4,8},{5,9},{6,10},{7,11},{8,12},{9,13},{1... | collective-permute-start | bytes 786440 | tf_op jit(solution)/shard_map/ppermute | solution.py:556
  182.2 27.1 %collective-permute-done.4.refs_6_ = f32[2,2,128,128]{3,2,1,0:T(8,128)} collective-permute-done((f32[2,2,128,128]{3,2,1,0:T(8,128)}, f32[2,2,128,128]{3,2,1,0:T(8,128)}, u32[]{:S(2)}, u32[]{:S(2)}) %collective-permute-start.4) | collective-permute-done | bytes 262176 | tf_op jit(solution)/shard_map/ppermute | solution.py:556
  231.8 24.5 %shard_map.118 = (f32[1,2,128,128]{3,2,1,0:T(8,128)}, f32[1,2,128,128]{3,2,1,0:T(8,128)}, f32[1,2,128,128]{3,2,1,0:T(8,128)}, f32[1,2,128,128]{3,2,1,0:T(8,128)}...) custom-call(s32[1]{0:T(128)} %bitcast.7.place.refs_0_, ...), custom_call_target="tpu_custom_call" | custom-call | tf_op jit(solution)/shard_map/pallas_call | solution.py:754
  256.3 24.8 %shard_map.119 = (f32[1,2,128,128]{3,2,1,0:T(8,128)}, f32[1,2,128,128]{3,2,1,0:T(8,128)}, f32[1,2,128,128]{3,2,1,0:T(8,128)}, f32[1,2,128,128]{3,2,1,0:T(8,128)}...) custom-call(s32[1]{0:T(128)} %bitcast.7.place.refs_0_, ...), custom_call_target="tpu_custom_call", output_to_operand_aliasing={{16}: (23, {})} | custom-call | tf_op jit(solution)/shard_map/pallas_call | solution.py:754
  319.4 69.9 %collective-permute-done.35.refs_1_ = f32[1,2,128,128]{3,2,1,0:T(8,128)} collective-permute-done((f32[1,2,128,128]{3,2,1,0:T(8,128)S(1)}, f32[1,2,128,128]{3,2,1,0:T(8,128)}, u32[]{:S(2)}, u32[]{:S(2)}) %collective-permute-start.35) | collective-permute-done | bytes 131104 | tf_op jit(solution)/shard_map/ppermute | solution.py:556
  390.5 25.4 %collective-permute-start.41 = (f32[1,2,128,128]{3,2,1,0:T(8,128)S(1)}, f32[1,2,128,128]{3,2,1,0:T(8,128)}, u32[]{:S(2)}, u32[]{:S(2)}) collective-permute-start(f32[1,2,128,128]{3,2,1,0:T(8,128)S(1)} %copy-done.33), channel_id=1, source_target_pairs={{0,7},{1,8},{2,9},{3,10},{4,11},{5,12},{6,13},{7,14},{8,15},{9,0},... | collective-permute-start | bytes 393224 | tf_op jit(solution)/shard_map/ppermute | solution.py:556
  418.9 13.0 %collective-permute-done.39.refs_5_ = f32[1,2,128,128]{3,2,1,0:T(8,128)} collective-permute-done((f32[1,2,128,128]{3,2,1,0:T(8,128)S(1)}, f32[1,2,128,128]{3,2,1,0:T(8,128)}, u32[]{:S(2)}, u32[]{:S(2)}) %collective-permute-start.39) | collective-permute-done | bytes 131104 | tf_op jit(solution)/shard_map/ppermute | solution.py:556
  496.3 38.5 %collective-permute-done.60.other = f32[128,4096]{1,0:T(8,128)} collective-permute-done((f32[128,4096]{1,0:T(8,128)}, f32[128,4096]{1,0:T(8,128)}, u32[]{:S(2)}, u32[]{:S(2)}) %collective-permute-start.60) | collective-permute-done | bytes 2097184 | tf_op jit(solution)/shard_map/ppermute | solution.py:25
  534.8 22.8 %shard_map.121 = (f32[16,2,2,128,128]{4,3,2,1,0:T(8,128)}, f32[128,4096]{1,0:T(8,128)}) custom-call(s32[1]{0:T(128)} %bitcast.7.place.refs_0_, f32[5]{0:T(128)} %shard_map.112.before.scalars, f32[128,4096]{1,0:T(8,128)} %shard_map.120.own, f32[128,4096]{1,0:T(8,128)} %collective-permute-done.60.other, f32[256,4096]{1,0:T(8,128)} %prestress.9, ...), custom_call_target="tpu_custom_call" | custom-call | tf_op jit(solution)/shard_map/pallas_call | solution.py:656
  581.1 46.7 %collective-permute-done.61.other = f32[128,4096]{1,0:T(8,128)} collective-permute-done((f32[128,4096]{1,0:T(8,128)}, f32[128,4096]{1,0:T(8,128)}, u32[]{:S(2)}, u32[]{:S(2)}) %collective-permute-start.61) | collective-permute-done | bytes 2097184 | tf_op jit(solution)/shard_map/ppermute | solution.py:25
  627.8 23.6 %shard_map.123 = (f32[1,2,128,128]{3,2,1,0:T(8,128)}, f32[1,2,128,128]{3,2,1,0:T(8,128)}, f32[1,2,128,128]{3,2,1,0:T(8,128)}, f32[1,2,128,128]{3,2,1,0:T(8,128)}...) custom-call(s32[1]{0:T(128)} %bitcast.7.place.refs_0_, ...), custom_call_target="tpu_custom_call" | custom-call | tf_op jit(solution)/shard_map/pallas_call | solution.py:656
  660.2 16.1 %collective-permute-done.62.refs_8_ = f32[1,2,128,128]{3,2,1,0:T(8,128)} collective-permute-done((f32[1,2,128,128]{3,2,1,0:T(8,128)}, f32[1,2,128,128]{3,2,1,0:T(8,128)}, u32[]{:S(2)}, u32[]{:S(2)}) %collective-permute-start.62) | collective-permute-done | bytes 131104 | tf_op jit(solution)/shard_map/ppermute | solution.py:556
  695.8 36.2 %collective-permute-done.67.refs_3_ = f32[1,2,128,128]{3,2,1,0:T(8,128)} collective-permute-done((f32[1,2,128,128]{3,2,1,0:T(8,128)S(1)}, f32[1,2,128,128]{3,2,1,0:T(8,128)}, u32[]{:S(2)}, u32[]{:S(2)}) %collective-permute-start.67) | collective-permute-done | bytes 131104 | tf_op jit(solution)/shard_map/ppermute | solution.py:556
  733.1 18.0 %collective-permute-start.73 = (f32[1,2,128,128]{3,2,1,0:T(8,128)S(1)}, f32[1,2,128,128]{3,2,1,0:T(8,128)}, u32[]{:S(2)}, u32[]{:S(2)}) collective-permute-start(f32[1,2,128,128]{3,2,1,0:T(8,128)S(1)} %copy-done.47), channel_id=1, source_target_pairs={{0,12},{1,13},{2,14},{3,15},{4,0},{5,1},{6,2},{7,3},{8,4},{9,5},{1... | collective-permute-start | bytes 393224 | tf_op jit(solution)/shard_map/ppermute | solution.py:556
  762.1 24.9 %shard_map.124 = (f32[1,2,128,128]{3,2,1,0:T(8,128)}, f32[1,2,128,128]{3,2,1,0:T(8,128)}, f32[1,2,128,128]{3,2,1,0:T(8,128)}, f32[1,2,128,128]{3,2,1,0:T(8,128)}...) custom-call(s32[1]{0:T(128)} %bitcast.7.place.refs_0_, ...), custom_call_target="tpu_custom_call" | custom-call | tf_op jit(solution)/shard_map/pallas_call | solution.py:754
  787.1 25.1 %shard_map.125 = (f32[1,2,128,128]{3,2,1,0:T(8,128)}, f32[1,2,128,128]{3,2,1,0:T(8,128)}, f32[1,2,128,128]{3,2,1,0:T(8,128)}, f32[1,2,128,128]{3,2,1,0:T(8,128)}...) custom-call(s32[1]{0:T(128)} %bitcast.7.place.refs_0_, ...), custom_call_target="tpu_custom_call", output_to_operand_aliasing={{16}: (10, {}), {17}: (11, {})} | custom-call | tf_op jit(solution)/shard_map/pallas_call | solution.py:754
  853.6 43.3 %collective-permute-done.100.refs_20_ = f32[1,2,128,128]{3,2,1,0:T(8,128)} collective-permute-done((f32[1,2,128,128]{3,2,1,0:T(8,128)S(1)}, f32[1,2,128,128]{3,2,1,0:T(8,128)}, u32[]{:S(2)}, u32[]{:S(2)}) %collective-permute-start.100) | collective-permute-done | bytes 131104 | tf_op jit(solution)/shard_map/ppermute | solution.py:556
  897.3 18.0 %collective-permute-done.101.refs_21_ = f32[1,2,128,128]{3,2,1,0:T(8,128)} collective-permute-done((f32[1,2,128,128]{3,2,1,0:T(8,128)S(1)}, f32[1,2,128,128]{3,2,1,0:T(8,128)}, u32[]{:S(2)}, u32[]{:S(2)}) %collective-permute-start.101) | collective-permute-done | bytes 131104 | tf_op jit(solution)/shard_map/ppermute | solution.py:556
  944.9 16.6 %collective-permute-done.86.refs_5_ = f32[1,2,128,128]{3,2,1,0:T(8,128)} collective-permute-done((f32[1,2,128,128]{3,2,1,0:T(8,128)S(1)}, f32[1,2,128,128]{3,2,1,0:T(8,128)}, u32[]{:S(2)}, u32[]{:S(2)}) %collective-permute-start.86) | collective-permute-done | bytes 131104 | tf_op jit(solution)/shard_map/ppermute | solution.py:556
  995.6 47.0 %collective-permute-done.107.other = f32[128,4096]{1,0:T(8,128)} collective-permute-done((f32[128,4096]{1,0:T(8,128)}, f32[128,4096]{1,0:T(8,128)}, u32[]{:S(2)}, u32[]{:S(2)}) %collective-permute-start.107) | collective-permute-done | bytes 2097184 | tf_op jit(solution)/shard_map/ppermute | solution.py:25
  (363 shorter events, 434.6 us)
Async XLA Ops:
  47.3 209.0 %all-to-all-start = ((f32[16,1,2,128,128]{4,3,2,1,0:T(8,128)}), f32[16,1,2,128,128]{4,3,2,1,0:T(8,128)}, u32[]{:S(2)}, u32[]{:S(2)}) async-start(f32[16,1,2,128,128]{4,3,2,1,0:T(8,128)} %get-tuple-element.240), calls=%async_computation | async-start | bytes 4194304 | tf_op jit(solution)/shard_map/all_to_all | solution.py:585
  53.8 59.3 %collective-permute-start.22 = (f32[1,2,128,128]{3,2,1,0:T(8,128)S(1)}, f32[1,2,128,128]{3,2,1,0:T(8,128)}, u32[]{:S(2)}, u32[]{:S(2)}) collective-permute-start(f32[1,2,128,128]{3,2,1,0:T(8,128)S(1)} %copy-done.58), channel_id=1, source_target_pairs={{0,3},{1,4},{2,5},{3,6},{4,7},{5,8},{6,9},{7,10},{8,11},{9,12},{10... | collective-permute-start | bytes 393224 | tf_op jit(solution)/shard_map/ppermute | solution.py:556
  56.1 60.4 %collective-permute-start.23 = (f32[1,2,128,128]{3,2,1,0:T(8,128)S(1)}, f32[1,2,128,128]{3,2,1,0:T(8,128)}, u32[]{:S(2)}, u32[]{:S(2)}) collective-permute-start(f32[1,2,128,128]{3,2,1,0:T(8,128)S(1)} %copy-done.55), channel_id=1, source_target_pairs={{0,4},{1,5},{2,6},{3,7},{4,8},{5,9},{6,10},{7,11},{8,12},{9,13},{1... | collective-permute-start | bytes 393224 | tf_op jit(solution)/shard_map/ppermute | solution.py:556
  57.6 59.1 %collective-permute-start.24 = (f32[1,2,128,128]{3,2,1,0:T(8,128)S(1)}, f32[1,2,128,128]{3,2,1,0:T(8,128)}, u32[]{:S(2)}, u32[]{:S(2)}) collective-permute-start(f32[1,2,128,128]{3,2,1,0:T(8,128)S(1)} %copy-done.52), channel_id=1, source_target_pairs={{0,5},{1,6},{2,7},{3,8},{4,9},{5,10},{6,11},{7,12},{8,13},{9,14},{... | collective-permute-start | bytes 393224 | tf_op jit(solution)/shard_map/ppermute | solution.py:556
  305.2 252.5 %all-to-all-start.1 = ((f32[16,2,2,128,128]{4,3,2,1,0:T(8,128)}), f32[16,2,2,128,128]{4,3,2,1,0:T(8,128)}, u32[]{:S(2)}, u32[]{:S(2)}) async-start(f32[16,2,2,128,128]{4,3,2,1,0:T(8,128)} %get-tuple-element.268), calls=%async_computation.1 | async-start | bytes 8388608 | tf_op jit(solution)/shard_map/all_to_all | solution.py:585
  313.5 75.8 %collective-permute-start.35 = (f32[1,2,128,128]{3,2,1,0:T(8,128)S(1)}, f32[1,2,128,128]{3,2,1,0:T(8,128)}, u32[]{:S(2)}, u32[]{:S(2)}) collective-permute-start(f32[1,2,128,128]{3,2,1,0:T(8,128)S(1)} %copy-done.40), channel_id=1, source_target_pairs={{0,1},{1,2},{2,3},{3,4},{4,5},{5,6},{6,7},{7,8},{8,9},{9,10},{10,1... | collective-permute-start | bytes 393224 | tf_op jit(solution)/shard_map/ppermute | solution.py:556
  313.9 76.6 %collective-permute-start.36 = (f32[1,2,128,128]{3,2,1,0:T(8,128)S(1)}, f32[1,2,128,128]{3,2,1,0:T(8,128)}, u32[]{:S(2)}, u32[]{:S(2)}) collective-permute-start(f32[1,2,128,128]{3,2,1,0:T(8,128)S(1)} %copy-done.38), channel_id=1, source_target_pairs={{0,2},{1,3},{2,4},{3,5},{4,6},{5,7},{6,8},{7,9},{8,10},{9,11},{10,... | collective-permute-start | bytes 393224 | tf_op jit(solution)/shard_map/ppermute | solution.py:556
  316.6 99.3 %collective-permute-start.37 = (f32[1,2,128,128]{3,2,1,0:T(8,128)S(1)}, f32[1,2,128,128]{3,2,1,0:T(8,128)}, u32[]{:S(2)}, u32[]{:S(2)}) collective-permute-start(f32[1,2,128,128]{3,2,1,0:T(8,128)S(1)} %copy-done.37), channel_id=1, source_target_pairs={{0,3},{1,4},{2,5},{3,6},{4,7},{5,8},{6,9},{7,10},{8,11},{9,12},{10... | collective-permute-start | bytes 393224 | tf_op jit(solution)/shard_map/ppermute | solution.py:556
  317.8 98.8 %collective-permute-start.38 = (f32[1,2,128,128]{3,2,1,0:T(8,128)S(1)}, f32[1,2,128,128]{3,2,1,0:T(8,128)}, u32[]{:S(2)}, u32[]{:S(2)}) collective-permute-start(f32[1,2,128,128]{3,2,1,0:T(8,128)S(1)} %copy-done.36), channel_id=1, source_target_pairs={{0,4},{1,5},{2,6},{3,7},{4,8},{5,9},{6,10},{7,11},{8,12},{9,13},{1... | collective-permute-start | bytes 393224 | tf_op jit(solution)/shard_map/ppermute | solution.py:556
  319.3 112.6 %collective-permute-start.39 = (f32[1,2,128,128]{3,2,1,0:T(8,128)S(1)}, f32[1,2,128,128]{3,2,1,0:T(8,128)}, u32[]{:S(2)}, u32[]{:S(2)}) collective-permute-start(f32[1,2,128,128]{3,2,1,0:T(8,128)S(1)} %copy-done.35), channel_id=1, source_target_pairs={{0,5},{1,6},{2,7},{3,8},{4,9},{5,10},{6,11},{7,12},{8,13},{9,14},{... | collective-permute-start | bytes 393224 | tf_op jit(solution)/shard_map/ppermute | solution.py:556
  486.7 48.1 %collective-permute-start.60 = (f32[128,4096]{1,0:T(8,128)}, f32[128,4096]{1,0:T(8,128)}, u32[]{:S(2)}, u32[]{:S(2)}) collective-permute-start(f32[128,4096]{1,0:T(8,128)} %shard_map.120.own), channel_id=1, source_target_pairs={{0,16},{16,0},{1,17},{17,1},{2,18},{18,2},{3,19},{19,3},{4,20},{20... | collective-permute-start | bytes 6291464 | tf_op jit(solution)/shard_map/ppermute | solution.py:25
  557.6 122.0 %all-to-all-start.2 = ((f32[16,2,2,128,128]{4,3,2,1,0:T(8,128)}), f32[16,2,2,128,128]{4,3,2,1,0:T(8,128)}, u32[]{:S(2)}, u32[]{:S(2)}) async-start(f32[16,2,2,128,128]{4,3,2,1,0:T(8,128)} %get-tuple-element.303), calls=%async_computation.2 | async-start | bytes 8388608 | tf_op jit(solution)/shard_map/all_to_all | solution.py:585
  579.6 48.2 %collective-permute-start.61 = (f32[128,4096]{1,0:T(8,128)}, f32[128,4096]{1,0:T(8,128)}, u32[]{:S(2)}, u32[]{:S(2)}) collective-permute-start(f32[128,4096]{1,0:T(8,128)} %shard_map.122.own), channel_id=1, source_target_pairs={{0,16},{16,0},{1,17},{17,1},{2,18},{18,2},{3,19},{19,3},{4,20},{20... | collective-permute-start | bytes 6291464 | tf_op jit(solution)/shard_map/ppermute | solution.py:25
  679.6 107.4 %all-to-all-start.3 = ((f32[16,1,2,128,128]{4,3,2,1,0:T(8,128)}), f32[16,1,2,128,128]{4,3,2,1,0:T(8,128)}, u32[]{:S(2)}, u32[]{:S(2)}) async-start(f32[16,1,2,128,128]{4,3,2,1,0:T(8,128)} %get-tuple-element.312), calls=%async_computation.3 | async-start | bytes 4194304 | tf_op jit(solution)/shard_map/all_to_all | solution.py:585
  691.9 59.3 %collective-permute-start.69 = (f32[1,2,128,128]{3,2,1,0:T(8,128)S(1)}, f32[1,2,128,128]{3,2,1,0:T(8,128)}, u32[]{:S(2)}, u32[]{:S(2)}) collective-permute-start(f32[1,2,128,128]{3,2,1,0:T(8,128)S(1)} %copy-done.56), channel_id=1, source_target_pairs={{0,3},{1,4},{2,5},{3,6},{4,7},{5,8},{6,9},{7,10},{8,11},{9,12},{10... | collective-permute-start | bytes 393224 | tf_op jit(solution)/shard_map/ppermute | solution.py:556
  694.2 60.4 %collective-permute-start.70 = (f32[1,2,128,128]{3,2,1,0:T(8,128)S(1)}, f32[1,2,128,128]{3,2,1,0:T(8,128)}, u32[]{:S(2)}, u32[]{:S(2)}) collective-permute-start(f32[1,2,128,128]{3,2,1,0:T(8,128)S(1)} %copy-done.53), channel_id=1, source_target_pairs={{0,4},{1,5},{2,6},{3,7},{4,8},{5,9},{6,10},{7,11},{8,12},{9,13},{1... | collective-permute-start | bytes 393224 | tf_op jit(solution)/shard_map/ppermute | solution.py:556
  695.6 59.1 %collective-permute-start.71 = (f32[1,2,128,128]{3,2,1,0:T(8,128)S(1)}, f32[1,2,128,128]{3,2,1,0:T(8,128)}, u32[]{:S(2)}, u32[]{:S(2)}) collective-permute-start(f32[1,2,128,128]{3,2,1,0:T(8,128)S(1)} %copy-done.50), channel_id=1, source_target_pairs={{0,5},{1,6},{2,7},{3,8},{4,9},{5,10},{6,11},{7,12},{8,13},{9,14},{... | collective-permute-start | bytes 393224 | tf_op jit(solution)/shard_map/ppermute | solution.py:556
  834.1 208.4 %all-to-all-start.4 = ((f32[16,2,2,80,128]{4,3,2,1,0:T(8,128)}), f32[16,2,2,80,128]{4,3,2,1,0:T(8,128)}, u32[]{:S(2)}, u32[]{:S(2)}) async-start(f32[16,2,2,80,128]{4,3,2,1,0:T(8,128)} %get-tuple-element.344), calls=%async_computation.4 | async-start | bytes 5242880 | tf_op jit(solution)/shard_map/all_to_all | solution.py:585
  846.2 50.7 %collective-permute-start.100 = (f32[1,2,128,128]{3,2,1,0:T(8,128)S(1)}, f32[1,2,128,128]{3,2,1,0:T(8,128)}, u32[]{:S(2)}, u32[]{:S(2)}) collective-permute-start(f32[1,2,128,128]{3,2,1,0:T(8,128)S(1)} %copy-done.63), channel_id=1, source_target_pairs={{0,4},{1,5},{2,6},{3,7},{4,8},{5,9},{6,10},{7,11},{8,12},{9,13},{1... | collective-permute-start | bytes 393224 | tf_op jit(solution)/shard_map/ppermute | solution.py:556
  848.1 67.2 %collective-permute-start.101 = (f32[1,2,128,128]{3,2,1,0:T(8,128)S(1)}, f32[1,2,128,128]{3,2,1,0:T(8,128)}, u32[]{:S(2)}, u32[]{:S(2)}) collective-permute-start(f32[1,2,128,128]{3,2,1,0:T(8,128)S(1)} %copy-done.60), channel_id=1, source_target_pairs={{0,5},{1,6},{2,7},{3,8},{4,9},{5,10},{6,11},{7,12},{8,13},{9,14},{... | collective-permute-start | bytes 393224 | tf_op jit(solution)/shard_map/ppermute | solution.py:556
  849.0 66.3 %collective-permute-start.102 = (f32[1,2,128,128]{3,2,1,0:T(8,128)S(1)}, f32[1,2,128,128]{3,2,1,0:T(8,128)}, u32[]{:S(2)}, u32[]{:S(2)}) collective-permute-start(f32[1,2,128,128]{3,2,1,0:T(8,128)S(1)} %copy-done.57), channel_id=1, source_target_pairs={{0,11},{1,12},{2,13},{3,14},{4,15},{5,0},{6,1},{7,2},{8,3},{9,4},{... | collective-permute-start | bytes 393224 | tf_op jit(solution)/shard_map/ppermute | solution.py:556
  851.7 64.2 %collective-permute-start.103 = (f32[1,2,128,128]{3,2,1,0:T(8,128)S(1)}, f32[1,2,128,128]{3,2,1,0:T(8,128)}, u32[]{:S(2)}, u32[]{:S(2)}) collective-permute-start(f32[1,2,128,128]{3,2,1,0:T(8,128)S(1)} %copy-done.54), channel_id=1, source_target_pairs={{0,12},{1,13},{2,14},{3,15},{4,0},{5,1},{6,2},{7,3},{8,4},{9,5},{1... | collective-permute-start | bytes 393224 | tf_op jit(solution)/shard_map/ppermute | solution.py:556
  853.6 64.6 %collective-permute-start.104 = (f32[1,2,128,128]{3,2,1,0:T(8,128)S(1)}, f32[1,2,128,128]{3,2,1,0:T(8,128)}, u32[]{:S(2)}, u32[]{:S(2)}) collective-permute-start(f32[1,2,128,128]{3,2,1,0:T(8,128)S(1)} %copy-done.51), channel_id=1, source_target_pairs={{0,13},{1,14},{2,15},{3,0},{4,1},{5,2},{6,3},{7,4},{8,5},{9,6},{10... | collective-permute-start | bytes 393224 | tf_op jit(solution)/shard_map/ppermute | solution.py:556
  994.0 48.5 %collective-permute-start.107 = (f32[128,4096]{1,0:T(8,128)}, f32[128,4096]{1,0:T(8,128)}, u32[]{:S(2)}, u32[]{:S(2)}) collective-permute-start(f32[128,4096]{1,0:T(8,128)} %shard_map.126.own), channel_id=1, source_target_pairs={{0,16},{16,0},{1,17},{17,1},{2,18},{18,2},{3,19},{19,3},{4,20},{20... | collective-permute-start | bytes 6291464 | tf_op jit(solution)/shard_map/ppermute | solution.py:25
  (157 other events, 7694.8 us)

commit v7 on v6

--- a/solution.py
+++ b/solution.py
@@ -548,12 +548,14 @@
     return min(distance, count - distance) * 3 <= count
 
 
-def ringed(blocks):
+def ringed(blocks, which=(False, True)):
     count = lax.axis_size("slab")
-    moved = [blocks[0]]
+    moved = list(blocks)
     for n in range(1, count):
+        if is_light(n, count) not in which:
+            continue
         pairs = [(source, (source + n) % count) for source in range(count)]
-        moved.append(lax.ppermute(blocks[n], "slab", pairs))
+        moved[n] = lax.ppermute(blocks[n], "slab", pairs)
     return moved
 
 
@@ -807,16 +809,19 @@
         near = ringed(sent[1][:slabs])
         if step_index == 0:
             sums = past_sums()
-        else:
-            scalars = ticked(scalars)
+        scalars = ticked(scalars)
         near, far, sums = after_first(near, (sent[1][slabs], sums))
         far = exchanged(far)
         outs = spectral(0, ring, near, sums[step_index], past[0], pieces, None)
         if step_index == 0:
             past[0] = outs[-1]
         late = outs[slabs : slabs + len(pieces) - 1]
-        back = ringed(outs[:slabs])
-        far, late = hold((far, list(late)))
+        back = ringed(outs[:slabs], (True,))
+        long = [n for n in range(1, slabs) if not is_light(n, slabs)]
+        far, late, rest = hold((far, list(late), [back[n] for n in long]))
+        for n, value in zip(long, rest):
+            back[n] = value
+        back = ringed(back, (False,))
         outs = spectral(1, ring, [far], sums[step_index], past[1], pieces, late)
         if step_index == 0:
             past[1] = outs[-1]
@@ -827,12 +832,14 @@
         waiting = exchanged(late[0])
         own = inverse(*back, *more)
         other = swapped(own, "side", 0)
-        if not last:
+        if last:
+            scalars = ticked(scalars)
+        else:
             sent[0], states[0] = middle(scalars, 0, own, other, states[0])
         if not last:
             waiting, sent[0], states[0] = hold((waiting, sent[0], states[0]))
             continue
-        waiting, own, other, final = hold((waiting, own, other, late[1]))
+        waiting, scalars, final = hold((waiting, scalars, late[1]))
         final = exchanged(final)
         own_near = inverse(waiting)
         other_near = swapped(own_near, "side", 0)

time: 1120 us -> 1140 us (1.018)
  starting transfers between devices: 298 us -> 318 us
    all_to_all x6, waiting for transfers between devices: 5.69 us -> 46.2 us  [exchanged(): lax.all_to_all(value, 'slab', split_axis=0, concat_axis=0, tiled=True)]
    ppermute x105, waiting for transfers between devices: 380 us -> 347 us  [ringed(): moved[n] = lax.ppermute(blocks[n], 'slab', pairs)]
    ppermute x105, starting transfers between devices: 240 us -> 252 us  [ringed(): moved[n] = lax.ppermute(blocks[n], 'slab', pairs)]
    ppermute x5, waiting for transfers between devices: 143 us -> 131 us  [swapped(): return lax.ppermute(value, axis, pairs)]
  transfers between devices with their start and end apart: 116 -> 116, of which waited for: 48 -> 52; matrix products, arithmetic and copies ran while one was open for 0% -> 0% of each run, Pallas kernels for 19% -> 19%
where the time goes in v7:
time: 1140 us; the launch traced here: 1130 us
  waiting for transfers between devices  524 us (46%)
  starting transfers between devices  318 us (28%)
  Pallas kernels  281 us (25%)
    ppermute x105, waiting for transfers between devices, ringed(): moved[n] = lax.ppermute(blocks[n], 'slab', pairs)  347 us
    ppermute x105, starting transfers between devices, ringed(): moved[n] = lax.ppermute(blocks[n], 'slab', pairs)  252 us
    ppermute x5, waiting for transfers between devices, swapped(): return lax.ppermute(value, axis, pairs)  131 us
    pallas_call x4, Pallas kernels, spectral(): pl.pallas_call(functools.partial(spectral_kernel, (len(ring), len(near)),...  99.4 us
    all_to_all x6, starting transfers between devices, exchanged(): lax.all_to_all(value, 'slab', split_axis=0, concat_axis=0, tiled=True)  59.6 us
    pallas_call x5, Pallas kernels, inverse(): pl.pallas_call(functools.partial(inverse_kernel, len(blocks)), out_shape=...  52.8 us
    pallas_call x2, Pallas kernels, middle(): pl.pallas_call(middle_kernel, out_shape=shapes + [rows_shape], grid=(1,),...  46.4 us
    all_to_all x6, waiting for transfers between devices, exchanged(): lax.all_to_all(value, 'slab', split_axis=0, concat_axis=0, tiled=True)  46.2 us
  transfers between devices with their start and end apart: 116, of which 52 were waited for; matrix products, arithmetic and copies ran while one was open for 0% of the time, Pallas kernels for 19%

profile of v7, /device:TPU:0, one launch (start us, length us, event | category | flops | bytes accessed | tf_op | source)
XLA Modules:
  0.0 1132.2 jit_solution(16160915282358054477)
XLA Ops:
  22.4 24.8 %shard_map.114 = (f32[2,256,4096]{2,1,0:T(8,128)}, f32[2,256,4096]{2,1,0:T(8,128)}) custom-call(bf16[1,9,256,4096]{3,2,1,0:T(8,128)(2,1)} %refs_8_.1, bf16[1,8,2,256,4096]{4,3,2,1,0:T(8,128)(2,1)} %history.1), custom_call_target="tpu_custom_call" | custom-call | tf_op jit(solution)/shard_map/pallas_call | solution.py:704
  57.8 36.2 %collective-permute-done.20.refs_18_ = f32[1,2,128,128]{3,2,1,0:T(8,128)} collective-permute-done((f32[1,2,128,128]{3,2,1,0:T(8,128)S(1)}, f32[1,2,128,128]{3,2,1,0:T(8,128)}, u32[]{:S(2)}, u32[]{:S(2)}) %collective-permute-start.20) | collective-permute-done | bytes 131104 | tf_op jit(solution)/shard_map/ppermute | solution.py:558
  95.1 18.0 %collective-permute-start.26 = (f32[1,2,128,128]{3,2,1,0:T(8,128)}, f32[1,2,128,128]{3,2,1,0:T(8,128)}, u32[]{:S(2)}, u32[]{:S(2)}) collective-permute-start(f32[1,2,128,128]{3,2,1,0:T(8,128)} %get-tuple-element.262), channel_id=1, source_target_pairs={{0,12},{1,13},{2,14},{3,15},{4,0},{5,1},{6,2},{7,3},{8,4},{9,5},{1... | collective-permute-start | bytes 393224 | tf_op jit(solution)/shard_map/ppermute | solution.py:558
  121.0 12.7 %shard_map.112 = (f32[2,2,128,128]{3,2,1,0:T(8,128)}, f32[2,2,128,128]{3,2,1,0:T(8,128)}, f32[2,2,128,128]{3,2,1,0:T(8,128)}, f32[2,2,128,128]{3,2,1,0:T(8,128)}...) custom-call(s32[1]{0:T(128)} %bitcast.place.refs_0_, ...), custom_call_target="tpu_custom_call" | custom-call | tf_op jit(solution)/shard_map/pallas_call | solution.py:641
  151.3 19.6 %collective-permute-start.3 = (f32[2,2,128,128]{3,2,1,0:T(8,128)}, f32[2,2,128,128]{3,2,1,0:T(8,128)}, u32[]{:S(2)}, u32[]{:S(2)}) collective-permute-start(f32[2,2,128,128]{3,2,1,0:T(8,128)} %get-tuple-element.212), channel_id=1, source_target_pairs={{0,4},{1,5},{2,6},{3,7},{4,8},{5,9},{6,10},{7,11},{8,12},{9,13},{1... | collective-permute-start | bytes 786440 | tf_op jit(solution)/shard_map/ppermute | solution.py:558
  182.2 27.1 %collective-permute-done.4.refs_6_ = f32[2,2,128,128]{3,2,1,0:T(8,128)} collective-permute-done((f32[2,2,128,128]{3,2,1,0:T(8,128)}, f32[2,2,128,128]{3,2,1,0:T(8,128)}, u32[]{:S(2)}, u32[]{:S(2)}) %collective-permute-start.4) | collective-permute-done | bytes 262176 | tf_op jit(solution)/shard_map/ppermute | solution.py:558
  231.8 24.5 %shard_map.115 = (f32[1,2,128,128]{3,2,1,0:T(8,128)}, f32[1,2,128,128]{3,2,1,0:T(8,128)}, f32[1,2,128,128]{3,2,1,0:T(8,128)}, f32[1,2,128,128]{3,2,1,0:T(8,128)}...) custom-call(s32[1]{0:T(128)} %bitcast.place.refs_0_, ...), custom_call_target="tpu_custom_call" | custom-call | tf_op jit(solution)/shard_map/pallas_call | solution.py:756
  256.3 24.8 %shard_map.116 = (f32[1,2,128,128]{3,2,1,0:T(8,128)}, f32[1,2,128,128]{3,2,1,0:T(8,128)}, f32[1,2,128,128]{3,2,1,0:T(8,128)}, f32[1,2,128,128]{3,2,1,0:T(8,128)}...) custom-call(s32[1]{0:T(128)} %bitcast.place.refs_0_, ...), custom_call_target="tpu_custom_call", output_to_operand_aliasing={{16}: (23, {})} | custom-call | tf_op jit(solution)/shard_map/pallas_call | solution.py:756
  319.4 69.9 %collective-permute-done.35.refs_1_ = f32[1,2,128,128]{3,2,1,0:T(8,128)} collective-permute-done((f32[1,2,128,128]{3,2,1,0:T(8,128)S(1)}, f32[1,2,128,128]{3,2,1,0:T(8,128)}, u32[]{:S(2)}, u32[]{:S(2)}) %collective-permute-start.35) | collective-permute-done | bytes 131104 | tf_op jit(solution)/shard_map/ppermute | solution.py:558
  390.4 29.2 %collective-permute-start.46 = (f32[1,2,128,128]{3,2,1,0:T(8,128)S(1)}, f32[1,2,128,128]{3,2,1,0:T(8,128)}, u32[]{:S(2)}, u32[]{:S(2)}) collective-permute-start(f32[1,2,128,128]{3,2,1,0:T(8,128)S(1)} %copy-done.32), channel_id=1, source_target_pairs={{0,12},{1,13},{2,14},{3,15},{4,0},{5,1},{6,2},{7,3},{8,4},{9,5},{1... | collective-permute-start | bytes 393224 | tf_op jit(solution)/shard_map/ppermute | solution.py:558
  497.8 36.1 %collective-permute-done.60.other = f32[128,4096]{1,0:T(8,128)} collective-permute-done((f32[128,4096]{1,0:T(8,128)}, f32[128,4096]{1,0:T(8,128)}, u32[]{:S(2)}, u32[]{:S(2)}) %collective-permute-start.60) | collective-permute-done | bytes 2097184 | tf_op jit(solution)/shard_map/ppermute | solution.py:25
  533.9 22.8 %shard_map.120 = (f32[16,2,2,128,128]{4,3,2,1,0:T(8,128)}, f32[128,4096]{1,0:T(8,128)}) custom-call(s32[1]{0:T(128)} %bitcast.place.refs_0_, f32[5]{0:T(128)} %shard_map.118.scalars.before, f32[128,4096]{1,0:T(8,128)} %shard_map.119.own, f32[128,4096]{1,0:T(8,128)} %collective-permute-done.60.other, f32[256,4096]{1,0:T(8,128)} %prestress.9, ...), custom_call_target="tpu_custom_call" | custom-call | tf_op jit(solution)/shard_map/pallas_call | solution.py:658
  580.8 46.7 %collective-permute-done.61.other = f32[128,4096]{1,0:T(8,128)} collective-permute-done((f32[128,4096]{1,0:T(8,128)}, f32[128,4096]{1,0:T(8,128)}, u32[]{:S(2)}, u32[]{:S(2)}) %collective-permute-start.61) | collective-permute-done | bytes 2097184 | tf_op jit(solution)/shard_map/ppermute | solution.py:25
  627.5 23.6 %shard_map.122 = (f32[1,2,128,128]{3,2,1,0:T(8,128)}, f32[1,2,128,128]{3,2,1,0:T(8,128)}, f32[1,2,128,128]{3,2,1,0:T(8,128)}, f32[1,2,128,128]{3,2,1,0:T(8,128)}...) custom-call(s32[1]{0:T(128)} %bitcast.place.refs_0_, ...), custom_call_target="tpu_custom_call" | custom-call | tf_op jit(solution)/shard_map/pallas_call | solution.py:658
  659.9 16.1 %collective-permute-done.62.refs_8_ = f32[1,2,128,128]{3,2,1,0:T(8,128)} collective-permute-done((f32[1,2,128,128]{3,2,1,0:T(8,128)}, f32[1,2,128,128]{3,2,1,0:T(8,128)}, u32[]{:S(2)}, u32[]{:S(2)}) %collective-permute-start.62) | collective-permute-done | bytes 131104 | tf_op jit(solution)/shard_map/ppermute | solution.py:558
  695.5 36.2 %collective-permute-done.67.refs_3_ = f32[1,2,128,128]{3,2,1,0:T(8,128)} collective-permute-done((f32[1,2,128,128]{3,2,1,0:T(8,128)S(1)}, f32[1,2,128,128]{3,2,1,0:T(8,128)}, u32[]{:S(2)}, u32[]{:S(2)}) %collective-permute-start.67) | collective-permute-done | bytes 131104 | tf_op jit(solution)/shard_map/ppermute | solution.py:558
  732.9 18.0 %collective-permute-start.73 = (f32[1,2,128,128]{3,2,1,0:T(8,128)S(1)}, f32[1,2,128,128]{3,2,1,0:T(8,128)}, u32[]{:S(2)}, u32[]{:S(2)}) collective-permute-start(f32[1,2,128,128]{3,2,1,0:T(8,128)S(1)} %copy-done.49), channel_id=1, source_target_pairs={{0,12},{1,13},{2,14},{3,15},{4,0},{5,1},{6,2},{7,3},{8,4},{9,5},{1... | collective-permute-start | bytes 393224 | tf_op jit(solution)/shard_map/ppermute | solution.py:558
  761.8 25.0 %shard_map.123 = (f32[1,2,128,128]{3,2,1,0:T(8,128)}, f32[1,2,128,128]{3,2,1,0:T(8,128)}, f32[1,2,128,128]{3,2,1,0:T(8,128)}, f32[1,2,128,128]{3,2,1,0:T(8,128)}...) custom-call(s32[1]{0:T(128)} %bitcast.place.refs_0_, ...), custom_call_target="tpu_custom_call" | custom-call | tf_op jit(solution)/shard_map/pallas_call | solution.py:756
  786.8 25.1 %shard_map.124 = (f32[1,2,128,128]{3,2,1,0:T(8,128)}, f32[1,2,128,128]{3,2,1,0:T(8,128)}, f32[1,2,128,128]{3,2,1,0:T(8,128)}, f32[1,2,128,128]{3,2,1,0:T(8,128)}...) custom-call(s32[1]{0:T(128)} %bitcast.place.refs_0_, ...), custom_call_target="tpu_custom_call", output_to_operand_aliasing={{16}: (10, {}), {17}: (11, {})} | custom-call | tf_op jit(solution)/shard_map/pallas_call | solution.py:756
  849.6 46.2 %all-to-all-done.4.refs_0_ = f32[16,2,2,80,128]{4,3,2,1,0:T(8,128)} async-done(((f32[16,2,2,80,128]{4,3,2,1,0:T(8,128)}), f32[16,2,2,80,128]{4,3,2,1,0:T(8,128)}, u32[]{:S(2)}, u32[]{:S(2)}) %all-to-all-start.4) | async-done | bytes 2621472 | tf_op jit(solution)/shard_map/all_to_all | solution.py:587
  895.8 13.4 %all-to-all-start.5 = ((f32[16,2,2,48,128]{4,3,2,1,0:T(8,128)}), f32[16,2,2,48,128]{4,3,2,1,0:T(8,128)}, u32[]{:S(2)}, u32[]{:S(2)}) async-start(f32[16,2,2,48,128]{4,3,2,1,0:T(8,128)} %get-tuple-element.366), calls=%async_computation.5 | async-start | bytes 3145728 | tf_op jit(solution)/shard_map/all_to_all | solution.py:587
  916.6 26.4 %collective-permute-done.100.refs_20_ = f32[1,2,128,128]{3,2,1,0:T(8,128)} collective-permute-done((f32[1,2,128,128]{3,2,1,0:T(8,128)S(1)}, f32[1,2,128,128]{3,2,1,0:T(8,128)}, u32[]{:S(2)}, u32[]{:S(2)}) %collective-permute-start.100) | collective-permute-done | bytes 131104 | tf_op jit(solution)/shard_map/ppermute | solution.py:558
  1047.2 37.1 %collective-permute-done.107.other = f32[128,4096]{1,0:T(8,128)} collective-permute-done((f32[128,4096]{1,0:T(8,128)}, f32[128,4096]{1,0:T(8,128)}, u32[]{:S(2)}, u32[]{:S(2)}) %collective-permute-start.107) | collective-permute-done | bytes 2097184 | tf_op jit(solution)/shard_map/ppermute | solution.py:25
  1084.3 12.5 %shard_map.130 = (f32[1,256,4096]{2,1,0:T(8,128)}, f32[256,4096]{1,0:T(8,128)}, f32[256,4096]{1,0:T(8,128)}) custom-call(f32[5]{0:T(128)} %shard_map.127.scalars, f32[128,4096]{1,0:T(8,128)} %shard_map.129.own, f32[128,4096]{1,0:T(8,128)} %collective-permute-done.107.other, f32[256,4096]{1,0:T(8,128)} %prestress.9, f32[256,4096]{1,0:T(8,128)} %strength.9, ...), custom_call_target="tpu_custom_call" | custom-call | tf_op jit(solution)/shard_map/pallas_call | solution.py:690
  (365 shorter events, 453.4 us)
Async XLA Ops:
  47.3 209.0 %all-to-all-start = ((f32[16,1,2,128,128]{4,3,2,1,0:T(8,128)}), f32[16,1,2,128,128]{4,3,2,1,0:T(8,128)}, u32[]{:S(2)}, u32[]{:S(2)}) async-start(f32[16,1,2,128,128]{4,3,2,1,0:T(8,128)} %get-tuple-element.249), calls=%async_computation | async-start | bytes 4194304 | tf_op jit(solution)/shard_map/all_to_all | solution.py:587
  53.8 59.3 %collective-permute-start.22 = (f32[1,2,128,128]{3,2,1,0:T(8,128)S(1)}, f32[1,2,128,128]{3,2,1,0:T(8,128)}, u32[]{:S(2)}, u32[]{:S(2)}) collective-permute-start(f32[1,2,128,128]{3,2,1,0:T(8,128)S(1)} %copy-done.60), channel_id=1, source_target_pairs={{0,3},{1,4},{2,5},{3,6},{4,7},{5,8},{6,9},{7,10},{8,11},{9,12},{10... | collective-permute-start | bytes 393224 | tf_op jit(solution)/shard_map/ppermute | solution.py:558
  56.1 60.4 %collective-permute-start.23 = (f32[1,2,128,128]{3,2,1,0:T(8,128)S(1)}, f32[1,2,128,128]{3,2,1,0:T(8,128)}, u32[]{:S(2)}, u32[]{:S(2)}) collective-permute-start(f32[1,2,128,128]{3,2,1,0:T(8,128)S(1)} %copy-done.57), channel_id=1, source_target_pairs={{0,4},{1,5},{2,6},{3,7},{4,8},{5,9},{6,10},{7,11},{8,12},{9,13},{1... | collective-permute-start | bytes 393224 | tf_op jit(solution)/shard_map/ppermute | solution.py:558
  57.6 59.1 %collective-permute-start.24 = (f32[1,2,128,128]{3,2,1,0:T(8,128)S(1)}, f32[1,2,128,128]{3,2,1,0:T(8,128)}, u32[]{:S(2)}, u32[]{:S(2)}) collective-permute-start(f32[1,2,128,128]{3,2,1,0:T(8,128)S(1)} %copy-done.54), channel_id=1, source_target_pairs={{0,5},{1,6},{2,7},{3,8},{4,9},{5,10},{6,11},{7,12},{8,13},{9,14},{... | collective-permute-start | bytes 393224 | tf_op jit(solution)/shard_map/ppermute | solution.py:558
  174.9 45.7 %collective-permute-start.6 = (f32[2,2,128,128]{3,2,1,0:T(8,128)}, f32[2,2,128,128]{3,2,1,0:T(8,128)}, u32[]{:S(2)}, u32[]{:S(2)}) collective-permute-start(f32[2,2,128,128]{3,2,1,0:T(8,128)} %get-tuple-element.215), channel_id=1, source_target_pairs={{0,7},{1,8},{2,9},{3,10},{4,11},{5,12},{6,13},{7,14},{8,15},{9,0},... | collective-permute-start | bytes 786440 | tf_op jit(solution)/shard_map/ppermute | solution.py:558
  175.9 44.8 %collective-permute-start.7 = (f32[2,2,128,128]{3,2,1,0:T(8,128)}, f32[2,2,128,128]{3,2,1,0:T(8,128)}, u32[]{:S(2)}, u32[]{:S(2)}) collective-permute-start(f32[2,2,128,128]{3,2,1,0:T(8,128)} %get-tuple-element.216), channel_id=1, source_target_pairs={{0,8},{1,9},{2,10},{3,11},{4,12},{5,13},{6,14},{7,15},{8,0},{9,1},... | collective-permute-start | bytes 786440 | tf_op jit(solution)/shard_map/ppermute | solution.py:558
  305.1 251.6 %all-to-all-start.1 = ((f32[16,2,2,128,128]{4,3,2,1,0:T(8,128)}), f32[16,2,2,128,128]{4,3,2,1,0:T(8,128)}, u32[]{:S(2)}, u32[]{:S(2)}) async-start(f32[16,2,2,128,128]{4,3,2,1,0:T(8,128)} %get-tuple-element.282), calls=%async_computation.1 | async-start | bytes 8388608 | tf_op jit(solution)/shard_map/all_to_all | solution.py:587
  313.5 75.8 %collective-permute-start.35 = (f32[1,2,128,128]{3,2,1,0:T(8,128)S(1)}, f32[1,2,128,128]{3,2,1,0:T(8,128)}, u32[]{:S(2)}, u32[]{:S(2)}) collective-permute-start(f32[1,2,128,128]{3,2,1,0:T(8,128)S(1)} %copy-done.43), channel_id=1, source_target_pairs={{0,1},{1,2},{2,3},{3,4},{4,5},{5,6},{6,7},{7,8},{8,9},{9,10},{10,1... | collective-permute-start | bytes 393224 | tf_op jit(solution)/shard_map/ppermute | solution.py:558
  313.9 76.6 %collective-permute-start.36 = (f32[1,2,128,128]{3,2,1,0:T(8,128)S(1)}, f32[1,2,128,128]{3,2,1,0:T(8,128)}, u32[]{:S(2)}, u32[]{:S(2)}) collective-permute-start(f32[1,2,128,128]{3,2,1,0:T(8,128)S(1)} %copy-done.41), channel_id=1, source_target_pairs={{0,2},{1,3},{2,4},{3,5},{4,6},{5,7},{6,8},{7,9},{8,10},{9,11},{10,... | collective-permute-start | bytes 393224 | tf_op jit(solution)/shard_map/ppermute | solution.py:558
  316.6 103.0 %collective-permute-start.37 = (f32[1,2,128,128]{3,2,1,0:T(8,128)S(1)}, f32[1,2,128,128]{3,2,1,0:T(8,128)}, u32[]{:S(2)}, u32[]{:S(2)}) collective-permute-start(f32[1,2,128,128]{3,2,1,0:T(8,128)S(1)} %copy-done.39), channel_id=1, source_target_pairs={{0,3},{1,4},{2,5},{3,6},{4,7},{5,8},{6,9},{7,10},{8,11},{9,12},{10... | collective-permute-start | bytes 393224 | tf_op jit(solution)/shard_map/ppermute | solution.py:558
  317.8 105.2 %collective-permute-start.38 = (f32[1,2,128,128]{3,2,1,0:T(8,128)S(1)}, f32[1,2,128,128]{3,2,1,0:T(8,128)}, u32[]{:S(2)}, u32[]{:S(2)}) collective-permute-start(f32[1,2,128,128]{3,2,1,0:T(8,128)S(1)} %copy-done.37), channel_id=1, source_target_pairs={{0,4},{1,5},{2,6},{3,7},{4,8},{5,9},{6,10},{7,11},{8,12},{9,13},{1... | collective-permute-start | bytes 393224 | tf_op jit(solution)/shard_map/ppermute | solution.py:558
  319.2 104.1 %collective-permute-start.39 = (f32[1,2,128,128]{3,2,1,0:T(8,128)S(1)}, f32[1,2,128,128]{3,2,1,0:T(8,128)}, u32[]{:S(2)}, u32[]{:S(2)}) collective-permute-start(f32[1,2,128,128]{3,2,1,0:T(8,128)S(1)} %copy-done.35), channel_id=1, source_target_pairs={{0,5},{1,6},{2,7},{3,8},{4,9},{5,10},{6,11},{7,12},{8,13},{9,14},{... | collective-permute-start | bytes 393224 | tf_op jit(solution)/shard_map/ppermute | solution.py:558
  486.7 47.2 %collective-permute-start.60 = (f32[128,4096]{1,0:T(8,128)}, f32[128,4096]{1,0:T(8,128)}, u32[]{:S(2)}, u32[]{:S(2)}) collective-permute-start(f32[128,4096]{1,0:T(8,128)} %shard_map.119.own), channel_id=1, source_target_pairs={{0,16},{16,0},{1,17},{17,1},{2,18},{18,2},{3,19},{19,3},{4,20},{20... | collective-permute-start | bytes 6291464 | tf_op jit(solution)/shard_map/ppermute | solution.py:25
  556.7 122.7 %all-to-all-start.2 = ((f32[16,2,2,128,128]{4,3,2,1,0:T(8,128)}), f32[16,2,2,128,128]{4,3,2,1,0:T(8,128)}, u32[]{:S(2)}, u32[]{:S(2)}) async-start(f32[16,2,2,128,128]{4,3,2,1,0:T(8,128)} %get-tuple-element.317), calls=%async_computation.2 | async-start | bytes 8388608 | tf_op jit(solution)/shard_map/all_to_all | solution.py:587
  579.3 48.2 %collective-permute-start.61 = (f32[128,4096]{1,0:T(8,128)}, f32[128,4096]{1,0:T(8,128)}, u32[]{:S(2)}, u32[]{:S(2)}) collective-permute-start(f32[128,4096]{1,0:T(8,128)} %shard_map.121.own), channel_id=1, source_target_pairs={{0,16},{16,0},{1,17},{17,1},{2,18},{18,2},{3,19},{19,3},{4,20},{20... | collective-permute-start | bytes 6291464 | tf_op jit(solution)/shard_map/ppermute | solution.py:25
  679.4 107.4 %all-to-all-start.3 = ((f32[16,1,2,128,128]{4,3,2,1,0:T(8,128)}), f32[16,1,2,128,128]{4,3,2,1,0:T(8,128)}, u32[]{:S(2)}, u32[]{:S(2)}) async-start(f32[16,1,2,128,128]{4,3,2,1,0:T(8,128)} %get-tuple-element.326), calls=%async_computation.3 | async-start | bytes 4194304 | tf_op jit(solution)/shard_map/all_to_all | solution.py:587
  691.7 59.3 %collective-permute-start.69 = (f32[1,2,128,128]{3,2,1,0:T(8,128)S(1)}, f32[1,2,128,128]{3,2,1,0:T(8,128)}, u32[]{:S(2)}, u32[]{:S(2)}) collective-permute-start(f32[1,2,128,128]{3,2,1,0:T(8,128)S(1)} %copy-done.59), channel_id=1, source_target_pairs={{0,3},{1,4},{2,5},{3,6},{4,7},{5,8},{6,9},{7,10},{8,11},{9,12},{10... | collective-permute-start | bytes 393224 | tf_op jit(solution)/shard_map/ppermute | solution.py:558
  693.9 60.4 %collective-permute-start.70 = (f32[1,2,128,128]{3,2,1,0:T(8,128)S(1)}, f32[1,2,128,128]{3,2,1,0:T(8,128)}, u32[]{:S(2)}, u32[]{:S(2)}) collective-permute-start(f32[1,2,128,128]{3,2,1,0:T(8,128)S(1)} %copy-done.56), channel_id=1, source_target_pairs={{0,4},{1,5},{2,6},{3,7},{4,8},{5,9},{6,10},{7,11},{8,12},{9,13},{1... | collective-permute-start | bytes 393224 | tf_op jit(solution)/shard_map/ppermute | solution.py:558
  695.4 59.1 %collective-permute-start.71 = (f32[1,2,128,128]{3,2,1,0:T(8,128)S(1)}, f32[1,2,128,128]{3,2,1,0:T(8,128)}, u32[]{:S(2)}, u32[]{:S(2)}) collective-permute-start(f32[1,2,128,128]{3,2,1,0:T(8,128)S(1)} %copy-done.53), channel_id=1, source_target_pairs={{0,5},{1,6},{2,7},{3,8},{4,9},{5,10},{6,11},{7,12},{8,13},{9,14},{... | collective-permute-start | bytes 393224 | tf_op jit(solution)/shard_map/ppermute | solution.py:558
  833.7 62.1 %all-to-all-start.4 = ((f32[16,2,2,80,128]{4,3,2,1,0:T(8,128)}), f32[16,2,2,80,128]{4,3,2,1,0:T(8,128)}, u32[]{:S(2)}, u32[]{:S(2)}) async-start(f32[16,2,2,80,128]{4,3,2,1,0:T(8,128)} %get-tuple-element.363), calls=%async_computation.4 | async-start | bytes 5242880 | tf_op jit(solution)/shard_map/all_to_all | solution.py:587
  895.8 201.1 %all-to-all-start.5 = ((f32[16,2,2,48,128]{4,3,2,1,0:T(8,128)}), f32[16,2,2,48,128]{4,3,2,1,0:T(8,128)}, u32[]{:S(2)}, u32[]{:S(2)}) async-start(f32[16,2,2,48,128]{4,3,2,1,0:T(8,128)} %get-tuple-element.366), calls=%async_computation.5 | async-start | bytes 3145728 | tf_op jit(solution)/shard_map/all_to_all | solution.py:587
  911.1 44.7 %collective-permute-start.101 = (f32[1,2,128,128]{3,2,1,0:T(8,128)S(1)}, f32[1,2,128,128]{3,2,1,0:T(8,128)}, u32[]{:S(2)}, u32[]{:S(2)}) collective-permute-start(f32[1,2,128,128]{3,2,1,0:T(8,128)S(1)} %copy-done.55), channel_id=1, source_target_pairs={{0,5},{1,6},{2,7},{3,8},{4,9},{5,10},{6,11},{7,12},{8,13},{9,14},{... | collective-permute-start | bytes 393224 | tf_op jit(solution)/shard_map/ppermute | solution.py:558
  1035.4 48.9 %collective-permute-start.107 = (f32[128,4096]{1,0:T(8,128)}, f32[128,4096]{1,0:T(8,128)}, u32[]{:S(2)}, u32[]{:S(2)}) collective-permute-start(f32[128,4096]{1,0:T(8,128)} %shard_map.129.own), channel_id=1, source_target_pairs={{0,16},{16,0},{1,17},{17,1},{2,18},{18,2},{3,19},{19,3},{4,20},{20... | collective-permute-start | bytes 6291464 | tf_op jit(solution)/shard_map/ppermute | solution.py:25
  1046.7 65.7 %collective-permute-start.109 = (f32[80,4096]{1,0:T(8,128)}, f32[80,4096]{1,0:T(8,128)}, u32[]{:S(2)}, u32[]{:S(2)}) collective-permute-start(f32[80,4096]{1,0:T(8,128)} %shard_map.128.own), channel_id=1, source_target_pairs={{0,16},{16,0},{1,17},{17,1},{2,18},{18,2},{3,19},{19,3},{4,20},{20... | collective-permute-start | bytes 3932168 | tf_op jit(solution)/shard_map/ppermute | solution.py:25
  (157 other events, 8433.8 us)

commit v8 on v7

--- a/solution.py
+++ b/solution.py
@@ -411,8 +411,20 @@
     outs, rest = rest[: len(pieces)], rest[len(pieces) :]
     if not has_past:
         spec_out = rest.pop(0)
-    held, turned, total, spread = rest
+    held, turned, total, spread, sum_held, lag_held, spec_held, sems = rest
     rows = 128
+    own_rows = pl.ds(half * rows, rows)
+    copies = [
+        pltpu.make_async_copy(past_sum.at[:, own_rows, :], sum_held, sems.at[0]),
+        pltpu.make_async_copy(kernel_now.at[0, 0, own_rows, :], lag_held.at[0], sems.at[1]),
+    ]
+    if has_past:
+        copies += [
+            pltpu.make_async_copy(kernel_past.at[0, 1, own_rows, :], lag_held.at[1], sems.at[2]),
+            pltpu.make_async_copy(spec_past, spec_held, sems.at[3]),
+        ]
+    for copy in copies:
+        copy.start()
     inner = RADIX * 16
     length = total.shape[2]
 
@@ -443,22 +455,28 @@
 
     lax.fori_loop(0, RADIX // 2, wave, 0)
 
+    for copy in copies:
+        copy.wait()
+
     def convolve(b, carry):
         cols = pl.ds(pl.multiple_of(b * 256, 256), 256)
-        weight = kernel_now[0, 0, :, cols].astype(f32)
+        weight = lag_held[0, :, cols].astype(f32)
         for part in range(2):
             spec = turned[part, cols, :].T.astype(bf16)
-            value = weight * spec.astype(f32) + past_sum[part, :, cols]
+            value = weight * spec.astype(f32) + sum_held[part, :, cols]
             if has_past:
-                value = value + kernel_past[0, 0, :, cols].astype(f32) * spec_past[
+                value = value + lag_held[1, :, cols].astype(f32) * spec_held[
                     part, :, cols
                 ].astype(f32)
             else:
-                spec_out[part, :, cols] = spec
+                spec_held[part, :, cols] = spec
             total[part, :, cols] = value
         return carry
 
     lax.fori_loop(0, length // 256, convolve, 0)
+    if not has_past:
+        leaving = pltpu.make_async_copy(spec_held, spec_out, sems.at[2])
+        leaving.start()
 
     def group_back(g, carry):
         at = pl.ds(pl.multiple_of(g * 16, 16), 16)
@@ -491,6 +509,8 @@
         return carry
 
     lax.fori_loop(0, RADIX // 2, wave_back, 0)
+    if not has_past:
+        leaving.wait()
 
 
 def inverse_kernel(count, *refs):
@@ -719,12 +739,7 @@
             shape = (slabs, 1, 2, array.shape[3], 128)
             return pl.BlockSpec(shape, lambda *_: (0, place, 0, 0, 0))
 
-        lag_spec = [
-            pl.BlockSpec((1, 1, 128, length), functools.partial(lambda lag, *_: (0, lag, half, 0), lag))
-            for lag in range(2)
-        ]
-        sum_spec = pl.BlockSpec((2, 128, length), lambda *_: (0, half, 0))
-        spec_spec = pl.BlockSpec((2, 128, length), lambda *_: (0, 0, 0))
+        anywhere = pl.BlockSpec(memory_space=pl.ANY)
 
         def arrived(tile):
             if len(tile) == 1:
@@ -733,7 +748,7 @@
             return [pl.BlockSpec((1, 2, 128, 128), lambda *_: (spot, 0, 0, 0))] * slabs
 
         operands = [place, *ring, *near, kernel, past_sum, table, twist, twist_ring]
-        in_specs = [SCALARS] + arrived(ring) + arrived(near) + [lag_spec[0], sum_spec]
+        in_specs = [SCALARS] + arrived(ring) + arrived(near) + [anywhere, anywhere]
         in_specs += [whole_spec(table), whole_spec(twist), whole_spec(twist_ring)]
         out_shape = []
         for row, count in pieces[1:]:
@@ -744,10 +759,10 @@
         out_specs = [whole_spec(shape) for shape in shapes] + out_specs
         if past is not None:
             operands += [kernel, past]
-            in_specs += [lag_spec[1], spec_spec]
+            in_specs += [anywhere, anywhere]
         else:
             out_shape.append(jax.ShapeDtypeStruct((2, 128, length), bf16))
-            out_specs.append(spec_spec)
+            out_specs.append(anywhere)
         aliases = {}
         if before is not None:
             aliases = {len(operands) + n: slabs + n for n in range(len(before))}
@@ -767,6 +782,10 @@
                 pltpu.VMEM((2, length, 128), f32),
                 pltpu.VMEM((2, 128, length), f32),
                 spread,
+                pltpu.VMEM((2, 128, length), f32),
+                pltpu.VMEM((2, 128, length), bf16),
+                pltpu.VMEM((2, 128, length), bf16),
+                pltpu.SemaphoreType.DMA((4,)),
             ],
             compiler_params=PARAMS,
         )(*operands)

time: 1140 us -> 1130 us (level)
  no operation moved by 1% of the time
where the time goes in v8:
time: 1130 us; the launch traced here: 1120 us
  waiting for transfers between devices  524 us (46%)
  starting transfers between devices  318 us (28%)
  Pallas kernels  271 us (24%)
    ppermute x105, waiting for transfers between devices, ringed(): moved[n] = lax.ppermute(blocks[n], 'slab', pairs)  347 us
    ppermute x105, starting transfers between devices, ringed(): moved[n] = lax.ppermute(blocks[n], 'slab', pairs)  252 us
    ppermute x5, waiting for transfers between devices, swapped(): return lax.ppermute(value, axis, pairs)  131 us
    pallas_call x4, Pallas kernels, spectral(): pl.pallas_call(functools.partial(spectral_kernel, (len(ring), len(near)),...  89.8 us
    all_to_all x6, starting transfers between devices, exchanged(): lax.all_to_all(value, 'slab', split_axis=0, concat_axis=0, tiled=True)  59.6 us
    pallas_call x5, Pallas kernels, inverse(): pl.pallas_call(functools.partial(inverse_kernel, len(blocks)), out_shape=...  52.8 us
    pallas_call x2, Pallas kernels, middle(): pl.pallas_call(middle_kernel, out_shape=shapes + [rows_shape], grid=(1,),...  46.4 us
    all_to_all x6, waiting for transfers between devices, exchanged(): lax.all_to_all(value, 'slab', split_axis=0, concat_axis=0, tiled=True)  46.2 us
  transfers between devices with their start and end apart: 116, of which 52 were waited for; matrix products, arithmetic and copies ran while one was open for 0% of the time, Pallas kernels for 19%

profile of v8, /device:TPU:0, one launch (start us, length us, event | category | flops | bytes accessed | tf_op | source)
XLA Modules:
  0.0 1122.8 jit_solution(13302485923438487446)
XLA Ops:
  22.4 24.8 %shard_map.114 = (f32[2,256,4096]{2,1,0:T(8,128)}, f32[2,256,4096]{2,1,0:T(8,128)}) custom-call(bf16[1,9,256,4096]{3,2,1,0:T(8,128)(2,1)} %refs_8_.1, bf16[1,8,2,256,4096]{4,3,2,1,0:T(8,128)(2,1)} %history.1), custom_call_target="tpu_custom_call" | custom-call | tf_op jit(solution)/shard_map/pallas_call | solution.py:724
  57.8 36.2 %collective-permute-done.20.refs_18_ = f32[1,2,128,128]{3,2,1,0:T(8,128)} collective-permute-done((f32[1,2,128,128]{3,2,1,0:T(8,128)S(1)}, f32[1,2,128,128]{3,2,1,0:T(8,128)}, u32[]{:S(2)}, u32[]{:S(2)}) %collective-permute-start.20) | collective-permute-done | bytes 131104 | tf_op jit(solution)/shard_map/ppermute | solution.py:578
  95.1 18.0 %collective-permute-start.26 = (f32[1,2,128,128]{3,2,1,0:T(8,128)}, f32[1,2,128,128]{3,2,1,0:T(8,128)}, u32[]{:S(2)}, u32[]{:S(2)}) collective-permute-start(f32[1,2,128,128]{3,2,1,0:T(8,128)} %get-tuple-element.262), channel_id=1, source_target_pairs={{0,12},{1,13},{2,14},{3,15},{4,0},{5,1},{6,2},{7,3},{8,4},{9,5},{1... | collective-permute-start | bytes 393224 | tf_op jit(solution)/shard_map/ppermute | solution.py:578
  121.0 12.7 %shard_map.112 = (f32[2,2,128,128]{3,2,1,0:T(8,128)}, f32[2,2,128,128]{3,2,1,0:T(8,128)}, f32[2,2,128,128]{3,2,1,0:T(8,128)}, f32[2,2,128,128]{3,2,1,0:T(8,128)}...) custom-call(s32[1]{0:T(128)} %bitcast.place.refs_0_, ...), custom_call_target="tpu_custom_call" | custom-call | tf_op jit(solution)/shard_map/pallas_call | solution.py:661
  151.3 19.6 %collective-permute-start.3 = (f32[2,2,128,128]{3,2,1,0:T(8,128)}, f32[2,2,128,128]{3,2,1,0:T(8,128)}, u32[]{:S(2)}, u32[]{:S(2)}) collective-permute-start(f32[2,2,128,128]{3,2,1,0:T(8,128)} %get-tuple-element.212), channel_id=1, source_target_pairs={{0,4},{1,5},{2,6},{3,7},{4,8},{5,9},{6,10},{7,11},{8,12},{9,13},{1... | collective-permute-start | bytes 786440 | tf_op jit(solution)/shard_map/ppermute | solution.py:578
  182.2 27.1 %collective-permute-done.4.refs_6_ = f32[2,2,128,128]{3,2,1,0:T(8,128)} collective-permute-done((f32[2,2,128,128]{3,2,1,0:T(8,128)}, f32[2,2,128,128]{3,2,1,0:T(8,128)}, u32[]{:S(2)}, u32[]{:S(2)}) %collective-permute-start.4) | collective-permute-done | bytes 262176 | tf_op jit(solution)/shard_map/ppermute | solution.py:578
  231.8 22.4 %shard_map.115 = (f32[1,2,128,128]{3,2,1,0:T(8,128)}, f32[1,2,128,128]{3,2,1,0:T(8,128)}, f32[1,2,128,128]{3,2,1,0:T(8,128)}, f32[1,2,128,128]{3,2,1,0:T(8,128)}...) custom-call(s32[1]{0:T(128)} %bitcast.place.refs_0_, ...), custom_call_target="tpu_custom_call" | custom-call | tf_op jit(solution)/shard_map/pallas_call | solution.py:771
  254.2 22.5 %shard_map.116 = (f32[1,2,128,128]{3,2,1,0:T(8,128)}, f32[1,2,128,128]{3,2,1,0:T(8,128)}, f32[1,2,128,128]{3,2,1,0:T(8,128)}, f32[1,2,128,128]{3,2,1,0:T(8,128)}...) custom-call(s32[1]{0:T(128)} %bitcast.place.refs_0_, ...), custom_call_target="tpu_custom_call", output_to_operand_aliasing={{16}: (23, {})} | custom-call | tf_op jit(solution)/shard_map/pallas_call | solution.py:771
  314.9 69.9 %collective-permute-done.35.refs_1_ = f32[1,2,128,128]{3,2,1,0:T(8,128)} collective-permute-done((f32[1,2,128,128]{3,2,1,0:T(8,128)S(1)}, f32[1,2,128,128]{3,2,1,0:T(8,128)}, u32[]{:S(2)}, u32[]{:S(2)}) %collective-permute-start.35) | collective-permute-done | bytes 131104 | tf_op jit(solution)/shard_map/ppermute | solution.py:578
  386.0 29.2 %collective-permute-start.46 = (f32[1,2,128,128]{3,2,1,0:T(8,128)S(1)}, f32[1,2,128,128]{3,2,1,0:T(8,128)}, u32[]{:S(2)}, u32[]{:S(2)}) collective-permute-start(f32[1,2,128,128]{3,2,1,0:T(8,128)S(1)} %copy-done.32), channel_id=1, source_target_pairs={{0,12},{1,13},{2,14},{3,15},{4,0},{5,1},{6,2},{7,3},{8,4},{9,5},{1... | collective-permute-start | bytes 393224 | tf_op jit(solution)/shard_map/ppermute | solution.py:578
  493.3 36.1 %collective-permute-done.60.other = f32[128,4096]{1,0:T(8,128)} collective-permute-done((f32[128,4096]{1,0:T(8,128)}, f32[128,4096]{1,0:T(8,128)}, u32[]{:S(2)}, u32[]{:S(2)}) %collective-permute-start.60) | collective-permute-done | bytes 2097184 | tf_op jit(solution)/shard_map/ppermute | solution.py:25
  529.5 22.8 %shard_map.120 = (f32[16,2,2,128,128]{4,3,2,1,0:T(8,128)}, f32[128,4096]{1,0:T(8,128)}) custom-call(s32[1]{0:T(128)} %bitcast.place.refs_0_, f32[5]{0:T(128)} %shard_map.118.scalars.before, f32[128,4096]{1,0:T(8,128)} %shard_map.119.own, f32[128,4096]{1,0:T(8,128)} %collective-permute-done.60.other, f32[256,4096]{1,0:T(8,128)} %prestress.9, ...), custom_call_target="tpu_custom_call" | custom-call | tf_op jit(solution)/shard_map/pallas_call | solution.py:678
  576.4 46.7 %collective-permute-done.61.other = f32[128,4096]{1,0:T(8,128)} collective-permute-done((f32[128,4096]{1,0:T(8,128)}, f32[128,4096]{1,0:T(8,128)}, u32[]{:S(2)}, u32[]{:S(2)}) %collective-permute-start.61) | collective-permute-done | bytes 2097184 | tf_op jit(solution)/shard_map/ppermute | solution.py:25
  623.1 23.5 %shard_map.122 = (f32[1,2,128,128]{3,2,1,0:T(8,128)}, f32[1,2,128,128]{3,2,1,0:T(8,128)}, f32[1,2,128,128]{3,2,1,0:T(8,128)}, f32[1,2,128,128]{3,2,1,0:T(8,128)}...) custom-call(s32[1]{0:T(128)} %bitcast.place.refs_0_, ...), custom_call_target="tpu_custom_call" | custom-call | tf_op jit(solution)/shard_map/pallas_call | solution.py:678
  655.5 16.1 %collective-permute-done.62.refs_8_ = f32[1,2,128,128]{3,2,1,0:T(8,128)} collective-permute-done((f32[1,2,128,128]{3,2,1,0:T(8,128)}, f32[1,2,128,128]{3,2,1,0:T(8,128)}, u32[]{:S(2)}, u32[]{:S(2)}) %collective-permute-start.62) | collective-permute-done | bytes 131104 | tf_op jit(solution)/shard_map/ppermute | solution.py:578
  691.1 36.2 %collective-permute-done.67.refs_3_ = f32[1,2,128,128]{3,2,1,0:T(8,128)} collective-permute-done((f32[1,2,128,128]{3,2,1,0:T(8,128)S(1)}, f32[1,2,128,128]{3,2,1,0:T(8,128)}, u32[]{:S(2)}, u32[]{:S(2)}) %collective-permute-start.67) | collective-permute-done | bytes 131104 | tf_op jit(solution)/shard_map/ppermute | solution.py:578
  728.4 18.0 %collective-permute-start.73 = (f32[1,2,128,128]{3,2,1,0:T(8,128)S(1)}, f32[1,2,128,128]{3,2,1,0:T(8,128)}, u32[]{:S(2)}, u32[]{:S(2)}) collective-permute-start(f32[1,2,128,128]{3,2,1,0:T(8,128)S(1)} %copy-done.49), channel_id=1, source_target_pairs={{0,12},{1,13},{2,14},{3,15},{4,0},{5,1},{6,2},{7,3},{8,4},{9,5},{1... | collective-permute-start | bytes 393224 | tf_op jit(solution)/shard_map/ppermute | solution.py:578
  757.4 22.4 %shard_map.123 = (f32[1,2,128,128]{3,2,1,0:T(8,128)}, f32[1,2,128,128]{3,2,1,0:T(8,128)}, f32[1,2,128,128]{3,2,1,0:T(8,128)}, f32[1,2,128,128]{3,2,1,0:T(8,128)}...) custom-call(s32[1]{0:T(128)} %bitcast.place.refs_0_, ...), custom_call_target="tpu_custom_call" | custom-call | tf_op jit(solution)/shard_map/pallas_call | solution.py:771
  779.8 22.6 %shard_map.124 = (f32[1,2,128,128]{3,2,1,0:T(8,128)}, f32[1,2,128,128]{3,2,1,0:T(8,128)}, f32[1,2,128,128]{3,2,1,0:T(8,128)}, f32[1,2,128,128]{3,2,1,0:T(8,128)}...) custom-call(s32[1]{0:T(128)} %bitcast.place.refs_0_, ...), custom_call_target="tpu_custom_call", output_to_operand_aliasing={{16}: (10, {}), {17}: (11, {})} | custom-call | tf_op jit(solution)/shard_map/pallas_call | solution.py:771
  840.1 46.2 %all-to-all-done.4.refs_0_ = f32[16,2,2,80,128]{4,3,2,1,0:T(8,128)} async-done(((f32[16,2,2,80,128]{4,3,2,1,0:T(8,128)}), f32[16,2,2,80,128]{4,3,2,1,0:T(8,128)}, u32[]{:S(2)}, u32[]{:S(2)}) %all-to-all-start.4) | async-done | bytes 2621472 | tf_op jit(solution)/shard_map/all_to_all | solution.py:607
  886.3 13.4 %all-to-all-start.5 = ((f32[16,2,2,48,128]{4,3,2,1,0:T(8,128)}), f32[16,2,2,48,128]{4,3,2,1,0:T(8,128)}, u32[]{:S(2)}, u32[]{:S(2)}) async-start(f32[16,2,2,48,128]{4,3,2,1,0:T(8,128)} %get-tuple-element.366), calls=%async_computation.5 | async-start | bytes 3145728 | tf_op jit(solution)/shard_map/all_to_all | solution.py:607
  907.2 26.4 %collective-permute-done.100.refs_20_ = f32[1,2,128,128]{3,2,1,0:T(8,128)} collective-permute-done((f32[1,2,128,128]{3,2,1,0:T(8,128)S(1)}, f32[1,2,128,128]{3,2,1,0:T(8,128)}, u32[]{:S(2)}, u32[]{:S(2)}) %collective-permute-start.100) | collective-permute-done | bytes 131104 | tf_op jit(solution)/shard_map/ppermute | solution.py:578
  1037.8 37.1 %collective-permute-done.107.other = f32[128,4096]{1,0:T(8,128)} collective-permute-done((f32[128,4096]{1,0:T(8,128)}, f32[128,4096]{1,0:T(8,128)}, u32[]{:S(2)}, u32[]{:S(2)}) %collective-permute-start.107) | collective-permute-done | bytes 2097184 | tf_op jit(solution)/shard_map/ppermute | solution.py:25
  1074.9 12.5 %shard_map.130 = (f32[1,256,4096]{2,1,0:T(8,128)}, f32[256,4096]{1,0:T(8,128)}, f32[256,4096]{1,0:T(8,128)}) custom-call(f32[5]{0:T(128)} %shard_map.127.scalars, f32[128,4096]{1,0:T(8,128)} %shard_map.129.own, f32[128,4096]{1,0:T(8,128)} %collective-permute-done.107.other, f32[256,4096]{1,0:T(8,128)} %prestress.9, f32[256,4096]{1,0:T(8,128)} %strength.9, ...), custom_call_target="tpu_custom_call" | custom-call | tf_op jit(solution)/shard_map/pallas_call | solution.py:710
  (365 shorter events, 453.5 us)
Async XLA Ops:
  47.3 206.9 %all-to-all-start = ((f32[16,1,2,128,128]{4,3,2,1,0:T(8,128)}), f32[16,1,2,128,128]{4,3,2,1,0:T(8,128)}, u32[]{:S(2)}, u32[]{:S(2)}) async-start(f32[16,1,2,128,128]{4,3,2,1,0:T(8,128)} %get-tuple-element.249), calls=%async_computation | async-start | bytes 4194304 | tf_op jit(solution)/shard_map/all_to_all | solution.py:607
  53.8 59.3 %collective-permute-start.22 = (f32[1,2,128,128]{3,2,1,0:T(8,128)S(1)}, f32[1,2,128,128]{3,2,1,0:T(8,128)}, u32[]{:S(2)}, u32[]{:S(2)}) collective-permute-start(f32[1,2,128,128]{3,2,1,0:T(8,128)S(1)} %copy-done.60), channel_id=1, source_target_pairs={{0,3},{1,4},{2,5},{3,6},{4,7},{5,8},{6,9},{7,10},{8,11},{9,12},{10... | collective-permute-start | bytes 393224 | tf_op jit(solution)/shard_map/ppermute | solution.py:578
  56.1 60.4 %collective-permute-start.23 = (f32[1,2,128,128]{3,2,1,0:T(8,128)S(1)}, f32[1,2,128,128]{3,2,1,0:T(8,128)}, u32[]{:S(2)}, u32[]{:S(2)}) collective-permute-start(f32[1,2,128,128]{3,2,1,0:T(8,128)S(1)} %copy-done.57), channel_id=1, source_target_pairs={{0,4},{1,5},{2,6},{3,7},{4,8},{5,9},{6,10},{7,11},{8,12},{9,13},{1... | collective-permute-start | bytes 393224 | tf_op jit(solution)/shard_map/ppermute | solution.py:578
  57.6 59.1 %collective-permute-start.24 = (f32[1,2,128,128]{3,2,1,0:T(8,128)S(1)}, f32[1,2,128,128]{3,2,1,0:T(8,128)}, u32[]{:S(2)}, u32[]{:S(2)}) collective-permute-start(f32[1,2,128,128]{3,2,1,0:T(8,128)S(1)} %copy-done.54), channel_id=1, source_target_pairs={{0,5},{1,6},{2,7},{3,8},{4,9},{5,10},{6,11},{7,12},{8,13},{9,14},{... | collective-permute-start | bytes 393224 | tf_op jit(solution)/shard_map/ppermute | solution.py:578
  174.9 45.7 %collective-permute-start.6 = (f32[2,2,128,128]{3,2,1,0:T(8,128)}, f32[2,2,128,128]{3,2,1,0:T(8,128)}, u32[]{:S(2)}, u32[]{:S(2)}) collective-permute-start(f32[2,2,128,128]{3,2,1,0:T(8,128)} %get-tuple-element.215), channel_id=1, source_target_pairs={{0,7},{1,8},{2,9},{3,10},{4,11},{5,12},{6,13},{7,14},{8,15},{9,0},... | collective-permute-start | bytes 786440 | tf_op jit(solution)/shard_map/ppermute | solution.py:578
  175.9 44.8 %collective-permute-start.7 = (f32[2,2,128,128]{3,2,1,0:T(8,128)}, f32[2,2,128,128]{3,2,1,0:T(8,128)}, u32[]{:S(2)}, u32[]{:S(2)}) collective-permute-start(f32[2,2,128,128]{3,2,1,0:T(8,128)} %get-tuple-element.216), channel_id=1, source_target_pairs={{0,8},{1,9},{2,10},{3,11},{4,12},{5,13},{6,14},{7,15},{8,0},{9,1},... | collective-permute-start | bytes 786440 | tf_op jit(solution)/shard_map/ppermute | solution.py:578
  300.7 251.6 %all-to-all-start.1 = ((f32[16,2,2,128,128]{4,3,2,1,0:T(8,128)}), f32[16,2,2,128,128]{4,3,2,1,0:T(8,128)}, u32[]{:S(2)}, u32[]{:S(2)}) async-start(f32[16,2,2,128,128]{4,3,2,1,0:T(8,128)} %get-tuple-element.282), calls=%async_computation.1 | async-start | bytes 8388608 | tf_op jit(solution)/shard_map/all_to_all | solution.py:607
  309.0 75.8 %collective-permute-start.35 = (f32[1,2,128,128]{3,2,1,0:T(8,128)S(1)}, f32[1,2,128,128]{3,2,1,0:T(8,128)}, u32[]{:S(2)}, u32[]{:S(2)}) collective-permute-start(f32[1,2,128,128]{3,2,1,0:T(8,128)S(1)} %copy-done.43), channel_id=1, source_target_pairs={{0,1},{1,2},{2,3},{3,4},{4,5},{5,6},{6,7},{7,8},{8,9},{9,10},{10,1... | collective-permute-start | bytes 393224 | tf_op jit(solution)/shard_map/ppermute | solution.py:578
  309.4 76.6 %collective-permute-start.36 = (f32[1,2,128,128]{3,2,1,0:T(8,128)S(1)}, f32[1,2,128,128]{3,2,1,0:T(8,128)}, u32[]{:S(2)}, u32[]{:S(2)}) collective-permute-start(f32[1,2,128,128]{3,2,1,0:T(8,128)S(1)} %copy-done.41), channel_id=1, source_target_pairs={{0,2},{1,3},{2,4},{3,5},{4,6},{5,7},{6,8},{7,9},{8,10},{9,11},{10,... | collective-permute-start | bytes 393224 | tf_op jit(solution)/shard_map/ppermute | solution.py:578
  312.2 103.0 %collective-permute-start.37 = (f32[1,2,128,128]{3,2,1,0:T(8,128)S(1)}, f32[1,2,128,128]{3,2,1,0:T(8,128)}, u32[]{:S(2)}, u32[]{:S(2)}) collective-permute-start(f32[1,2,128,128]{3,2,1,0:T(8,128)S(1)} %copy-done.39), channel_id=1, source_target_pairs={{0,3},{1,4},{2,5},{3,6},{4,7},{5,8},{6,9},{7,10},{8,11},{9,12},{10... | collective-permute-start | bytes 393224 | tf_op jit(solution)/shard_map/ppermute | solution.py:578
  313.3 105.2 %collective-permute-start.38 = (f32[1,2,128,128]{3,2,1,0:T(8,128)S(1)}, f32[1,2,128,128]{3,2,1,0:T(8,128)}, u32[]{:S(2)}, u32[]{:S(2)}) collective-permute-start(f32[1,2,128,128]{3,2,1,0:T(8,128)S(1)} %copy-done.37), channel_id=1, source_target_pairs={{0,4},{1,5},{2,6},{3,7},{4,8},{5,9},{6,10},{7,11},{8,12},{9,13},{1... | collective-permute-start | bytes 393224 | tf_op jit(solution)/shard_map/ppermute | solution.py:578
  314.8 104.1 %collective-permute-start.39 = (f32[1,2,128,128]{3,2,1,0:T(8,128)S(1)}, f32[1,2,128,128]{3,2,1,0:T(8,128)}, u32[]{:S(2)}, u32[]{:S(2)}) collective-permute-start(f32[1,2,128,128]{3,2,1,0:T(8,128)S(1)} %copy-done.35), channel_id=1, source_target_pairs={{0,5},{1,6},{2,7},{3,8},{4,9},{5,10},{6,11},{7,12},{8,13},{9,14},{... | collective-permute-start | bytes 393224 | tf_op jit(solution)/shard_map/ppermute | solution.py:578
  482.2 47.2 %collective-permute-start.60 = (f32[128,4096]{1,0:T(8,128)}, f32[128,4096]{1,0:T(8,128)}, u32[]{:S(2)}, u32[]{:S(2)}) collective-permute-start(f32[128,4096]{1,0:T(8,128)} %shard_map.119.own), channel_id=1, source_target_pairs={{0,16},{16,0},{1,17},{17,1},{2,18},{18,2},{3,19},{19,3},{4,20},{20... | collective-permute-start | bytes 6291464 | tf_op jit(solution)/shard_map/ppermute | solution.py:25
  552.3 122.6 %all-to-all-start.2 = ((f32[16,2,2,128,128]{4,3,2,1,0:T(8,128)}), f32[16,2,2,128,128]{4,3,2,1,0:T(8,128)}, u32[]{:S(2)}, u32[]{:S(2)}) async-start(f32[16,2,2,128,128]{4,3,2,1,0:T(8,128)} %get-tuple-element.317), calls=%async_computation.2 | async-start | bytes 8388608 | tf_op jit(solution)/shard_map/all_to_all | solution.py:607
  574.9 48.2 %collective-permute-start.61 = (f32[128,4096]{1,0:T(8,128)}, f32[128,4096]{1,0:T(8,128)}, u32[]{:S(2)}, u32[]{:S(2)}) collective-permute-start(f32[128,4096]{1,0:T(8,128)} %shard_map.121.own), channel_id=1, source_target_pairs={{0,16},{16,0},{1,17},{17,1},{2,18},{18,2},{3,19},{19,3},{4,20},{20... | collective-permute-start | bytes 6291464 | tf_op jit(solution)/shard_map/ppermute | solution.py:25
  674.9 104.9 %all-to-all-start.3 = ((f32[16,1,2,128,128]{4,3,2,1,0:T(8,128)}), f32[16,1,2,128,128]{4,3,2,1,0:T(8,128)}, u32[]{:S(2)}, u32[]{:S(2)}) async-start(f32[16,1,2,128,128]{4,3,2,1,0:T(8,128)} %get-tuple-element.326), calls=%async_computation.3 | async-start | bytes 4194304 | tf_op jit(solution)/shard_map/all_to_all | solution.py:607
  687.2 59.3 %collective-permute-start.69 = (f32[1,2,128,128]{3,2,1,0:T(8,128)S(1)}, f32[1,2,128,128]{3,2,1,0:T(8,128)}, u32[]{:S(2)}, u32[]{:S(2)}) collective-permute-start(f32[1,2,128,128]{3,2,1,0:T(8,128)S(1)} %copy-done.59), channel_id=1, source_target_pairs={{0,3},{1,4},{2,5},{3,6},{4,7},{5,8},{6,9},{7,10},{8,11},{9,12},{10... | collective-permute-start | bytes 393224 | tf_op jit(solution)/shard_map/ppermute | solution.py:578
  689.5 60.4 %collective-permute-start.70 = (f32[1,2,128,128]{3,2,1,0:T(8,128)S(1)}, f32[1,2,128,128]{3,2,1,0:T(8,128)}, u32[]{:S(2)}, u32[]{:S(2)}) collective-permute-start(f32[1,2,128,128]{3,2,1,0:T(8,128)S(1)} %copy-done.56), channel_id=1, source_target_pairs={{0,4},{1,5},{2,6},{3,7},{4,8},{5,9},{6,10},{7,11},{8,12},{9,13},{1... | collective-permute-start | bytes 393224 | tf_op jit(solution)/shard_map/ppermute | solution.py:578
  690.9 59.1 %collective-permute-start.71 = (f32[1,2,128,128]{3,2,1,0:T(8,128)S(1)}, f32[1,2,128,128]{3,2,1,0:T(8,128)}, u32[]{:S(2)}, u32[]{:S(2)}) collective-permute-start(f32[1,2,128,128]{3,2,1,0:T(8,128)S(1)} %copy-done.53), channel_id=1, source_target_pairs={{0,5},{1,6},{2,7},{3,8},{4,9},{5,10},{6,11},{7,12},{8,13},{9,14},{... | collective-permute-start | bytes 393224 | tf_op jit(solution)/shard_map/ppermute | solution.py:578
  824.2 62.1 %all-to-all-start.4 = ((f32[16,2,2,80,128]{4,3,2,1,0:T(8,128)}), f32[16,2,2,80,128]{4,3,2,1,0:T(8,128)}, u32[]{:S(2)}, u32[]{:S(2)}) async-start(f32[16,2,2,80,128]{4,3,2,1,0:T(8,128)} %get-tuple-element.363), calls=%async_computation.4 | async-start | bytes 5242880 | tf_op jit(solution)/shard_map/all_to_all | solution.py:607
  886.3 201.1 %all-to-all-start.5 = ((f32[16,2,2,48,128]{4,3,2,1,0:T(8,128)}), f32[16,2,2,48,128]{4,3,2,1,0:T(8,128)}, u32[]{:S(2)}, u32[]{:S(2)}) async-start(f32[16,2,2,48,128]{4,3,2,1,0:T(8,128)} %get-tuple-element.366), calls=%async_computation.5 | async-start | bytes 3145728 | tf_op jit(solution)/shard_map/all_to_all | solution.py:607
  901.6 44.7 %collective-permute-start.101 = (f32[1,2,128,128]{3,2,1,0:T(8,128)S(1)}, f32[1,2,128,128]{3,2,1,0:T(8,128)}, u32[]{:S(2)}, u32[]{:S(2)}) collective-permute-start(f32[1,2,128,128]{3,2,1,0:T(8,128)S(1)} %copy-done.55), channel_id=1, source_target_pairs={{0,5},{1,6},{2,7},{3,8},{4,9},{5,10},{6,11},{7,12},{8,13},{9,14},{... | collective-permute-start | bytes 393224 | tf_op jit(solution)/shard_map/ppermute | solution.py:578
  1026.0 48.9 %collective-permute-start.107 = (f32[128,4096]{1,0:T(8,128)}, f32[128,4096]{1,0:T(8,128)}, u32[]{:S(2)}, u32[]{:S(2)}) collective-permute-start(f32[128,4096]{1,0:T(8,128)} %shard_map.129.own), channel_id=1, source_target_pairs={{0,16},{16,0},{1,17},{17,1},{2,18},{18,2},{3,19},{19,3},{4,20},{20... | collective-permute-start | bytes 6291464 | tf_op jit(solution)/shard_map/ppermute | solution.py:25
  1037.3 65.7 %collective-permute-start.109 = (f32[80,4096]{1,0:T(8,128)}, f32[80,4096]{1,0:T(8,128)}, u32[]{:S(2)}, u32[]{:S(2)}) collective-permute-start(f32[80,4096]{1,0:T(8,128)} %shard_map.128.own), channel_id=1, source_target_pairs={{0,16},{16,0},{1,17},{17,1},{2,18},{18,2},{3,19},{19,3},{4,20},{20... | collective-permute-start | bytes 3932168 | tf_op jit(solution)/shard_map/ppermute | solution.py:25
  (157 other events, 8433.8 us)
